TPU v7x, 512 devices: a whole 4x4x16 slice. The times are simulated.
512 devices in a mesh: rows: 32 (over y, z_hi, core), cols: 16 (over x, z_lo).
Axes of the slice: x: 4, y: 4, z: 16 (z_hi: 4, z_lo: 4; z = z_hi * 4 + z_lo), core: 2. Of those that a mesh axis runs over, the one named last changes fastest.
Arguments:
- a_vals: float32 [6144, 64, 896], P(('rows', 'cols')), may hold values from -0.1875 to 0.1875
- a_cols: int32 [6144, 14], P(('rows', 'cols')), may hold values from 0 to 6143, as said below
- a_count: int32 [6144], P(('rows', 'cols')), may hold values from 3 to 14, as said below
- p_vals: float32 [6144, 64, 320], P(('rows', 'cols')), may hold values from -3 to 3
- p_mask: int32 [6144, 5], P(('rows', 'cols')), may hold values 0 or 1
Outputs:
- coarse: float32 [512, 64, 704], P(('rows', 'cols'))
Inputs may be any that keep to these rules, and one draw needn't show every extreme that they name: `a_cols`: each block row names 14 different block columns, the first its own; all lie among the 12 rows of its own slab or of the slab just before or after it, slabs taken in the order of rows, then cols; where those slabs exist, the second lies in the slab before and the third in the slab after. Slots at or after a_count of a block row are ignored; some block row has all 14 slots live.
All inputs are finite; a program needn't handle non-finite values. No bound on the sum of `p_mask` on one device may be relied on, other than what follows from the above.
Results may differ from a plain program's by a relative error of at most 0.0003.
Values sent between devices are 32-bit elements; how exact they have to be, the bound alone decides.
A program may use at most 128 MiB of HBM per device.

v0:
```python
import jax
import jax.numpy as jnp
from jax import lax
from jax.sharding import PartitionSpec as P

FULL_PRECISION = lax.Precision.HIGHEST


def from_behind(array, axis, by):
    count = lax.axis_size(axis)
    pairs = [(i, i + by) for i in range(count) if 0 <= i + by < count]
    return lax.ppermute(array, axis, pairs)


def shards(a_vals, a_cols, a_count, p_vals, p_mask):
    rows_here = a_cols.shape[0]
    slot_count = a_cols.shape[1]
    block_size = a_vals.shape[1]
    prol_slots = p_mask.shape[1]
    group_total = lax.axis_size("rows") * lax.axis_size("cols")
    position = lax.axis_index("rows") * lax.axis_size("cols") + lax.axis_index("cols")
    slot_ids = jnp.arange(prol_slots, dtype=jnp.int32)
    target = position + slot_ids - 2
    inside = ((target >= 0) & (target < group_total)).astype(jnp.float32)
    keep_mask = p_mask.astype(jnp.float32) * inside[None, :]
    pblocks = (
        p_vals.reshape(rows_here, block_size, prol_slots, block_size) * keep_mask[:, None, :, None]
    )
    pflat = pblocks.reshape(rows_here, block_size, prol_slots * block_size)
    lower_rows = from_behind(pflat, ("rows", "cols"), 1)
    upper_rows = from_behind(pflat, ("rows", "cols"), -1)
    widened = jnp.concatenate([lower_rows, pflat, upper_rows], axis=0)
    local_cols = a_cols - (position - 1) * rows_here
    side_index = local_cols // rows_here
    live_mask = jnp.arange(slot_count, dtype=jnp.int32)[None, :] < a_count[:, None]
    side_ids = jnp.arange(3, dtype=jnp.int32)
    weights = (live_mask[:, :, None] & (side_index[:, :, None] == side_ids[None, None, :])).astype(
        jnp.float32
    )
    matrix_rows = a_vals.reshape(rows_here, block_size, slot_count, block_size)
    gathered = jnp.take(widened, local_cols.reshape(-1), axis=0).reshape(
        rows_here, slot_count, block_size, prol_slots * block_size
    )
    products = jnp.einsum("ifkg,ikgc->ikfc", matrix_rows, gathered, precision=FULL_PRECISION)
    mixed = jnp.einsum("ikd,ikfc->idfc", weights, products, precision=FULL_PRECISION)
    ap_rows = jnp.zeros((rows_here, block_size, (prol_slots + 2) * block_size), jnp.float32)
    for side in range(3):
        ap_rows = ap_rows + jnp.pad(
            mixed[:, side], ((0, 0), (0, 0), (side * block_size, (2 - side) * block_size))
        )
    terms = jnp.einsum("ifsc,ifq->scq", pblocks, ap_rows, precision=FULL_PRECISION)
    spread = [
        jnp.pad(terms[s], ((0, 0), ((prol_slots - 1 - s) * block_size, s * block_size)))
        for s in range(prol_slots)
    ]
    result = spread[2]
    result = result + from_behind(spread[3], ("rows", "cols"), 1)
    result = result + from_behind(spread[4], ("rows", "cols"), 2)
    result = result + from_behind(spread[1], ("rows", "cols"), -1)
    result = result + from_behind(spread[0], ("rows", "cols"), -2)
    return result.reshape(1, block_size, (prol_slots + 6) * block_size)


def solution(mesh):
    in_specs = (
        P(("rows", "cols"), None, None),
        P(("rows", "cols"), None),
        P(("rows", "cols")),
        P(("rows", "cols"), None, None),
        P(("rows", "cols"), None),
    )
    out_specs = P(("rows", "cols"), None, None)
    return jax.shard_map(shards, mesh=mesh, in_specs=in_specs, out_specs=out_specs, check_vma=False)
```

profile of v0, /device:TPU:1, one launch (start us, length us, event | category | flops | bytes accessed | tf_op | source)
XLA Modules:
  0.0 156.2 jit_solution(3349416244251099934)
XLA Ops:
  0.0 0.9 convert_multiply_fusion
  0.9 0.1 copy.11
  1.1 1.4 broadcast_multiply_fusion
  2.5 4.4 %collective-permute-start = (f32[12,64,320]{2,1,0:T(8,128)S(1)}, f32[12,64,320]{2,1,0:T(8,128)S(1)}, u32[]{:S(2)}, u32[]{:S(2)}) collective-permute-start(f32[12,64,320]{2,1,0:T(8,128)S(1)} %broadcast_multiply_fusion), channel_id=1, source_target_pairs={{0,1},{1,2},{2,3},{3,4},{4,5},{5,6},{6,7},{7,8},{8,9},{9,10},{10,1... | collective-permute-start | bytes 2949128 | tf_op jit(solution)/shard_map/ppermute | solution.py:12
  6.9 7.4 %collective-permute-start.1 = (f32[12,64,320]{2,1,0:T(8,128)S(1)}, f32[12,64,320]{2,1,0:T(8,128)}, u32[]{:S(2)}, u32[]{:S(2)}) collective-permute-start(f32[12,64,320]{2,1,0:T(8,128)S(1)} %broadcast_multiply_fusion), channel_id=1, source_target_pairs={{1,0},{2,1},{3,2},{4,3},{5,4},{6,5},{7,6},{8,7},{9,8},{10,9},{11,1... | collective-permute-start | bytes 2949128 | tf_op jit(solution)/shard_map/ppermute | solution.py:12
  14.3 1.9 %copy.10 = f32[12,64,320]{1,2,0:T(8,128)} copy(f32[12,64,320]{2,1,0:T(8,128)S(1)} %copy-done.1) | data formatting | bytes 1966080 | tf_op args[3]
  16.2 0.7 add_select_fusion
  17.0 5.4 %copy.21 = f32[12,64,896]{1,2,0:T(8,128)} copy(f32[12,64,896]{2,1,0:T(8,128)} %param.5) | data formatting | bytes 5505024 | tf_op jit(solution)/shard_map/reshape | solution.py:40
  22.4 0.6 pad_clamp_fusion
  23.0 0.6 iota_compare_fusion.1
  23.6 0.6 compare_and_fusion
  24.2 13.3 %collective-permute-done = f32[12,64,320]{2,1,0:T(8,128)S(1)} collective-permute-done((f32[12,64,320]{2,1,0:T(8,128)S(1)}, f32[12,64,320]{2,1,0:T(8,128)S(1)}, u32[]{:S(2)}, u32[]{:S(2)}) %collective-permute-start) | collective-permute-done | bytes 983072 | tf_op jit(solution)/shard_map/ppermute | solution.py:12
  37.5 1.0 copy-done.3
  38.5 22.8 %collective-permute-done.1 = f32[12,64,320]{2,1,0:T(8,128)} collective-permute-done((f32[12,64,320]{2,1,0:T(8,128)S(1)}, f32[12,64,320]{2,1,0:T(8,128)}, u32[]{:S(2)}, u32[]{:S(2)}) %collective-permute-start.1) | collective-permute-done | bytes 983072 | tf_op jit(solution)/shard_map/ppermute | solution.py:12
  61.3 2.2 %pad_maximum_fusion = f32[36,64,320]{2,1,0:T(8,128)S(1)} fusion(f32[12,64,320]{2,1,0:T(8,128)} %collective-permute-done.1, f32[12,64,320]{2,1,0:T(8,128)} %copy-done.2, f32[12,64,320]{2,1,0:T(8,128)} %copy-done.3), kind=kLoop, calls=%fused_computation.8 | loop fusion | flops 1474560 | bytes 5898240 | tf_op jit(solution)/shard_map/concatenate | solution.py:32
  63.6 7.4 %gather_fusion = f32[168,64,320]{2,1,0:T(8,128)} fusion(f32[36,64,320]{2,1,0:T(8,128)S(1)} %pad_maximum_fusion, s32[1024]{0:T(1024)} %pad_clamp_fusion), kind=kCustom, calls=%fused_computation | custom fusion | bytes 27525792 | tf_op jit(solution)/shard_map/jit(_take)/gather | solution.py:41
  71.0 23.0 %fusion.3 = f32[12,14,320,64]{2,3,1,0:T(8,128)} fusion(f32[12,64,14,64]{1,3,2,0:T(8,128)} %bitcast.42, f32[12,14,64,320]{3,2,1,0:T(8,128)} %bitcast.41, pred[12,14]{1,0:T(8,128)(4,1)} %compare_and_fusion), kind=kOutput, calls=%fused_computation.4 | convolution fusion | flops 2645852160 | bytes 30277800 | tf_op jit(solution)/shard_map/ifkg,ikgc->ikfc/dot_general | solution.py:44
  94.0 21.5 %fusion = f32[12,3,64,320]{3,1,2,0:T(4,128)S(1)} fusion(f32[12,14,320,64]{2,3,1,0:T(8,128)} %fusion.3, s32[12,14]{1,0:T(8,128)S(1)} %get-tuple-element.5, pred[12,14]{1,0:T(8,128)(4,1)S(1)} %copy-done.4), kind=kOutput, calls=%fused_computation.1 | convolution fusion | flops 123864048 | bytes 16712520 | tf_op jit(solution)/shard_map/ikd,ikfc->idfc/dot_general | solution.py:45
  115.5 3.1 %fusion.29 = (f32[12,1,64,320]{3,1,2,0:T(1,128)S(1)}, f32[12,1,64,320]{3,1,2,0:T(1,128)S(1)}, f32[12,1,64,320]{3,1,2,0:T(1,128)S(1)}) fusion(f32[12,3,64,320]{3,1,2,0:T(4,128)S(1)} %fusion), kind=kLoop, calls=%fused_computation.48 | loop fusion | bytes 5898240 | tf_op jit(solution)/shard_map/slice | solution.py:49
  118.6 0.1 copy.32
  118.7 0.2 copy_bitcast_fusion
  118.9 1.3 copy-done
  120.2 2.5 %fusion.15 = f32[5,64,448]{2,1,0:T(8,128)S(1)} fusion(f32[12,64,320]{2,1,0:T(8,128)S(1)} %bitcast.44, f32[12,64,320]{2,1,0:T(8,128)S(1)} %get-tuple-element.15, f32[12,64,320]{2,1,0:T(8,128)S(1)} %get-tuple-element.16, f32[12,64,5,64]{1,3,2,0:T(8,128)S(1)} %bitcast.43, f32[12,5]{1,0:T(8,128)S(1)} %copy.11), kind=kOutput, calls=%fused_computation.17 | convolution fusion | flops 1322139648 | bytes 4505840 | tf_op jit(solution)/shard_map/ifsc,ifq->scq/dot_general | solution.py:51
  122.7 0.1 pad.36
  122.9 2.3 %collective-permute-start.2 = (f32[64,704]{1,0:T(8,128)S(1)}, f32[64,704]{1,0:T(8,128)S(1)}, u32[]{:S(2)}, u32[]{:S(2)}) collective-permute-start(f32[64,704]{1,0:T(8,128)S(1)} %pad.36), channel_id=1, source_target_pairs={{0,1},{1,2},{2,3},{3,4},{4,5},{5,6},{6,7},{7,8},{8,9},{9,10},{10,1... | collective-permute-start | bytes 540680 | tf_op jit(solution)/shard_map/ppermute | solution.py:12
  125.1 2.4 %collective-permute-start.3 = (f32[64,704]{1,0:T(8,128)S(1)}, f32[64,704]{1,0:T(8,128)S(1)}, u32[]{:S(2)}, u32[]{:S(2)}) collective-permute-start(f32[64,704]{1,0:T(8,128)S(1)} %pad.37), channel_id=1, source_target_pairs={{0,2},{1,3},{2,4},{3,5},{4,6},{5,7},{6,8},{7,9},{8,10},{9,11},{10,... | collective-permute-start | bytes 540680 | tf_op jit(solution)/shard_map/ppermute | solution.py:12
  127.5 0.1 pad.38
  127.6 6.8 %collective-permute-start.4 = (f32[64,704]{1,0:T(8,128)S(1)}, f32[64,704]{1,0:T(8,128)S(1)}, u32[]{:S(2)}, u32[]{:S(2)}) collective-permute-start(f32[64,704]{1,0:T(8,128)S(1)} %pad.38), channel_id=1, source_target_pairs={{1,0},{2,1},{3,2},{4,3},{5,4},{6,5},{7,6},{8,7},{9,8},{10,9},{11,1... | collective-permute-start | bytes 540680 | tf_op jit(solution)/shard_map/ppermute | solution.py:12
  134.4 3.9 %collective-permute-start.5 = (f32[64,704]{1,0:T(8,128)S(1)}, f32[64,704]{1,0:T(8,128)S(1)}, u32[]{:S(2)}, u32[]{:S(2)}) collective-permute-start(f32[64,704]{1,0:T(8,128)S(1)} %pad.39), channel_id=1, source_target_pairs={{2,0},{3,1},{4,2},{5,3},{6,4},{7,5},{8,6},{9,7},{10,8},{11,9},{12,... | collective-permute-start | bytes 540680 | tf_op jit(solution)/shard_map/ppermute | solution.py:12
  138.4 1.7 %collective-permute-done.3 = f32[64,704]{1,0:T(8,128)S(1)} collective-permute-done((f32[64,704]{1,0:T(8,128)S(1)}, f32[64,704]{1,0:T(8,128)S(1)}, u32[]{:S(2)}, u32[]{:S(2)}) %collective-permute-start.3) | collective-permute-done | bytes 180256 | tf_op jit(solution)/shard_map/ppermute | solution.py:12
  140.1 15.4 %collective-permute-done.5 = f32[64,704]{1,0:T(8,128)S(1)} collective-permute-done((f32[64,704]{1,0:T(8,128)S(1)}, f32[64,704]{1,0:T(8,128)S(1)}, u32[]{:S(2)}, u32[]{:S(2)}) %collective-permute-start.5) | collective-permute-done | bytes 180256 | tf_op jit(solution)/shard_map/ppermute | solution.py:12
  155.5 0.7 add_bitcast_fusion
  (20 shorter events, 0.3 us)
Async XLA Ops:
  0.0 14.3 %copy-start.1 = (f32[12,64,320]{2,1,0:T(8,128)S(1)}, f32[12,64,320]{2,1,0:T(8,128)}, u32[]{:S(2)}) copy-start(f32[12,64,320]{2,1,0:T(8,128)} %param.8) | copy-start | bytes 2949124
  2.5 19.8 %copy-start.2 = (f32[12,64,320]{2,1,0:T(8,128)}, f32[12,64,320]{2,1,0:T(8,128)S(1)}, u32[]{:S(2)}) copy-start(f32[12,64,320]{2,1,0:T(8,128)S(1)} %broadcast_multiply_fusion) | copy-start | bytes 2949124
  2.5 35.0 %collective-permute-start = (f32[12,64,320]{2,1,0:T(8,128)S(1)}, f32[12,64,320]{2,1,0:T(8,128)S(1)}, u32[]{:S(2)}, u32[]{:S(2)}) collective-permute-start(f32[12,64,320]{2,1,0:T(8,128)S(1)} %broadcast_multiply_fusion), channel_id=1, source_target_pairs={{0,1},{1,2},{2,3},{3,4},{4,5},{5,6},{6,7},{7,8},{8,9},{9,10},{10,1... | collective-permute-start | bytes 2949128 | tf_op jit(solution)/shard_map/ppermute | solution.py:12
  6.9 54.5 %collective-permute-start.1 = (f32[12,64,320]{2,1,0:T(8,128)S(1)}, f32[12,64,320]{2,1,0:T(8,128)}, u32[]{:S(2)}, u32[]{:S(2)}) collective-permute-start(f32[12,64,320]{2,1,0:T(8,128)S(1)} %broadcast_multiply_fusion), channel_id=1, source_target_pairs={{1,0},{2,1},{3,2},{4,3},{5,4},{6,5},{7,6},{8,7},{9,8},{10,9},{11,1... | collective-permute-start | bytes 2949128 | tf_op jit(solution)/shard_map/ppermute | solution.py:12
  17.0 6.0 %copy-start.5 = (s32[12]{0:T(128)S(1)}, s32[12]{0:T(128)}, u32[]{:S(2)}) copy-start(s32[12]{0:T(128)} %param.7) | copy-start | bytes 148
  37.5 1.0 copy-start.3
  71.0 23.0 %copy-start.4 = (pred[12,14]{1,0:T(8,128)(4,1)S(1)}, pred[12,14]{1,0:T(8,128)(4,1)}, u32[]{:S(2)}) copy-start(pred[12,14]{1,0:T(8,128)(4,1)} %iota_compare_fusion.1) | copy-start | bytes 508
  118.7 1.5 copy-start
  122.9 15.5 %collective-permute-start.2 = (f32[64,704]{1,0:T(8,128)S(1)}, f32[64,704]{1,0:T(8,128)S(1)}, u32[]{:S(2)}, u32[]{:S(2)}) collective-permute-start(f32[64,704]{1,0:T(8,128)S(1)} %pad.36), channel_id=1, source_target_pairs={{0,1},{1,2},{2,3},{3,4},{4,5},{5,6},{6,7},{7,8},{8,9},{9,10},{10,1... | collective-permute-start | bytes 540680 | tf_op jit(solution)/shard_map/ppermute | solution.py:12
  125.1 14.9 %collective-permute-start.3 = (f32[64,704]{1,0:T(8,128)S(1)}, f32[64,704]{1,0:T(8,128)S(1)}, u32[]{:S(2)}, u32[]{:S(2)}) collective-permute-start(f32[64,704]{1,0:T(8,128)S(1)} %pad.37), channel_id=1, source_target_pairs={{0,2},{1,3},{2,4},{3,5},{4,6},{5,7},{6,8},{7,9},{8,10},{9,11},{10,... | collective-permute-start | bytes 540680 | tf_op jit(solution)/shard_map/ppermute | solution.py:12
  127.6 12.4 %collective-permute-start.4 = (f32[64,704]{1,0:T(8,128)S(1)}, f32[64,704]{1,0:T(8,128)S(1)}, u32[]{:S(2)}, u32[]{:S(2)}) collective-permute-start(f32[64,704]{1,0:T(8,128)S(1)} %pad.38), channel_id=1, source_target_pairs={{1,0},{2,1},{3,2},{4,3},{5,4},{6,5},{7,6},{8,7},{9,8},{10,9},{11,1... | collective-permute-start | bytes 540680 | tf_op jit(solution)/shard_map/ppermute | solution.py:12
  134.4 21.0 %collective-permute-start.5 = (f32[64,704]{1,0:T(8,128)S(1)}, f32[64,704]{1,0:T(8,128)S(1)}, u32[]{:S(2)}, u32[]{:S(2)}) collective-permute-start(f32[64,704]{1,0:T(8,128)S(1)} %pad.39), channel_id=1, source_target_pairs={{2,0},{3,1},{4,2},{5,3},{6,4},{7,5},{8,6},{9,7},{10,8},{11,9},{12,... | collective-permute-start | bytes 540680 | tf_op jit(solution)/shard_map/ppermute | solution.py:12
where the time goes:
time: 157 us; the launch traced here: 156 us
  waiting for transfers between devices  53.2 us (34%)
  matrix products  46.9 us (30%)
  starting transfers between devices  27.1 us (17%)
  local copies, waits for them, and re-layouts  21 us (13%)
  other arithmetic  7.72 us (5%)
    ppermute x6, waiting for transfers between devices, from_behind(): return lax.ppermute(array, axis, pairs)  53.2 us
    ppermute x6, starting transfers between devices, from_behind(): return lax.ppermute(array, axis, pairs)  27.1 us
    dot_general x1, matrix products, shards(): jnp.einsum('ifkg,ikgc->ikfc', matrix_rows, gathered, precision=FULL_PRECI...  23 us
    dot_general x1, matrix products, shards(): jnp.einsum('ikd,ikfc->idfc', weights, products, precision=FULL_PRECISION)  21.5 us
    gather x1, local copies, waits for them, and re-layouts, shards(): jnp.take(widened, local_cols.reshape(-1), axis=0)  7.41 us
    reshape x1, local copies, waits for them, and re-layouts, shards(): matrix_rows = a_vals.reshape(rows_here, block_size, slot_count, block_size)  5.37 us
    unnamed x14, local copies, waits for them, and re-layouts  4.31 us
  transfers between devices with their start and end apart: 6, of which 4 were waited for; matrix products, arithmetic and copies ran while one was open for 6% of the time, Pallas kernels for 0%

commit v1 on v0

v1 whole, which is shorter than its diff:
```python
import jax
import jax.numpy as jnp
from jax import lax
from jax.sharding import PartitionSpec as P

FULL_PRECISION = lax.Precision.HIGHEST


def from_behind(array, axis, by):
    count = lax.axis_size(axis)
    pairs = [(i, i + by) for i in range(count) if 0 <= i + by < count]
    return lax.ppermute(array, axis, pairs)


def mm(a, b):
    return jnp.dot(a, b, precision=FULL_PRECISION, preferred_element_type=jnp.float32)


def shards(a_vals, a_cols, a_count, p_vals, p_mask):
    rows_here = a_cols.shape[0]
    slot_count = a_cols.shape[1]
    block_size = a_vals.shape[1]
    prol_slots = p_mask.shape[1]
    group_total = lax.axis_size("rows") * lax.axis_size("cols")
    position = lax.axis_index("rows") * lax.axis_size("cols") + lax.axis_index("cols")
    slot_ids = jnp.arange(prol_slots, dtype=jnp.int32)
    target = position + slot_ids - 2
    inside = ((target >= 0) & (target < group_total)).astype(jnp.float32)
    keep_mask = p_mask.astype(jnp.float32) * inside[None, :]
    pblocks = (
        p_vals.reshape(rows_here, block_size, prol_slots, block_size) * keep_mask[:, None, :, None]
    )
    pflat = pblocks.reshape(rows_here, block_size, prol_slots * block_size)
    lower_rows = from_behind(pflat, ("rows", "cols"), 1)
    upper_rows = from_behind(pflat, ("rows", "cols"), -1)

    local_cols = a_cols - (position - 1) * rows_here
    live_mask = jnp.arange(slot_count, dtype=jnp.int32)[None, :] < a_count[:, None]
    col_ids = jnp.arange(3 * rows_here, dtype=jnp.int32)
    onehot = (live_mask[:, :, None] & (local_cols[:, :, None] == col_ids[None, None, :])).astype(
        jnp.float32
    )
    matrix_rows = a_vals.reshape(rows_here, block_size, slot_count, block_size)
    dense = jnp.einsum("ifkg,ikn->ifng", matrix_rows, onehot, precision=FULL_PRECISION)
    dense = dense.reshape(rows_here * block_size, 3 * rows_here * block_size)
    span = rows_here * block_size
    width = prol_slots * block_size
    own = mm(dense[:, span : 2 * span], pflat.reshape(span, width))
    low = mm(dense[:, :span], lower_rows.reshape(span, width))
    high = mm(dense[:, 2 * span :], upper_rows.reshape(span, width))
    ap_rows = (
        jnp.pad(low, ((0, 0), (0, 2 * block_size)))
        + jnp.pad(own, ((0, 0), (block_size, block_size)))
        + jnp.pad(high, ((0, 0), (2 * block_size, 0)))
    )
    terms = lax.dot_general(
        pflat.reshape(span, width),
        ap_rows,
        (((0,), (0,)), ((), ())),
        precision=FULL_PRECISION,
        preferred_element_type=jnp.float32,
    ).reshape(prol_slots, block_size, (prol_slots + 2) * block_size)

    def spread(s, block):
        return jnp.pad(block, ((0, 0), ((prol_slots - 1 - s) * block_size, s * block_size)))

    result = spread(2, terms[2])
    result = result + spread(3, from_behind(terms[3], ("rows", "cols"), 1))
    result = result + spread(4, from_behind(terms[4], ("rows", "cols"), 2))
    result = result + spread(1, from_behind(terms[1], ("rows", "cols"), -1))
    result = result + spread(0, from_behind(terms[0], ("rows", "cols"), -2))
    return result.reshape(1, block_size, (prol_slots + 6) * block_size)


def solution(mesh):
    in_specs = (
        P(("rows", "cols"), None, None),
        P(("rows", "cols"), None),
        P(("rows", "cols")),
        P(("rows", "cols"), None, None),
        P(("rows", "cols"), None),
    )
    out_specs = P(("rows", "cols"), None, None)
    return jax.shard_map(shards, mesh=mesh, in_specs=in_specs, out_specs=out_specs, check_vma=False)
```

time: 157 us -> 96.4 us (0.61)
  waiting for transfers between devices: 53.2 us -> 6.58 us
  matrix products: 46.9 us -> 28.2 us
  local copies, waits for them, and re-layouts: 21 us -> 26.5 us
  other arithmetic: 7.72 us -> 5.98 us
    ppermute x6, waiting for transfers between devices: 53.2 us -> 6.58 us  [from_behind(): return lax.ppermute(array, axis, pairs)]
    dot_general x3 -> x5, matrix products: 46.9 us -> 28.2 us  [the longest x3 12.5 us: mm(): jnp.dot(a, b, precision=FULL_PRECISION, preferred_element_type=jnp.float32)]
    reshape x1, local copies, waits for them, and re-layouts: 0.08 us -> 13.3 us  [shards(): dense = dense.reshape(rows_here * block_size, 3 * rows_here * block_size)]
    gather x1 -> x0, local copies, waits for them, and re-layouts: 7.41 us -> none  [shards(): jnp.take(widened, local_cols.reshape(-1), axis=0)]
    mul x2 -> x5, local copies, waits for them, and re-layouts: 0.15 us -> 7.54 us  [shards(): p_vals.reshape(rows_here, block_size, prol_slots, block_size)]
    unnamed x14 -> x8, local copies, waits for them, and re-layouts: 4.31 us -> 0.02 us
    slice x1, local copies, waits for them, and re-layouts: 3.1 us -> 0.05 us  [shards(): result = spread(2, terms[2])]
    mul x1 -> x2, other arithmetic: 1.38 us -> 4.31 us  [shards(): p_vals.reshape(rows_here, block_size, prol_slots, block_size)]
  transfers between devices with their start and end apart: 6 -> 6, of which waited for: 4 -> 1; matrix products, arithmetic and copies ran while one was open for 6% -> 51% of each run, Pallas kernels for 0% -> 0%
where the time goes in v1:
time: 96.4 us; the launch traced here: 94.5 us
  matrix products  28.2 us (29%)
  starting transfers between devices  27.1 us (28%)
  local copies, waits for them, and re-layouts  26.5 us (27%)
  waiting for transfers between devices  6.58 us (7%)
  other arithmetic  5.98 us (6%)
    ppermute x6, starting transfers between devices, from_behind(): return lax.ppermute(array, axis, pairs)  27.1 us
    reshape x1, local copies, waits for them, and re-layouts, shards(): dense = dense.reshape(rows_here * block_size, 3 * rows_here * block_size)  13.3 us
    dot_general x3, matrix products, mm(): jnp.dot(a, b, precision=FULL_PRECISION, preferred_element_type=jnp.float32)  12.5 us
    dot_general x1, matrix products, shards(): jnp.einsum('ifkg,ikn->ifng', matrix_rows, onehot, precision=FULL_PRECISION)  11.8 us
    mul x5, local copies, waits for them, and re-layouts, shards(): p_vals.reshape(rows_here, block_size, prol_slots, block_size)  7.54 us
    ppermute x6, waiting for transfers between devices, from_behind(): return lax.ppermute(array, axis, pairs)  6.58 us
    reshape x1, local copies, waits for them, and re-layouts, shards(): matrix_rows = a_vals.reshape(rows_here, block_size, slot_count, block_size)  5.55 us
    mul x2, other arithmetic, shards(): p_vals.reshape(rows_here, block_size, prol_slots, block_size)  4.31 us
  transfers between devices with their start and end apart: 6, of which 1 were waited for; matrix products, arithmetic and copies ran while one was open for 51% of the time, Pallas kernels for 0%

profile of v1, /device:TPU:1, one launch (start us, length us, event | category | flops | bytes accessed | tf_op | source)
XLA Modules:
  0.0 94.5 jit_solution(12072573508701874673)
XLA Ops:
  0.0 0.8 convert_multiply_fusion
  0.8 0.1 copy.11
  0.9 0.1 mul.41
  0.9 0.1 mul.42
  1.0 2.4 %broadcast_multiply_fusion = f32[12,64,320]{2,1,0:T(8,128)} fusion(f32[12,64,320]{2,1,0:T(8,128)} %param.8, f32[12,320]{1,0:T(8,128)S(1)} %mul.42), kind=kLoop, calls=%fused_computation.14 | loop fusion | flops 245760 | bytes 1981440 | tf_op jit(solution)/shard_map/mul | solution.py:31
  3.4 9.8 %collective-permute-start.1 = (f32[12,64,320]{2,1,0:T(8,128)}, f32[12,64,320]{2,1,0:T(8,128)}, u32[]{:S(2)}, u32[]{:S(2)}) collective-permute-start(f32[12,64,320]{2,1,0:T(8,128)} %broadcast_multiply_fusion), channel_id=1, source_target_pairs={{1,0},{2,1},{3,2},{4,3},{5,4},{6,5},{7,6},{8,7},{9,8},{10,9},{11,1... | collective-permute-start | bytes 2949128 | tf_op jit(solution)/shard_map/ppermute | solution.py:12
  13.3 1.9 %collective-permute-start = (f32[12,64,320]{2,1,0:T(8,128)}, f32[12,64,320]{2,1,0:T(8,128)}, u32[]{:S(2)}, u32[]{:S(2)}) collective-permute-start(f32[12,64,320]{2,1,0:T(8,128)} %broadcast_multiply_fusion), channel_id=1, source_target_pairs={{0,1},{1,2},{2,3},{3,4},{4,5},{5,6},{6,7},{7,8},{8,9},{9,10},{10,1... | collective-permute-start | bytes 2949128 | tf_op jit(solution)/shard_map/ppermute | solution.py:12
  15.2 0.0 copy-start.1
  15.2 0.0 copy-start
  15.2 5.5 %reshape.66 = f32[12,64,14,64]{3,2,1,0:T(8,128)} reshape(f32[12,64,896]{2,1,0:T(8,128)} %param.5) | data formatting | bytes 5505024 | tf_op jit(solution)/shard_map/reshape | solution.py:43
  20.8 0.1 iota_compare_fusion.1
  20.9 11.8 %convolution_bitcast_fusion = f32[12,64,36,64]{3,2,1,0:T(8,128)} fusion(f32[12,64,14,64]{3,2,1,0:T(8,128)} %reshape.66, s32[12,14]{1,0:T(8,128)S(1)} %broadcast_subtract_fusion, pred[12,14]{1,0:T(8,128)(4,1)S(1)} %iota_compare_fusion.1), kind=kOutput, calls=%fused_computation | convolution fusion | flops 297283392 | bytes 9831240 | tf_op jit(solution)/shard_map/ifkg,ikn->ifng/dot_general | solution.py:44
  32.6 13.3 %reshape.67 = f32[768,2304]{1,0:T(8,128)} reshape(f32[12,64,36,64]{3,2,1,0:T(8,128)} %convolution_bitcast_fusion) | data formatting | bytes 14155776 | tf_op jit(solution)/shard_map/reshape | solution.py:45
  45.9 1.7 %mul.37 = f32[12,64,5,64]{1,0,3,2:T(8,128)} broadcast(f32[12,5]{0,1:T(8,128)S(1)} %convert_multiply_fusion), dimensions={0,2} | broadcast | bytes 983280 | tf_op jit(solution)/shard_map/mul | solution.py:31
  47.6 3.0 %mul.38 = f32[768,320]{0,1:T(8,128)} reshape(f32[12,64,5,64]{1,0,3,2:T(8,128)} %mul.37) | data formatting | bytes 1966080 | tf_op jit(solution)/shard_map/mul | solution.py:31
  50.7 2.6 %copy.10 = f32[768,320]{1,0:T(8,128)} copy(f32[768,320]{0,1:T(8,128)} %mul.38) | data formatting | bytes 1966080 | tf_op jit(solution)/shard_map/mul | solution.py:31
  53.3 1.9 %bitcast_multiply_fusion = f32[768,320]{1,0:T(8,128)S(1)} fusion(f32[768,320]{1,0:T(8,128)} %copy.10, f32[12,64,320]{2,1,0:T(8,128)} %param.8), kind=kLoop, calls=%fused_computation.13 | loop fusion | flops 245760 | bytes 2949120 | tf_op jit(solution)/shard_map/mul | solution.py:31
  55.2 4.6 %fusion.2 = f32[768,320]{0,1:T(8,128)S(1)} fusion(f32[768,320]{1,0:T(8,128)S(1)} %bitcast_multiply_fusion, f32[768,2304]{1,0:T(8,128)} %reshape.67), kind=kOutput, calls=%fused_computation.3 | convolution fusion | flops 2264924160 | bytes 4325376 | tf_op jit(solution)/shard_map/dot_general | solution.py:16
  59.8 0.0 collective-permute-done.1
  59.9 3.9 %fusion = f32[768,320]{0,1:T(8,128)S(1)} fusion(f32[768,320]{1,0:T(8,128)} %bitcast.5, f32[768,2304]{1,0:T(8,128)S(1)} %bitcast.21), kind=kOutput, calls=%fused_computation.1 | convolution fusion | flops 2264924160 | bytes 4325376 | tf_op jit(solution)/shard_map/dot_general | solution.py:16
  63.8 0.0 collective-permute-done
  63.8 3.9 %fusion.4 = f32[768,320]{0,1:T(8,128)S(1)} fusion(f32[768,320]{1,0:T(8,128)} %bitcast.4, f32[768,2304]{1,0:T(8,128)S(1)} %bitcast.21), kind=kOutput, calls=%fused_computation.5 | convolution fusion | flops 2264924160 | bytes 4325376 | tf_op jit(solution)/shard_map/dot_general | solution.py:16
  67.8 3.9 %fusion.6 = f32[320,448]{1,0:T(8,128)S(1)} fusion(f32[768,320]{1,0:T(8,128)S(1)} %bitcast_multiply_fusion, f32[768,320]{0,1:T(8,128)S(1)} %fusion, f32[768,320]{0,1:T(8,128)S(1)} %fusion.2, f32[768,320]{0,1:T(8,128)S(1)} %fusion.4), kind=kOutput, calls=%fused_computation.7 | convolution fusion | flops 1321893888 | bytes 4505600 | tf_op jit(solution)/shard_map/dot_general | solution.py:56
  71.7 1.9 %collective-permute-start.2 = (f32[64,448]{1,0:T(8,128)S(1)}, f32[64,448]{1,0:T(8,128)S(1)}, u32[]{:S(2)}, u32[]{:S(2)}) collective-permute-start(f32[64,448]{1,0:T(8,128)S(1)} %get-tuple-element.9), channel_id=1, source_target_pairs={{0,1},{1,2},{2,3},{3,4},{4,5},{5,6},{6,7},{7,8},{8,9},{9,10},{10,1... | collective-permute-start | bytes 344072 | tf_op jit(solution)/shard_map/ppermute | solution.py:12
  73.7 3.6 %collective-permute-start.3 = (f32[64,448]{1,0:T(8,128)S(1)}, f32[64,448]{1,0:T(8,128)S(1)}, u32[]{:S(2)}, u32[]{:S(2)}) collective-permute-start(f32[64,448]{1,0:T(8,128)S(1)} %get-tuple-element.8), channel_id=1, source_target_pairs={{0,2},{1,3},{2,4},{3,5},{4,6},{5,7},{6,8},{7,9},{8,10},{9,11},{10,... | collective-permute-start | bytes 344072 | tf_op jit(solution)/shard_map/ppermute | solution.py:12
  77.3 5.9 %collective-permute-start.4 = (f32[64,448]{1,0:T(8,128)S(1)}, f32[64,448]{1,0:T(8,128)S(1)}, u32[]{:S(2)}, u32[]{:S(2)}) collective-permute-start(f32[64,448]{1,0:T(8,128)S(1)} %get-tuple-element.7), channel_id=1, source_target_pairs={{1,0},{2,1},{3,2},{4,3},{5,4},{6,5},{7,6},{8,7},{9,8},{10,9},{11,1... | collective-permute-start | bytes 344072 | tf_op jit(solution)/shard_map/ppermute | solution.py:12
  83.2 3.9 %collective-permute-start.5 = (f32[64,448]{1,0:T(8,128)S(1)}, f32[64,448]{1,0:T(8,128)S(1)}, u32[]{:S(2)}, u32[]{:S(2)}) collective-permute-start(f32[64,448]{1,0:T(8,128)S(1)} %get-tuple-element.6), channel_id=1, source_target_pairs={{2,0},{3,1},{4,2},{5,3},{6,4},{7,5},{8,6},{9,7},{10,8},{11,9},{12,... | collective-permute-start | bytes 344072 | tf_op jit(solution)/shard_map/ppermute | solution.py:12
  87.1 0.0 collective-permute-done.2
  87.1 0.0 collective-permute-done.3
  87.1 0.0 collective-permute-done.4
  87.1 6.6 %collective-permute-done.5 = f32[64,448]{1,0:T(8,128)S(1)} collective-permute-done((f32[64,448]{1,0:T(8,128)S(1)}, f32[64,448]{1,0:T(8,128)S(1)}, u32[]{:S(2)}, u32[]{:S(2)}) %collective-permute-start.5) | collective-permute-done | bytes 114720 | tf_op jit(solution)/shard_map/ppermute | solution.py:12
  93.7 0.8 add_bitcast_fusion
  (10 shorter events, 0.1 us)
Async XLA Ops:
  3.4 56.4 %collective-permute-start.1 = (f32[12,64,320]{2,1,0:T(8,128)}, f32[12,64,320]{2,1,0:T(8,128)}, u32[]{:S(2)}, u32[]{:S(2)}) collective-permute-start(f32[12,64,320]{2,1,0:T(8,128)} %broadcast_multiply_fusion), channel_id=1, source_target_pairs={{1,0},{2,1},{3,2},{4,3},{5,4},{6,5},{7,6},{8,7},{9,8},{10,9},{11,1... | collective-permute-start | bytes 2949128 | tf_op jit(solution)/shard_map/ppermute | solution.py:12
  13.3 50.5 %collective-permute-start = (f32[12,64,320]{2,1,0:T(8,128)}, f32[12,64,320]{2,1,0:T(8,128)}, u32[]{:S(2)}, u32[]{:S(2)}) collective-permute-start(f32[12,64,320]{2,1,0:T(8,128)} %broadcast_multiply_fusion), channel_id=1, source_target_pairs={{0,1},{1,2},{2,3},{3,4},{4,5},{5,6},{6,7},{7,8},{8,9},{9,10},{10,1... | collective-permute-start | bytes 2949128 | tf_op jit(solution)/shard_map/ppermute | solution.py:12
  15.2 5.6 %copy-start.1 = (s32[12]{0:T(128)S(1)}, s32[12]{0:T(128)}, u32[]{:S(2)}) copy-start(s32[12]{0:T(128)} %param.7) | copy-start | bytes 148
  15.2 5.6 %copy-start = (s32[12,14]{1,0:T(8,128)S(1)}, s32[12,14]{1,0:T(8,128)}, u32[]{:S(2)}) copy-start(s32[12,14]{1,0:T(8,128)} %param.6) | copy-start | bytes 2020
  47.6 12.2 %slice-start = ((s8[7077888]{0:T(1024)(128)(4,1)}), s8[2883584]{0:T(1024)(128)(4,1)S(1)}, s32[]{:S(2)}) async-start(s8[7077888]{0:T(1024)(128)(4,1)} %bitcast.20), calls=%async_computation | async-start | bytes 5767168
  53.3 6.6 %slice-start.1 = ((s8[7077888]{0:T(1024)(128)(4,1)}), s8[4194304]{0:T(1024)(128)(4,1)S(1)}, s32[]{:S(2)}) async-start(s8[7077888]{0:T(1024)(128)(4,1)} %bitcast.20), calls=%async_computation.1 | async-start | bytes 8388608
  71.7 15.3 %collective-permute-start.2 = (f32[64,448]{1,0:T(8,128)S(1)}, f32[64,448]{1,0:T(8,128)S(1)}, u32[]{:S(2)}, u32[]{:S(2)}) collective-permute-start(f32[64,448]{1,0:T(8,128)S(1)} %get-tuple-element.9), channel_id=1, source_target_pairs={{0,1},{1,2},{2,3},{3,4},{4,5},{5,6},{6,7},{7,8},{8,9},{9,10},{10,1... | collective-permute-start | bytes 344072 | tf_op jit(solution)/shard_map/ppermute | solution.py:12
  73.7 13.4 %collective-permute-start.3 = (f32[64,448]{1,0:T(8,128)S(1)}, f32[64,448]{1,0:T(8,128)S(1)}, u32[]{:S(2)}, u32[]{:S(2)}) collective-permute-start(f32[64,448]{1,0:T(8,128)S(1)} %get-tuple-element.8), channel_id=1, source_target_pairs={{0,2},{1,3},{2,4},{3,5},{4,6},{5,7},{6,8},{7,9},{8,10},{9,11},{10,... | collective-permute-start | bytes 344072 | tf_op jit(solution)/shard_map/ppermute | solution.py:12
  77.3 9.9 %collective-permute-start.4 = (f32[64,448]{1,0:T(8,128)S(1)}, f32[64,448]{1,0:T(8,128)S(1)}, u32[]{:S(2)}, u32[]{:S(2)}) collective-permute-start(f32[64,448]{1,0:T(8,128)S(1)} %get-tuple-element.7), channel_id=1, source_target_pairs={{1,0},{2,1},{3,2},{4,3},{5,4},{6,5},{7,6},{8,7},{9,8},{10,9},{11,1... | collective-permute-start | bytes 344072 | tf_op jit(solution)/shard_map/ppermute | solution.py:12
  83.2 10.5 %collective-permute-start.5 = (f32[64,448]{1,0:T(8,128)S(1)}, f32[64,448]{1,0:T(8,128)S(1)}, u32[]{:S(2)}, u32[]{:S(2)}) collective-permute-start(f32[64,448]{1,0:T(8,128)S(1)} %get-tuple-element.6), channel_id=1, source_target_pairs={{2,0},{3,1},{4,2},{5,3},{6,4},{7,5},{8,6},{9,7},{10,8},{11,9},{12,... | collective-permute-start | bytes 344072 | tf_op jit(solution)/shard_map/ppermute | solution.py:12

commit v2 on v1

--- a/solution.py
+++ b/solution.py
@@ -39,20 +39,31 @@
     col_ids = jnp.arange(3 * rows_here, dtype=jnp.int32)
     onehot = (live_mask[:, :, None] & (local_cols[:, :, None] == col_ids[None, None, :])).astype(
         jnp.float32
-    )
-    matrix_rows = a_vals.reshape(rows_here, block_size, slot_count, block_size)
-    dense = jnp.einsum("ifkg,ikn->ifng", matrix_rows, onehot, precision=FULL_PRECISION)
-    dense = dense.reshape(rows_here * block_size, 3 * rows_here * block_size)
+    ).reshape(rows_here * slot_count, 3 * rows_here)
     span = rows_here * block_size
     width = prol_slots * block_size
-    own = mm(dense[:, span : 2 * span], pflat.reshape(span, width))
-    low = mm(dense[:, :span], lower_rows.reshape(span, width))
-    high = mm(dense[:, 2 * span :], upper_rows.reshape(span, width))
-    ap_rows = (
-        jnp.pad(low, ((0, 0), (0, 2 * block_size)))
-        + jnp.pad(own, ((0, 0), (block_size, block_size)))
-        + jnp.pad(high, ((0, 0), (2 * block_size, 0)))
+    wide = (prol_slots + 2) * block_size
+    flat_len = block_size * wide
+    matrix_rows = a_vals.reshape(rows_here, block_size, slot_count * block_size)
+
+    def gathered(weights, p_rows):
+        picked = mm(weights, p_rows.reshape(p_rows.shape[0], flat_len))
+        return picked.reshape(rows_here, slot_count * block_size, wide)
+
+    def times_a(picked):
+        return jnp.einsum("ifK,iKq->ifq", matrix_rows, picked, precision=FULL_PRECISION)
+
+    own_sh = jnp.pad(pflat, ((0, 0), (0, 0), (block_size, block_size)))
+    ap_own = times_a(gathered(onehot[:, rows_here : 2 * rows_here], own_sh))
+    side_sh = jnp.concatenate(
+        [
+            jnp.pad(lower_rows, ((0, 0), (0, 0), (0, 2 * block_size))),
+            jnp.pad(upper_rows, ((0, 0), (0, 0), (2 * block_size, 0))),
+        ],
+        axis=0,
     )
+    side_weights = jnp.concatenate([onehot[:, :rows_here], onehot[:, 2 * rows_here :]], axis=1)
+    ap_rows = (ap_own + times_a(gathered(side_weights, side_sh))).reshape(span, wide)
     terms = lax.dot_general(
         pflat.reshape(span, width),
         ap_rows,

time: 96.4 us -> 171 us (1.77)
  matrix products: 28.2 us -> 72.6 us
  local copies, waits for them, and re-layouts: 26.5 us -> 53.7 us
  other arithmetic: 5.98 us -> 9.36 us
    reshape x2 -> x4, local copies, waits for them, and re-layouts: 18.8 us -> 50.4 us  [the longest x2 42.9 us: gathered(): return picked.reshape(rows_here, slot_count * block_size, wide)]
    dot_general x1 -> x2, matrix products: 11.8 us -> 37.1 us  [times_a(): jnp.einsum('ifK,iKq->ifq', matrix_rows, picked, precision=FULL_PRECISION)]
    dot_general x3 -> x2, matrix products: 12.5 us -> 31.8 us  [mm(): jnp.dot(a, b, precision=FULL_PRECISION, preferred_element_type=jnp.float32)]
    mul x5 -> x2, local copies, waits for them, and re-layouts: 7.54 us -> 0.15 us  [shards(): p_vals.reshape(rows_here, block_size, prol_slots, block_size)]
    concatenate x0 -> x1, other arithmetic: none -> 3.71 us  [shards(): jnp.concatenate([jnp.pad(lower_rows, ((0, 0), (0, 0), (0, 2 * block_size)...]
    pad x0 -> x1, local copies, waits for them, and re-layouts: none -> 2.89 us  [shards(): own_sh = jnp.pad(pflat, ((0, 0), (0, 0), (block_size, block_size)))]
    mul x2 -> x1, other arithmetic: 4.31 us -> 2.45 us  [shards(): p_vals.reshape(rows_here, block_size, prol_slots, block_size)]
  transfers between devices with their start and end apart: 6 -> 6, of which waited for: 1 -> 1; matrix products, arithmetic and copies ran while one was open for 51% -> 36% of each run, Pallas kernels for 0% -> 0%
where the time goes in v2:
time: 171 us; the launch traced here: 169 us
  matrix products  72.6 us (42%)
  local copies, waits for them, and re-layouts  53.7 us (31%)
  starting transfers between devices  27.1 us (16%)
  other arithmetic  9.36 us (5%)
  waiting for transfers between devices  5.96 us (3%)
    reshape x2, local copies, waits for them, and re-layouts, gathered(): return picked.reshape(rows_here, slot_count * block_size, wide)  42.9 us
    dot_general x2, matrix products, times_a(): jnp.einsum('ifK,iKq->ifq', matrix_rows, picked, precision=FULL_PRECISION)  37.1 us
    dot_general x2, matrix products, mm(): jnp.dot(a, b, precision=FULL_PRECISION, preferred_element_type=jnp.float32)  31.8 us
    ppermute x6, starting transfers between devices, from_behind(): return lax.ppermute(array, axis, pairs)  27.1 us
    reshape x2, local copies, waits for them, and re-layouts, gathered(): picked = mm(weights, p_rows.reshape(p_rows.shape[0], flat_len))  7.52 us
    ppermute x6, waiting for transfers between devices, from_behind(): return lax.ppermute(array, axis, pairs)  5.96 us
    concatenate x1, other arithmetic, shards(): jnp.concatenate([jnp.pad(lower_rows, ((0, 0), (0, 0), (0, 2 * block_size)...  3.71 us
    dot_general x1, matrix products, shards(): lax.dot_general(pflat.reshape(span, width), ap_rows, (((0,), (0,)), ((),...  3.65 us
  transfers between devices with their start and end apart: 6, of which 1 were waited for; matrix products, arithmetic and copies ran while one was open for 36% of the time, Pallas kernels for 0%

profile of v2, /device:TPU:1, one launch (start us, length us, event | category | flops | bytes accessed | tf_op | source)
XLA Modules:
  0.0 168.8 jit_solution(11553055254913446496)
XLA Ops:
  0.0 0.9 convert_multiply_fusion
  0.9 0.1 copy.8
  1.0 0.1 mul.32
  1.1 0.1 mul.33
  1.2 2.4 %broadcast_multiply_fusion = f32[12,64,320]{2,1,0:T(8,128)} fusion(f32[12,64,320]{2,1,0:T(8,128)} %param.8, f32[12,320]{1,0:T(8,128)S(1)} %mul.33), kind=kLoop, calls=%fused_computation.7 | loop fusion | flops 245760 | bytes 1981440 | tf_op jit(solution)/shard_map/mul | solution.py:31
  3.6 4.4 %collective-permute-start = (f32[12,64,320]{2,1,0:T(8,128)}, f32[12,64,320]{2,1,0:T(8,128)}, u32[]{:S(2)}, u32[]{:S(2)}) collective-permute-start(f32[12,64,320]{2,1,0:T(8,128)} %broadcast_multiply_fusion), channel_id=1, source_target_pairs={{0,1},{1,2},{2,3},{3,4},{4,5},{5,6},{6,7},{7,8},{8,9},{9,10},{10,1... | collective-permute-start | bytes 2949128 | tf_op jit(solution)/shard_map/ppermute | solution.py:12
  8.0 7.4 %collective-permute-start.1 = (f32[12,64,320]{2,1,0:T(8,128)}, f32[12,64,320]{2,1,0:T(8,128)}, u32[]{:S(2)}, u32[]{:S(2)}) collective-permute-start(f32[12,64,320]{2,1,0:T(8,128)} %broadcast_multiply_fusion), channel_id=1, source_target_pairs={{1,0},{2,1},{3,2},{4,3},{5,4},{6,5},{7,6},{8,7},{9,8},{10,9},{11,1... | collective-permute-start | bytes 2949128 | tf_op jit(solution)/shard_map/ppermute | solution.py:12
  15.4 0.7 broadcast_subtract_fusion
  16.1 0.1 eq.17
  16.2 0.7 iota_compare_fusion.3
  16.9 0.1 lt.31
  17.0 2.9 %pad.32 = f32[12,64,448]{2,1,0:T(8,128)} pad(f32[12,64,320]{2,1,0:T(8,128)} %broadcast_multiply_fusion, f32[]{:T(128)} %constant.25.clone.1), padding=0_0x0_0x64_64 | pad | bytes 2359300 | tf_op jit(solution)/shard_map/jit(_pad)/pad | solution.py:56
  19.9 3.4 %reshape.73 = f32[12,28672]{1,0:T(8,128)} reshape(f32[12,64,448]{2,1,0:T(8,128)} %pad.32) | data formatting | bytes 2752512 | tf_op jit(solution)/shard_map/reshape | solution.py:50
  23.3 12.7 %fusion.11 = f32[168,28672]{1,0:T(8,128)} fusion(f32[12,28672]{1,0:T(8,128)} %reshape.73, pred[168,36]{0,1:T(8,128)(4,1)S(1)} %get-tuple-element.13), kind=kOutput, calls=%fused_computation.15 | convolution fusion | flops 693633024 | bytes 20647936 | tf_op jit(solution)/shard_map/dot_general | solution.py:16
  36.0 21.4 %reshape.74 = f32[12,896,448]{2,1,0:T(8,128)} reshape(f32[168,28672]{1,0:T(8,128)} %fusion.11) | data formatting | bytes 38535168 | tf_op jit(solution)/shard_map/reshape | solution.py:51
  57.5 19.2 %fusion.17 = f32[12,448,64]{1,2,0:T(8,128)} fusion(f32[12,896,448]{2,1,0:T(8,128)} %reshape.74, f32[12,64,896]{2,1,0:T(8,128)S(1)} %copy-done), kind=kOutput, calls=%fused_computation.25 | convolution fusion | flops 3699376128 | bytes 23396352 | tf_op jit(solution)/shard_map/ifK,iKq->ifq/dot_general | solution.py:54
  76.7 0.0 collective-permute-done
  76.7 0.0 collective-permute-done.1
  76.7 3.7 %select_maximum_fusion = f32[24,64,448]{2,1,0:T(8,128)} fusion(f32[12,64,320]{2,1,0:T(8,128)} %collective-permute-done.1, f32[12,64,320]{2,1,0:T(8,128)} %collective-permute-done), kind=kLoop, calls=%fused_computation | loop fusion | flops 3440640 | bytes 4718592 | tf_op jit(solution)/shard_map/concatenate | solution.py:58
  80.4 4.1 %reshape.75 = f32[24,28672]{1,0:T(8,128)} reshape(f32[24,64,448]{2,1,0:T(8,128)} %select_maximum_fusion) | data formatting | bytes 5505024 | tf_op jit(solution)/shard_map/reshape | solution.py:50
  84.5 19.1 %fusion.7 = f32[168,28672]{1,0:T(8,128)} fusion(f32[24,28672]{1,0:T(8,128)} %reshape.75, f32[168,12]{0,1:T(8,128)S(1)} %get-tuple-element.11, f32[168,12]{0,1:T(8,128)S(1)} %get-tuple-element.10), kind=kOutput, calls=%fused_computation.11 | convolution fusion | flops 1387270144 | bytes 22036224 | tf_op jit(solution)/shard_map/dot_general | solution.py:16
  103.6 21.4 %reshape.76 = f32[12,896,448]{2,1,0:T(8,128)} reshape(f32[168,28672]{1,0:T(8,128)} %fusion.7) | data formatting | bytes 38535168 | tf_op jit(solution)/shard_map/reshape | solution.py:51
  125.1 17.9 %fusion.18 = f32[12,448,64]{1,2,0:T(8,128)S(1)} fusion(f32[12,896,448]{2,1,0:T(8,128)} %reshape.76, f32[12,64,896]{2,1,0:T(8,128)S(1)} %copy-done), kind=kOutput, calls=%fused_computation.26 | convolution fusion | flops 3699376128 | bytes 23396352 | tf_op jit(solution)/shard_map/ifK,iKq->ifq/dot_general | solution.py:54
  143.0 3.6 %fusion.3 = f32[320,448]{1,0:T(8,128)S(1)} fusion(f32[12,64,320]{2,1,0:T(8,128)} %broadcast_multiply_fusion, f32[12,448,64]{1,2,0:T(8,128)S(1)} %copy-done.1, f32[12,448,64]{1,2,0:T(8,128)S(1)} %fusion.18), kind=kOutput, calls=%fused_computation.6 | convolution fusion | flops 1321549824 | bytes 4308992 | tf_op jit(solution)/shard_map/dot_general | solution.py:67
  146.7 1.9 %collective-permute-start.2 = (f32[64,448]{1,0:T(8,128)S(1)}, f32[64,448]{1,0:T(8,128)S(1)}, u32[]{:S(2)}, u32[]{:S(2)}) collective-permute-start(f32[64,448]{1,0:T(8,128)S(1)} %get-tuple-element.9), channel_id=1, source_target_pairs={{0,1},{1,2},{2,3},{3,4},{4,5},{5,6},{6,7},{7,8},{8,9},{9,10},{10,1... | collective-permute-start | bytes 344072 | tf_op jit(solution)/shard_map/ppermute | solution.py:12
  148.6 1.9 %collective-permute-start.3 = (f32[64,448]{1,0:T(8,128)S(1)}, f32[64,448]{1,0:T(8,128)S(1)}, u32[]{:S(2)}, u32[]{:S(2)}) collective-permute-start(f32[64,448]{1,0:T(8,128)S(1)} %get-tuple-element.8), channel_id=1, source_target_pairs={{0,2},{1,3},{2,4},{3,5},{4,6},{5,7},{6,8},{7,9},{8,10},{9,11},{10,... | collective-permute-start | bytes 344072 | tf_op jit(solution)/shard_map/ppermute | solution.py:12
  150.5 7.5 %collective-permute-start.4 = (f32[64,448]{1,0:T(8,128)S(1)}, f32[64,448]{1,0:T(8,128)S(1)}, u32[]{:S(2)}, u32[]{:S(2)}) collective-permute-start(f32[64,448]{1,0:T(8,128)S(1)} %get-tuple-element.7), channel_id=1, source_target_pairs={{1,0},{2,1},{3,2},{4,3},{5,4},{6,5},{7,6},{8,7},{9,8},{10,9},{11,1... | collective-permute-start | bytes 344072 | tf_op jit(solution)/shard_map/ppermute | solution.py:12
  158.1 3.9 %collective-permute-start.5 = (f32[64,448]{1,0:T(8,128)S(1)}, f32[64,448]{1,0:T(8,128)S(1)}, u32[]{:S(2)}, u32[]{:S(2)}) collective-permute-start(f32[64,448]{1,0:T(8,128)S(1)} %get-tuple-element.6), channel_id=1, source_target_pairs={{2,0},{3,1},{4,2},{5,3},{6,4},{7,5},{8,6},{9,7},{10,8},{11,9},{12,... | collective-permute-start | bytes 344072 | tf_op jit(solution)/shard_map/ppermute | solution.py:12
  162.0 0.0 collective-permute-done.3
  162.0 0.0 collective-permute-done.4
  162.1 5.9 %collective-permute-done.5 = f32[64,448]{1,0:T(8,128)S(1)} collective-permute-done((f32[64,448]{1,0:T(8,128)S(1)}, f32[64,448]{1,0:T(8,128)S(1)}, u32[]{:S(2)}, u32[]{:S(2)}) %collective-permute-start.5) | collective-permute-done | bytes 114720 | tf_op jit(solution)/shard_map/ppermute | solution.py:12
  168.0 0.8 add_bitcast_fusion
  (9 shorter events, 0.1 us)
Async XLA Ops:
  0.0 57.5 %copy-start = (f32[12,64,896]{2,1,0:T(8,128)S(1)}, f32[12,64,896]{2,1,0:T(8,128)}, u32[]{:S(2)}) copy-start(f32[12,64,896]{2,1,0:T(8,128)} %param.5) | copy-start | bytes 8257540
  3.6 73.1 %collective-permute-start = (f32[12,64,320]{2,1,0:T(8,128)}, f32[12,64,320]{2,1,0:T(8,128)}, u32[]{:S(2)}, u32[]{:S(2)}) collective-permute-start(f32[12,64,320]{2,1,0:T(8,128)} %broadcast_multiply_fusion), channel_id=1, source_target_pairs={{0,1},{1,2},{2,3},{3,4},{4,5},{5,6},{6,7},{7,8},{8,9},{9,10},{10,1... | collective-permute-start | bytes 2949128 | tf_op jit(solution)/shard_map/ppermute | solution.py:12
  8.0 68.7 %collective-permute-start.1 = (f32[12,64,320]{2,1,0:T(8,128)}, f32[12,64,320]{2,1,0:T(8,128)}, u32[]{:S(2)}, u32[]{:S(2)}) collective-permute-start(f32[12,64,320]{2,1,0:T(8,128)} %broadcast_multiply_fusion), channel_id=1, source_target_pairs={{1,0},{2,1},{3,2},{4,3},{5,4},{6,5},{7,6},{8,7},{9,8},{10,9},{11,1... | collective-permute-start | bytes 2949128 | tf_op jit(solution)/shard_map/ppermute | solution.py:12
  125.1 17.9 %copy-start.1 = (f32[12,448,64]{1,2,0:T(8,128)S(1)}, f32[12,448,64]{1,2,0:T(8,128)}, u32[]{:S(2)}) copy-start(f32[12,448,64]{1,2,0:T(8,128)} %fusion.17) | copy-start | bytes 4128772
  146.7 15.3 %collective-permute-start.2 = (f32[64,448]{1,0:T(8,128)S(1)}, f32[64,448]{1,0:T(8,128)S(1)}, u32[]{:S(2)}, u32[]{:S(2)}) collective-permute-start(f32[64,448]{1,0:T(8,128)S(1)} %get-tuple-element.9), channel_id=1, source_target_pairs={{0,1},{1,2},{2,3},{3,4},{4,5},{5,6},{6,7},{7,8},{8,9},{9,10},{10,1... | collective-permute-start | bytes 344072 | tf_op jit(solution)/shard_map/ppermute | solution.py:12
  148.6 13.4 %collective-permute-start.3 = (f32[64,448]{1,0:T(8,128)S(1)}, f32[64,448]{1,0:T(8,128)S(1)}, u32[]{:S(2)}, u32[]{:S(2)}) collective-permute-start(f32[64,448]{1,0:T(8,128)S(1)} %get-tuple-element.8), channel_id=1, source_target_pairs={{0,2},{1,3},{2,4},{3,5},{4,6},{5,7},{6,8},{7,9},{8,10},{9,11},{10,... | collective-permute-start | bytes 344072 | tf_op jit(solution)/shard_map/ppermute | solution.py:12
  150.5 11.5 %collective-permute-start.4 = (f32[64,448]{1,0:T(8,128)S(1)}, f32[64,448]{1,0:T(8,128)S(1)}, u32[]{:S(2)}, u32[]{:S(2)}) collective-permute-start(f32[64,448]{1,0:T(8,128)S(1)} %get-tuple-element.7), channel_id=1, source_target_pairs={{1,0},{2,1},{3,2},{4,3},{5,4},{6,5},{7,6},{8,7},{9,8},{10,9},{11,1... | collective-permute-start | bytes 344072 | tf_op jit(solution)/shard_map/ppermute | solution.py:12
  158.1 9.9 %collective-permute-start.5 = (f32[64,448]{1,0:T(8,128)S(1)}, f32[64,448]{1,0:T(8,128)S(1)}, u32[]{:S(2)}, u32[]{:S(2)}) collective-permute-start(f32[64,448]{1,0:T(8,128)S(1)} %get-tuple-element.6), channel_id=1, source_target_pairs={{2,0},{3,1},{4,2},{5,3},{6,4},{7,5},{8,6},{9,7},{10,8},{11,9},{12,... | collective-permute-start | bytes 344072 | tf_op jit(solution)/shard_map/ppermute | solution.py:12

commit v3 on v1

--- a/solution.py
+++ b/solution.py
@@ -1,9 +1,11 @@
 import jax
 import jax.numpy as jnp
 from jax import lax
+from jax.experimental import pallas as pl
+from jax.experimental.pallas import tpu as pltpu
 from jax.sharding import PartitionSpec as P
 
-FULL_PRECISION = lax.Precision.HIGHEST
+MATMUL_PRECISION = lax.Precision.HIGH
 
 
 def from_behind(array, axis, by):
@@ -13,7 +15,46 @@
 
 
 def mm(a, b):
-    return jnp.dot(a, b, precision=FULL_PRECISION, preferred_element_type=jnp.float32)
+    return jnp.dot(a, b, precision=MATMUL_PRECISION, preferred_element_type=jnp.float32)
+
+
+def dense_kernel(slot_ref, a_ref, out_ref):
+    sides, rows_here, block_size, span = out_ref.shape
+    per_side = span // block_size
+    lanes = 2 * block_size
+    left = lax.broadcasted_iota(jnp.int32, (block_size, lanes), 1) < block_size
+
+    def one_row(i, carry):
+        for d in range(sides):
+            for m in range(per_side // 2):
+                halves = []
+                for h in range(2):
+                    slot = slot_ref[(i * sides + d) * per_side + 2 * m + h]
+                    safe = jnp.maximum(slot, 0)
+                    start = pl.multiple_of((safe // 2) * lanes, lanes)
+                    tile = a_ref[i, :, pl.ds(start, lanes)]
+                    rolled = pltpu.roll(tile, block_size, 1)
+                    turn = (safe % 2) != h
+                    picked = jnp.where(turn, rolled, tile)
+                    halves.append(jnp.where(slot >= 0, picked, jnp.zeros_like(picked)))
+                out_ref[d, i, :, m * lanes : (m + 1) * lanes] = jnp.where(left, halves[0], halves[1])
+        return carry
+
+    lax.fori_loop(0, rows_here, one_row, 0)
+
+
+def dense_sides(slot_table, a_vals):
+    rows_here, block_size, _ = a_vals.shape
+    span = rows_here * block_size
+    return pl.pallas_call(
+        dense_kernel,
+        out_shape=jax.ShapeDtypeStruct((3, rows_here, block_size, span), jnp.float32),
+        in_specs=[
+            pl.BlockSpec(memory_space=pltpu.SMEM),
+            pl.BlockSpec(memory_space=pltpu.VMEM),
+        ],
+        out_specs=pl.BlockSpec(memory_space=pltpu.VMEM),
+    )(slot_table, a_vals)
 
 
 def shards(a_vals, a_cols, a_count, p_vals, p_mask):
@@ -37,17 +78,15 @@
     local_cols = a_cols - (position - 1) * rows_here
     live_mask = jnp.arange(slot_count, dtype=jnp.int32)[None, :] < a_count[:, None]
     col_ids = jnp.arange(3 * rows_here, dtype=jnp.int32)
-    onehot = (live_mask[:, :, None] & (local_cols[:, :, None] == col_ids[None, None, :])).astype(
-        jnp.float32
-    )
-    matrix_rows = a_vals.reshape(rows_here, block_size, slot_count, block_size)
-    dense = jnp.einsum("ifkg,ikn->ifng", matrix_rows, onehot, precision=FULL_PRECISION)
-    dense = dense.reshape(rows_here * block_size, 3 * rows_here * block_size)
+    hit = live_mask[:, :, None] & (local_cols[:, :, None] == col_ids[None, None, :])
+    slot_numbers = jnp.arange(1, slot_count + 1, dtype=jnp.int32)[None, :, None]
+    slot_table = (jnp.sum(jnp.where(hit, slot_numbers, 0), axis=1) - 1).reshape(-1)
     span = rows_here * block_size
     width = prol_slots * block_size
-    own = mm(dense[:, span : 2 * span], pflat.reshape(span, width))
-    low = mm(dense[:, :span], lower_rows.reshape(span, width))
-    high = mm(dense[:, 2 * span :], upper_rows.reshape(span, width))
+    dense = dense_sides(slot_table, a_vals).reshape(3, span, span)
+    own = mm(dense[1], pflat.reshape(span, width))
+    low = mm(dense[0], lower_rows.reshape(span, width))
+    high = mm(dense[2], upper_rows.reshape(span, width))
     ap_rows = (
         jnp.pad(low, ((0, 0), (0, 2 * block_size)))
         + jnp.pad(own, ((0, 0), (block_size, block_size)))
@@ -57,7 +96,7 @@
         pflat.reshape(span, width),
         ap_rows,
         (((0,), (0,)), ((), ())),
-        precision=FULL_PRECISION,
+        precision=MATMUL_PRECISION,
         preferred_element_type=jnp.float32,
     ).reshape(prol_slots, block_size, (prol_slots + 2) * block_size)
 

time: 96.4 us -> 98.7 us (1.024)
  the two profiles are of different devices: /device:TPU:1 before, /device:TPU:24 now
where the time goes in v3:
time: 98.7 us; the launch traced here: 98.3 us
  starting transfers between devices  52.2 us (53%)
  waiting for transfers between devices  13.5 us (14%)
  matrix products  10.8 us (11%)
  Pallas kernels  9.28 us (9%)
  local copies, waits for them, and re-layouts  8 us (8%)
  other arithmetic  4.37 us (4%)
    ppermute x6, starting transfers between devices, from_behind(): return lax.ppermute(array, axis, pairs)  52.2 us
    ppermute x6, waiting for transfers between devices, from_behind(): return lax.ppermute(array, axis, pairs)  13.5 us
    pallas_call x1, Pallas kernels, dense_sides(): pl.pallas_call(dense_kernel, out_shape=jax.ShapeDtypeStruct((3, rows_here...  9.28 us
    dot_general x3, matrix products, mm(): jnp.dot(a, b, precision=MATMUL_PRECISION, preferred_element_type=jnp.floa...  8.73 us
    slice x1, local copies, waits for them, and re-layouts, shards(): low = mm(dense[0], lower_rows.reshape(span, width))  3.64 us
    mul x5, local copies, waits for them, and re-layouts, shards(): p_vals.reshape(rows_here, block_size, prol_slots, block_size)  3.54 us
    mul x2, other arithmetic, shards(): p_vals.reshape(rows_here, block_size, prol_slots, block_size)  2.55 us
    dot_general x1, matrix products, shards(): lax.dot_general(pflat.reshape(span, width), ap_rows, (((0,), (0,)), ((),...  2.04 us
  transfers between devices with their start and end apart: 6, of which 4 were waited for; matrix products, arithmetic and copies ran while one was open for 14% of the time, Pallas kernels for 9%

profile of v3, /device:TPU:24, one launch (start us, length us, event | category | flops | bytes accessed | tf_op | source)
XLA Modules:
  0.0 98.3 jit_solution(14778439228334996984)
XLA Ops:
  0.0 0.8 convert_multiply_fusion
  0.8 0.1 copy.13
  0.9 0.1 mul.44
  0.9 0.1 mul.45
  1.0 2.4 %broadcast_multiply_fusion = f32[12,64,320]{2,1,0:T(8,128)} fusion(f32[12,64,320]{2,1,0:T(8,128)} %param.8, f32[12,320]{1,0:T(8,128)S(1)} %mul.45), kind=kLoop, calls=%fused_computation.7 | loop fusion | flops 245760 | bytes 1981440 | tf_op jit(solution)/shard_map/mul | solution.py:72
  3.4 13.2 %collective-permute-start.1 = (f32[12,64,320]{2,1,0:T(8,128)}, f32[12,64,320]{2,1,0:T(8,128)}, u32[]{:S(2)}, u32[]{:S(2)}) collective-permute-start(f32[12,64,320]{2,1,0:T(8,128)} %broadcast_multiply_fusion), channel_id=1, source_target_pairs={{1,0},{2,1},{3,2},{4,3},{5,4},{6,5},{7,6},{8,7},{9,8},{10,9},{11,1... | collective-permute-start | bytes 2949128 | tf_op jit(solution)/shard_map/ppermute | solution.py:14
  16.6 1.9 %collective-permute-start = (f32[12,64,320]{2,1,0:T(8,128)}, f32[12,64,320]{2,1,0:T(8,128)}, u32[]{:S(2)}, u32[]{:S(2)}) collective-permute-start(f32[12,64,320]{2,1,0:T(8,128)} %broadcast_multiply_fusion), channel_id=1, source_target_pairs={{0,1},{1,2},{2,3},{3,4},{4,5},{5,6},{6,7},{7,8},{8,9},{9,10},{10,1... | collective-permute-start | bytes 2949128 | tf_op jit(solution)/shard_map/ppermute | solution.py:14
  18.6 0.2 mul.40
  18.8 1.6 %mul.41 = f32[768,320]{0,1:T(8,128)} reshape(f32[12,64,5,64]{1,0,3,2:T(8,128)S(1)} %mul.40) | data formatting | bytes 1966080 | tf_op jit(solution)/shard_map/mul | solution.py:72
  20.4 1.6 %copy.12 = f32[768,320]{1,0:T(8,128)S(1)} copy(f32[768,320]{0,1:T(8,128)} %mul.41) | data formatting | bytes 1966080 | tf_op jit(solution)/shard_map/mul | solution.py:72
  22.0 0.0 copy-done.2
  22.0 0.1 iota_compare_fusion.1
  22.1 0.1 select_reduce_fusion
  22.2 0.7 sub.23.slot_ref
  22.9 9.3 %shard_map.55 = f32[3,12,64,768]{3,2,1,0:T(8,128)} custom-call(s32[432]{0:T(512)} %sub.23.slot_ref, f32[12,64,896]{2,1,0:T(8,128)} %a_ref.1), custom_call_target="tpu_custom_call" | custom-call | tf_op jit(solution)/shard_map/pallas_call | solution.py:49
  32.2 3.6 %fusion.8 = (f32[1,12,64,768]{3,2,1,0:T(8,128)S(1)}, f32[1,12,64,768]{3,2,1,0:T(8,128)S(1)}, f32[1,12,64,768]{3,2,1,0:T(8,128)S(1)}) fusion(f32[3,12,64,768]{3,2,1,0:T(8,128)} %shard_map.55), kind=kLoop, calls=%fused_computation.19 | loop fusion | bytes 14155776 | tf_op jit(solution)/shard_map/slice | solution.py:88
  35.8 0.1 bitcast_multiply_fusion
  36.0 2.9 %fusion.11 = f32[768,320]{0,1:T(8,128)S(1)} fusion(f32[768,768]{1,0:T(8,128)S(1)} %bitcast.21, f32[768,320]{1,0:T(8,128)} %bitcast.4), kind=kOutput, calls=%fused_computation.22 | convolution fusion | flops 1132462080 | bytes 4325376 | tf_op jit(solution)/shard_map/dot_general | solution.py:18
  38.9 0.8 collective-permute-done.1
  39.7 2.9 %fusion.12 = f32[768,320]{0,1:T(8,128)S(1)} fusion(f32[768,768]{1,0:T(8,128)S(1)} %bitcast.20, f32[768,320]{1,0:T(8,128)} %bitcast.6), kind=kOutput, calls=%fused_computation.23 | convolution fusion | flops 1132462080 | bytes 4325376 | tf_op jit(solution)/shard_map/dot_general | solution.py:18
  42.6 3.0 %collective-permute-done = f32[12,64,320]{2,1,0:T(8,128)} collective-permute-done((f32[12,64,320]{2,1,0:T(8,128)}, f32[12,64,320]{2,1,0:T(8,128)}, u32[]{:S(2)}, u32[]{:S(2)}) %collective-permute-start) | collective-permute-done | bytes 983072 | tf_op jit(solution)/shard_map/ppermute | solution.py:14
  45.6 2.9 %fusion.10 = f32[768,320]{0,1:T(8,128)S(1)} fusion(f32[768,768]{1,0:T(8,128)S(1)} %bitcast.19, f32[768,320]{1,0:T(8,128)} %bitcast.2), kind=kOutput, calls=%fused_computation.21 | convolution fusion | flops 1132462080 | bytes 4325376 | tf_op jit(solution)/shard_map/dot_general | solution.py:18
  48.5 2.0 %fusion = f32[320,448]{1,0:T(8,128)S(1)} fusion(f32[768,320]{1,0:T(8,128)S(1)} %bitcast_multiply_fusion, f32[768,320]{0,1:T(8,128)S(1)} %fusion.12, f32[768,320]{0,1:T(8,128)S(1)} %fusion.11, f32[768,320]{0,1:T(8,128)S(1)} %fusion.10), kind=kOutput, calls=%fused_computation | convolution fusion | flops 661291008 | bytes 4505600 | tf_op jit(solution)/shard_map/dot_general | solution.py:95
  50.6 28.4 %collective-permute-start.5 = (f32[64,448]{1,0:T(8,128)S(1)}, f32[64,448]{1,0:T(8,128)S(1)}, u32[]{:S(2)}, u32[]{:S(2)}) collective-permute-start(f32[64,448]{1,0:T(8,128)S(1)} %get-tuple-element.9), channel_id=1, source_target_pairs={{2,0},{3,1},{4,2},{5,3},{6,4},{7,5},{8,6},{9,7},{10,8},{11,9},{12,... | collective-permute-start | bytes 344072 | tf_op jit(solution)/shard_map/ppermute | solution.py:14
  79.1 1.9 %collective-permute-start.4 = (f32[64,448]{1,0:T(8,128)S(1)}, f32[64,448]{1,0:T(8,128)S(1)}, u32[]{:S(2)}, u32[]{:S(2)}) collective-permute-start(f32[64,448]{1,0:T(8,128)S(1)} %get-tuple-element.10), channel_id=1, source_target_pairs={{1,0},{2,1},{3,2},{4,3},{5,4},{6,5},{7,6},{8,7},{9,8},{10,9},{11,1... | collective-permute-start | bytes 344072 | tf_op jit(solution)/shard_map/ppermute | solution.py:14
  81.0 4.8 %collective-permute-start.3 = (f32[64,448]{1,0:T(8,128)S(1)}, f32[64,448]{1,0:T(8,128)S(1)}, u32[]{:S(2)}, u32[]{:S(2)}) collective-permute-start(f32[64,448]{1,0:T(8,128)S(1)} %get-tuple-element.11), channel_id=1, source_target_pairs={{0,2},{1,3},{2,4},{3,5},{4,6},{5,7},{6,8},{7,9},{8,10},{9,11},{10,... | collective-permute-start | bytes 344072 | tf_op jit(solution)/shard_map/ppermute | solution.py:14
  85.8 1.9 %collective-permute-start.2 = (f32[64,448]{1,0:T(8,128)S(1)}, f32[64,448]{1,0:T(8,128)S(1)}, u32[]{:S(2)}, u32[]{:S(2)}) collective-permute-start(f32[64,448]{1,0:T(8,128)S(1)} %get-tuple-element.12), channel_id=1, source_target_pairs={{0,1},{1,2},{2,3},{3,4},{4,5},{5,6},{6,7},{7,8},{8,9},{9,10},{10,1... | collective-permute-start | bytes 344072 | tf_op jit(solution)/shard_map/ppermute | solution.py:14
  87.7 0.0 collective-permute-done.5
  87.8 2.0 %collective-permute-done.4 = f32[64,448]{1,0:T(8,128)S(1)} collective-permute-done((f32[64,448]{1,0:T(8,128)S(1)}, f32[64,448]{1,0:T(8,128)S(1)}, u32[]{:S(2)}, u32[]{:S(2)}) %collective-permute-start.4) | collective-permute-done | bytes 114720 | tf_op jit(solution)/shard_map/ppermute | solution.py:14
  89.7 7.7 %collective-permute-done.3 = f32[64,448]{1,0:T(8,128)S(1)} collective-permute-done((f32[64,448]{1,0:T(8,128)S(1)}, f32[64,448]{1,0:T(8,128)S(1)}, u32[]{:S(2)}, u32[]{:S(2)}) %collective-permute-start.3) | collective-permute-done | bytes 114720 | tf_op jit(solution)/shard_map/ppermute | solution.py:14
  97.4 0.0 collective-permute-done.2
  97.4 0.8 add_bitcast_fusion
  (10 shorter events, 0.1 us)
Async XLA Ops:
  3.4 36.3 %collective-permute-start.1 = (f32[12,64,320]{2,1,0:T(8,128)}, f32[12,64,320]{2,1,0:T(8,128)}, u32[]{:S(2)}, u32[]{:S(2)}) collective-permute-start(f32[12,64,320]{2,1,0:T(8,128)} %broadcast_multiply_fusion), channel_id=1, source_target_pairs={{1,0},{2,1},{3,2},{4,3},{5,4},{6,5},{7,6},{8,7},{9,8},{10,9},{11,1... | collective-permute-start | bytes 2949128 | tf_op jit(solution)/shard_map/ppermute | solution.py:14
  16.6 29.0 %collective-permute-start = (f32[12,64,320]{2,1,0:T(8,128)}, f32[12,64,320]{2,1,0:T(8,128)}, u32[]{:S(2)}, u32[]{:S(2)}) collective-permute-start(f32[12,64,320]{2,1,0:T(8,128)} %broadcast_multiply_fusion), channel_id=1, source_target_pairs={{0,1},{1,2},{2,3},{3,4},{4,5},{5,6},{6,7},{7,8},{8,9},{9,10},{10,1... | collective-permute-start | bytes 2949128 | tf_op jit(solution)/shard_map/ppermute | solution.py:14
  20.4 1.6 %copy-start.2 = (s32[12]{0:T(128)S(1)}, s32[12]{0:T(128)}, u32[]{:S(2)}) copy-start(s32[12]{0:T(128)} %param.7) | copy-start | bytes 148
  20.4 1.7 %copy-start.1 = (s32[12,14]{1,0:T(8,128)S(1)}, s32[12,14]{1,0:T(8,128)}, u32[]{:S(2)}) copy-start(s32[12,14]{1,0:T(8,128)} %param.6) | copy-start | bytes 2020
  32.2 3.6 %copy-start = (f32[12,64,320]{2,1,0:T(8,128)S(1)}, f32[12,64,320]{2,1,0:T(8,128)}, u32[]{:S(2)}) copy-start(f32[12,64,320]{2,1,0:T(8,128)} %param.8) | copy-start | bytes 2949124
  50.6 37.1 %collective-permute-start.5 = (f32[64,448]{1,0:T(8,128)S(1)}, f32[64,448]{1,0:T(8,128)S(1)}, u32[]{:S(2)}, u32[]{:S(2)}) collective-permute-start(f32[64,448]{1,0:T(8,128)S(1)} %get-tuple-element.9), channel_id=1, source_target_pairs={{2,0},{3,1},{4,2},{5,3},{6,4},{7,5},{8,6},{9,7},{10,8},{11,9},{12,... | collective-permute-start | bytes 344072 | tf_op jit(solution)/shard_map/ppermute | solution.py:14
  79.1 10.6 %collective-permute-start.4 = (f32[64,448]{1,0:T(8,128)S(1)}, f32[64,448]{1,0:T(8,128)S(1)}, u32[]{:S(2)}, u32[]{:S(2)}) collective-permute-start(f32[64,448]{1,0:T(8,128)S(1)} %get-tuple-element.10), channel_id=1, source_target_pairs={{1,0},{2,1},{3,2},{4,3},{5,4},{6,5},{7,6},{8,7},{9,8},{10,9},{11,1... | collective-permute-start | bytes 344072 | tf_op jit(solution)/shard_map/ppermute | solution.py:14
  81.0 16.4 %collective-permute-start.3 = (f32[64,448]{1,0:T(8,128)S(1)}, f32[64,448]{1,0:T(8,128)S(1)}, u32[]{:S(2)}, u32[]{:S(2)}) collective-permute-start(f32[64,448]{1,0:T(8,128)S(1)} %get-tuple-element.11), channel_id=1, source_target_pairs={{0,2},{1,3},{2,4},{3,5},{4,6},{5,7},{6,8},{7,9},{8,10},{9,11},{10,... | collective-permute-start | bytes 344072 | tf_op jit(solution)/shard_map/ppermute | solution.py:14
  85.8 11.6 %collective-permute-start.2 = (f32[64,448]{1,0:T(8,128)S(1)}, f32[64,448]{1,0:T(8,128)S(1)}, u32[]{:S(2)}, u32[]{:S(2)}) collective-permute-start(f32[64,448]{1,0:T(8,128)S(1)} %get-tuple-element.12), channel_id=1, source_target_pairs={{0,1},{1,2},{2,3},{3,4},{4,5},{5,6},{6,7},{7,8},{8,9},{9,10},{10,1... | collective-permute-start | bytes 344072 | tf_op jit(solution)/shard_map/ppermute | solution.py:14

commit v4 on v3

--- a/solution.py
+++ b/solution.py
@@ -64,16 +64,23 @@
     prol_slots = p_mask.shape[1]
     group_total = lax.axis_size("rows") * lax.axis_size("cols")
     position = lax.axis_index("rows") * lax.axis_size("cols") + lax.axis_index("cols")
+    flat_axis = ("rows", "cols")
+    lower_raw = from_behind(p_vals, flat_axis, 1)
+    upper_raw = from_behind(p_vals, flat_axis, -1)
+    lower_mask = from_behind(p_mask, flat_axis, 1)
+    upper_mask = from_behind(p_mask, flat_axis, -1)
     slot_ids = jnp.arange(prol_slots, dtype=jnp.int32)
-    target = position + slot_ids - 2
-    inside = ((target >= 0) & (target < group_total)).astype(jnp.float32)
-    keep_mask = p_mask.astype(jnp.float32) * inside[None, :]
-    pblocks = (
-        p_vals.reshape(rows_here, block_size, prol_slots, block_size) * keep_mask[:, None, :, None]
-    )
-    pflat = pblocks.reshape(rows_here, block_size, prol_slots * block_size)
-    lower_rows = from_behind(pflat, ("rows", "cols"), 1)
-    upper_rows = from_behind(pflat, ("rows", "cols"), -1)
+    span = rows_here * block_size
+    width = prol_slots * block_size
+
+    def masked(values, mask, owner):
+        target = owner + slot_ids - 2
+        inside = ((target >= 0) & (target < group_total)).astype(jnp.float32)
+        keep = mask.astype(jnp.float32) * inside[None, :]
+        blocks = values.reshape(rows_here, block_size, prol_slots, block_size) * keep[:, None, :, None]
+        return blocks.reshape(span, width)
+
+    p_own = masked(p_vals, p_mask, position)
 
     local_cols = a_cols - (position - 1) * rows_here
     live_mask = jnp.arange(slot_count, dtype=jnp.int32)[None, :] < a_count[:, None]
@@ -81,33 +88,34 @@
     hit = live_mask[:, :, None] & (local_cols[:, :, None] == col_ids[None, None, :])
     slot_numbers = jnp.arange(1, slot_count + 1, dtype=jnp.int32)[None, :, None]
     slot_table = (jnp.sum(jnp.where(hit, slot_numbers, 0), axis=1) - 1).reshape(-1)
-    span = rows_here * block_size
-    width = prol_slots * block_size
     dense = dense_sides(slot_table, a_vals).reshape(3, span, span)
-    own = mm(dense[1], pflat.reshape(span, width))
-    low = mm(dense[0], lower_rows.reshape(span, width))
-    high = mm(dense[2], upper_rows.reshape(span, width))
-    ap_rows = (
-        jnp.pad(low, ((0, 0), (0, 2 * block_size)))
-        + jnp.pad(own, ((0, 0), (block_size, block_size)))
-        + jnp.pad(high, ((0, 0), (2 * block_size, 0)))
-    )
-    terms = lax.dot_general(
-        pflat.reshape(span, width),
-        ap_rows,
-        (((0,), (0,)), ((), ())),
-        precision=MATMUL_PRECISION,
-        preferred_element_type=jnp.float32,
+
+    def pt_times(side):
+        return lax.dot_general(
+            p_own,
+            dense[side],
+            (((0,), (0,)), ((), ())),
+            precision=MATMUL_PRECISION,
+            preferred_element_type=jnp.float32,
+        )
+
+    t_own = mm(pt_times(1), p_own)
+    t_low = mm(pt_times(0), masked(lower_raw, lower_mask, position - 1))
+    t_high = mm(pt_times(2), masked(upper_raw, upper_mask, position + 1))
+    terms = (
+        jnp.pad(t_low, ((0, 0), (0, 2 * block_size)))
+        + jnp.pad(t_own, ((0, 0), (block_size, block_size)))
+        + jnp.pad(t_high, ((0, 0), (2 * block_size, 0)))
     ).reshape(prol_slots, block_size, (prol_slots + 2) * block_size)
 
     def spread(s, block):
         return jnp.pad(block, ((0, 0), ((prol_slots - 1 - s) * block_size, s * block_size)))
 
     result = spread(2, terms[2])
-    result = result + spread(3, from_behind(terms[3], ("rows", "cols"), 1))
-    result = result + spread(4, from_behind(terms[4], ("rows", "cols"), 2))
-    result = result + spread(1, from_behind(terms[1], ("rows", "cols"), -1))
-    result = result + spread(0, from_behind(terms[0], ("rows", "cols"), -2))
+    result = result + spread(3, from_behind(terms[3], flat_axis, 1))
+    result = result + spread(4, from_behind(terms[4], flat_axis, 2))
+    result = result + spread(1, from_behind(terms[1], flat_axis, -1))
+    result = result + spread(0, from_behind(terms[0], flat_axis, -2))
     return result.reshape(1, block_size, (prol_slots + 6) * block_size)
 
 

time: 98.7 us -> 101 us (1.023)
  local copies, waits for them, and re-layouts: 8 us -> 23.4 us
  starting transfers between devices: 52.2 us -> 40.9 us
  waiting for transfers between devices: 13.5 us -> 3.58 us
  other arithmetic: 4.37 us -> 10.1 us
  matrix products: 10.8 us -> 13.3 us
    mul x6 -> x12, local copies, waits for them, and re-layouts: 3.64 us -> 16 us  [the longest x11 15.9 us: masked(): values.reshape(rows_here, block_size, prol_slots, block_size)]
    ppermute x6 -> x8, starting transfers between devices: 52.2 us -> 40.9 us  [from_behind(): return lax.ppermute(array, axis, pairs)]
    ppermute x6 -> x8, waiting for transfers between devices: 13.5 us -> 3.58 us  [from_behind(): return lax.ppermute(array, axis, pairs)]
    dot_general x1 -> x3, matrix products: 2.04 us -> 7.95 us  [pt_times(): lax.dot_general(p_own, dense[side], (((0,), (0,)), ((), ())), precision=M...]
    mul x3 -> x7, other arithmetic: 3.3 us -> 7.47 us  [the longest x4 7.25 us: masked(): values.reshape(rows_here, block_size, prol_slots, block_size)]
    dot_general x3, matrix products: 8.73 us -> 5.31 us  [mm(): jnp.dot(a, b, precision=MATMUL_PRECISION, preferred_element_type=jnp.floa...]
    slice x1, local copies, waits for them, and re-layouts: 3.64 us -> 5.99 us  [pt_times(): dense[side]]
  transfers between devices with their start and end apart: 6 -> 8, of which waited for: 4 -> 1; matrix products, arithmetic and copies ran while one was open for 14% -> 42% of each run, Pallas kernels for 9% -> 9%
where the time goes in v4:
time: 101 us
  starting transfers between devices  40.9 us (40%)
  local copies, waits for them, and re-layouts  23.4 us (23%)
  matrix products  13.3 us (13%)
  other arithmetic  10.1 us (10%)
  Pallas kernels  9.25 us (9%)
  waiting for transfers between devices  3.58 us (4%)
    ppermute x8, starting transfers between devices, from_behind(): return lax.ppermute(array, axis, pairs)  40.9 us
    mul x11, local copies, waits for them, and re-layouts, masked(): values.reshape(rows_here, block_size, prol_slots, block_size)  15.9 us
    pallas_call x1, Pallas kernels, dense_sides(): pl.pallas_call(dense_kernel, out_shape=jax.ShapeDtypeStruct((3, rows_here...  9.25 us
    dot_general x3, matrix products, pt_times(): lax.dot_general(p_own, dense[side], (((0,), (0,)), ((), ())), precision=M...  7.95 us
    mul x4, other arithmetic, masked(): values.reshape(rows_here, block_size, prol_slots, block_size)  7.25 us
    slice x1, local copies, waits for them, and re-layouts, pt_times(): dense[side]  5.99 us
    dot_general x3, matrix products, mm(): jnp.dot(a, b, precision=MATMUL_PRECISION, preferred_element_type=jnp.floa...  5.31 us
    ppermute x8, waiting for transfers between devices, from_behind(): return lax.ppermute(array, axis, pairs)  3.58 us
  transfers between devices with their start and end apart: 8, of which 1 were waited for; matrix products, arithmetic and copies ran while one was open for 42% of the time, Pallas kernels for 9%

profile of v4, /device:TPU:24, one launch (start us, length us, event | category | flops | bytes accessed | tf_op | source)
XLA Modules:
  0.0 100.7 jit_solution(16529840436190610626)
XLA Ops:
  0.0 3.8 %collective-permute-start.1 = (s32[12,5]{0,1:T(8,128)}, s32[12,5]{0,1:T(8,128)S(1)}, u32[]{:S(2)}, u32[]{:S(2)}) collective-permute-start(s32[12,5]{0,1:T(8,128)} %param.9), channel_id=1, source_target_pairs={{0,1},{1,2},{2,3},{3,4},{4,5},{5,6},{6,7},{7,8},{8,9},{9,10},{10,1... | collective-permute-start | bytes 728 | tf_op jit(solution)/shard_map/ppermute | solution.py:14
  3.8 11.3 %collective-permute-start.3 = (s32[12,5]{0,1:T(8,128)}, s32[12,5]{0,1:T(8,128)S(1)}, u32[]{:S(2)}, u32[]{:S(2)}) collective-permute-start(s32[12,5]{0,1:T(8,128)} %param.9), channel_id=1, source_target_pairs={{1,0},{2,1},{3,2},{4,3},{5,4},{6,5},{7,6},{8,7},{9,8},{10,9},{11,1... | collective-permute-start | bytes 728 | tf_op jit(solution)/shard_map/ppermute | solution.py:14
  15.1 1.9 %collective-permute-start = (f32[12,64,320]{2,1,0:T(8,128)}, f32[12,64,320]{2,1,0:T(8,128)}, u32[]{:S(2)}, u32[]{:S(2)}) collective-permute-start(f32[12,64,320]{2,1,0:T(8,128)} %param.8), channel_id=1, source_target_pairs={{0,1},{1,2},{2,3},{3,4},{4,5},{5,6},{6,7},{7,8},{8,9},{9,10},{10,1... | collective-permute-start | bytes 2949128 | tf_op jit(solution)/shard_map/ppermute | solution.py:14
  17.1 7.9 %collective-permute-start.2 = (f32[12,64,320]{2,1,0:T(8,128)}, f32[12,64,320]{2,1,0:T(8,128)}, u32[]{:S(2)}, u32[]{:S(2)}) collective-permute-start(f32[12,64,320]{2,1,0:T(8,128)} %param.8), channel_id=1, source_target_pairs={{1,0},{2,1},{3,2},{4,3},{5,4},{6,5},{7,6},{8,7},{9,8},{10,9},{11,1... | collective-permute-start | bytes 2949128 | tf_op jit(solution)/shard_map/ppermute | solution.py:14
  25.0 0.7 iota_compare_fusion.1
  25.7 0.7 broadcast_subtract_fusion
  27.2 9.2 %shard_map.55 = f32[3,12,64,768]{3,2,1,0:T(8,128)} custom-call(s32[432]{0:T(512)} %sub.30.slot_ref, f32[12,64,896]{2,1,0:T(8,128)} %a_ref.1), custom_call_target="tpu_custom_call" | custom-call | tf_op jit(solution)/shard_map/pallas_call | solution.py:49
  36.5 6.0 %fusion.1 = (f32[1,12,64,768]{3,2,1,0:T(8,128)}, f32[1,12,64,768]{3,2,1,0:T(8,128)S(1)}, f32[1,12,64,768]{3,2,1,0:T(8,128)}) fusion(f32[3,12,64,768]{3,2,1,0:T(8,128)} %shard_map.55), kind=kLoop, calls=%fused_computation.19 | loop fusion | bytes 14155776 | tf_op jit(solution)/shard_map/slice | solution.py:96
  42.7 0.7 mul.80
  43.4 1.5 %broadcast_multiply_fusion = f32[12,64,320]{2,1,0:T(8,128)S(1)} fusion(f32[12,64,320]{2,1,0:T(8,128)} %param.8, f32[12,320]{1,0:T(8,128)} %mul.80), kind=kLoop, calls=%fused_computation.4 | loop fusion | flops 245760 | bytes 1981440 | tf_op jit(solution)/shard_map/mul | solution.py:80
  45.5 2.7 %fusion.3 = f32[320,768]{1,0:T(8,128)} fusion(f32[768,320]{1,0:T(8,128)S(1)} %bitcast.30, f32[768,768]{1,0:T(8,128)S(1)} %bitcast.35), kind=kOutput, calls=%fused_computation.21 | convolution fusion | flops 1132462080 | bytes 4325376 | tf_op jit(solution)/shard_map/dot_general | solution.py:94
  48.1 2.7 %fusion.5 = f32[320,768]{1,0:T(8,128)} fusion(f32[768,320]{1,0:T(8,128)S(1)} %bitcast.31, f32[768,768]{1,0:T(8,128)S(1)} %bitcast.34), kind=kOutput, calls=%fused_computation.23 | convolution fusion | flops 1132462080 | bytes 4325376 | tf_op jit(solution)/shard_map/dot_general | solution.py:94
  50.8 1.7 %mul.90 = f32[12,64,5,64]{1,0,3,2:T(8,128)} broadcast(f32[12,5]{0,1:T(8,128)S(1)} %convert_multiply_fusion.2), dimensions={0,2} | broadcast | bytes 983280 | tf_op jit(solution)/shard_map/mul | solution.py:80
  52.6 2.9 %mul.91 = f32[768,320]{0,1:T(8,128)} reshape(f32[12,64,5,64]{1,0,3,2:T(8,128)} %mul.90) | data formatting | bytes 1966080 | tf_op jit(solution)/shard_map/mul | solution.py:80
  55.5 2.6 %copy.20 = f32[768,320]{1,0:T(8,128)} copy(f32[768,320]{0,1:T(8,128)} %mul.91) | data formatting | bytes 1966080 | tf_op jit(solution)/shard_map/mul | solution.py:80
  58.1 2.8 %bitcast_multiply_fusion.1 = f32[768,320]{1,0:T(8,128)} fusion(f32[768,320]{1,0:T(8,128)} %copy.20, f32[12,64,320]{2,1,0:T(8,128)} %param.8), kind=kLoop, calls=%fused_computation.1 | loop fusion | flops 245760 | bytes 2949120 | tf_op jit(solution)/shard_map/mul | solution.py:80
  60.9 3.3 %fusion.6 = f32[320,320]{1,0:T(8,128)} fusion(f32[320,768]{1,0:T(8,128)} %fusion.5, f32[768,320]{1,0:T(8,128)} %bitcast_multiply_fusion.1), kind=kOutput, calls=%fused_computation.24 | convolution fusion | flops 471859200 | bytes 2375680 | tf_op jit(solution)/shard_map/dot_general | solution.py:18
  64.2 2.6 %fusion.7 = f32[320,768]{1,0:T(8,128)} fusion(f32[768,320]{1,0:T(8,128)S(1)} %bitcast.32, f32[768,768]{1,0:T(8,128)S(1)} %bitcast.33), kind=kOutput, calls=%fused_computation.25 | convolution fusion | flops 1132462080 | bytes 4325376 | tf_op jit(solution)/shard_map/dot_general | solution.py:94
  67.1 1.6 %mul.88 = f32[768,320]{0,1:T(8,128)} reshape(f32[12,64,5,64]{1,0,3,2:T(8,128)S(1)} %mul.87) | data formatting | bytes 1966080 | tf_op jit(solution)/shard_map/mul | solution.py:80
  68.7 2.6 %copy.19 = f32[768,320]{1,0:T(8,128)} copy(f32[768,320]{0,1:T(8,128)} %mul.88) | data formatting | bytes 1966080 | tf_op jit(solution)/shard_map/mul | solution.py:80
  71.6 1.6 %mul.96 = f32[768,320]{0,1:T(8,128)} reshape(f32[12,64,5,64]{1,0,3,2:T(8,128)S(1)} %mul.95) | data formatting | bytes 1966080 | tf_op jit(solution)/shard_map/mul | solution.py:80
  73.2 1.7 %copy.21 = f32[768,320]{1,0:T(8,128)S(1)} copy(f32[768,320]{0,1:T(8,128)} %mul.96) | data formatting | bytes 1966080 | tf_op jit(solution)/shard_map/mul | solution.py:80
  74.9 1.5 %bitcast_multiply_fusion.2 = f32[768,320]{1,0:T(8,128)S(1)} fusion(f32[768,320]{1,0:T(8,128)S(1)} %copy-done.2, f32[12,64,320]{2,1,0:T(8,128)} %collective-permute-done), kind=kLoop, calls=%fused_computation.2 | loop fusion | flops 245760 | bytes 2949120 | tf_op jit(solution)/shard_map/mul | solution.py:80
  76.4 1.0 fusion.4
  77.4 1.5 %bitcast_multiply_fusion = f32[768,320]{1,0:T(8,128)S(1)} fusion(f32[768,320]{1,0:T(8,128)S(1)} %copy.21, f32[12,64,320]{2,1,0:T(8,128)} %collective-permute-done.2), kind=kLoop, calls=%fused_computation | loop fusion | flops 245760 | bytes 2949120 | tf_op jit(solution)/shard_map/mul | solution.py:80
  79.0 1.0 fusion.8
  80.3 1.9 %collective-permute-start.4 = (f32[64,448]{1,0:T(8,128)S(1)}, f32[64,448]{1,0:T(8,128)S(1)}, u32[]{:S(2)}, u32[]{:S(2)}) collective-permute-start(f32[64,448]{1,0:T(8,128)S(1)} %get-tuple-element.12), channel_id=1, source_target_pairs={{0,1},{1,2},{2,3},{3,4},{4,5},{5,6},{6,7},{7,8},{8,9},{9,10},{10,1... | collective-permute-start | bytes 344072 | tf_op jit(solution)/shard_map/ppermute | solution.py:14
  82.2 1.9 %collective-permute-start.5 = (f32[64,448]{1,0:T(8,128)S(1)}, f32[64,448]{1,0:T(8,128)S(1)}, u32[]{:S(2)}, u32[]{:S(2)}) collective-permute-start(f32[64,448]{1,0:T(8,128)S(1)} %get-tuple-element.11), channel_id=1, source_target_pairs={{0,2},{1,3},{2,4},{3,5},{4,6},{5,7},{6,8},{7,9},{8,10},{9,11},{10,... | collective-permute-start | bytes 344072 | tf_op jit(solution)/shard_map/ppermute | solution.py:14
  84.2 7.9 %collective-permute-start.6 = (f32[64,448]{1,0:T(8,128)S(1)}, f32[64,448]{1,0:T(8,128)S(1)}, u32[]{:S(2)}, u32[]{:S(2)}) collective-permute-start(f32[64,448]{1,0:T(8,128)S(1)} %get-tuple-element.10), channel_id=1, source_target_pairs={{1,0},{2,1},{3,2},{4,3},{5,4},{6,5},{7,6},{8,7},{9,8},{10,9},{11,1... | collective-permute-start | bytes 344072 | tf_op jit(solution)/shard_map/ppermute | solution.py:14
  92.0 4.3 %collective-permute-start.7 = (f32[64,448]{1,0:T(8,128)S(1)}, f32[64,448]{1,0:T(8,128)S(1)}, u32[]{:S(2)}, u32[]{:S(2)}) collective-permute-start(f32[64,448]{1,0:T(8,128)S(1)} %get-tuple-element.9), channel_id=1, source_target_pairs={{2,0},{3,1},{4,2},{5,3},{6,4},{7,5},{8,6},{9,7},{10,8},{11,9},{12,... | collective-permute-start | bytes 344072 | tf_op jit(solution)/shard_map/ppermute | solution.py:14
  96.3 3.6 %collective-permute-done.7 = f32[64,448]{1,0:T(8,128)S(1)} collective-permute-done((f32[64,448]{1,0:T(8,128)S(1)}, f32[64,448]{1,0:T(8,128)S(1)}, u32[]{:S(2)}, u32[]{:S(2)}) %collective-permute-start.7) | collective-permute-done | bytes 114720 | tf_op jit(solution)/shard_map/ppermute | solution.py:14
  99.9 0.8 add_bitcast_fusion
  (37 shorter events, 2.7 us)
Async XLA Ops:
  0.0 66.8 %collective-permute-start.1 = (s32[12,5]{0,1:T(8,128)}, s32[12,5]{0,1:T(8,128)S(1)}, u32[]{:S(2)}, u32[]{:S(2)}) collective-permute-start(s32[12,5]{0,1:T(8,128)} %param.9), channel_id=1, source_target_pairs={{0,1},{1,2},{2,3},{3,4},{4,5},{5,6},{6,7},{7,8},{8,9},{9,10},{10,1... | collective-permute-start | bytes 728 | tf_op jit(solution)/shard_map/ppermute | solution.py:14
  3.8 67.5 %collective-permute-start.3 = (s32[12,5]{0,1:T(8,128)}, s32[12,5]{0,1:T(8,128)S(1)}, u32[]{:S(2)}, u32[]{:S(2)}) collective-permute-start(s32[12,5]{0,1:T(8,128)} %param.9), channel_id=1, source_target_pairs={{1,0},{2,1},{3,2},{4,3},{5,4},{6,5},{7,6},{8,7},{9,8},{10,9},{11,1... | collective-permute-start | bytes 728 | tf_op jit(solution)/shard_map/ppermute | solution.py:14
  15.1 59.7 %collective-permute-start = (f32[12,64,320]{2,1,0:T(8,128)}, f32[12,64,320]{2,1,0:T(8,128)}, u32[]{:S(2)}, u32[]{:S(2)}) collective-permute-start(f32[12,64,320]{2,1,0:T(8,128)} %param.8), channel_id=1, source_target_pairs={{0,1},{1,2},{2,3},{3,4},{4,5},{5,6},{6,7},{7,8},{8,9},{9,10},{10,1... | collective-permute-start | bytes 2949128 | tf_op jit(solution)/shard_map/ppermute | solution.py:14
  17.1 60.3 %collective-permute-start.2 = (f32[12,64,320]{2,1,0:T(8,128)}, f32[12,64,320]{2,1,0:T(8,128)}, u32[]{:S(2)}, u32[]{:S(2)}) collective-permute-start(f32[12,64,320]{2,1,0:T(8,128)} %param.8), channel_id=1, source_target_pairs={{1,0},{2,1},{3,2},{4,3},{5,4},{6,5},{7,6},{8,7},{9,8},{10,9},{11,1... | collective-permute-start | bytes 2949128 | tf_op jit(solution)/shard_map/ppermute | solution.py:14
  36.5 6.0 %copy-start.6 = (s32[12,5]{0,1:T(8,128)S(1)}, s32[12,5]{0,1:T(8,128)}, u32[]{:S(2)}) copy-start(s32[12,5]{0,1:T(8,128)} %param.9) | copy-start | bytes 724
  43.4 2.0 %copy-start.1 = (f32[1,12,64,768]{3,2,1,0:T(8,128)S(1)}, f32[1,12,64,768]{3,2,1,0:T(8,128)}, u32[]{:S(2)}) copy-start(f32[1,12,64,768]{3,2,1,0:T(8,128)} %get-tuple-element.5) | copy-start | bytes 7077892
  45.5 2.7 %copy-start = (f32[1,12,64,768]{3,2,1,0:T(8,128)S(1)}, f32[1,12,64,768]{3,2,1,0:T(8,128)}, u32[]{:S(2)}) copy-start(f32[1,12,64,768]{3,2,1,0:T(8,128)} %get-tuple-element.7) | copy-start | bytes 7077892
  73.2 1.7 %copy-start.2 = (f32[768,320]{1,0:T(8,128)S(1)}, f32[768,320]{1,0:T(8,128)}, u32[]{:S(2)}) copy-start(f32[768,320]{1,0:T(8,128)} %copy.19) | copy-start | bytes 2949124
  74.8 1.6 %copy-start.3 = (f32[320,768]{1,0:T(8,128)S(1)}, f32[320,768]{1,0:T(8,128)}, u32[]{:S(2)}) copy-start(f32[320,768]{1,0:T(8,128)} %fusion.3) | copy-start | bytes 2949124
  77.4 1.6 %copy-start.4 = (f32[320,768]{1,0:T(8,128)S(1)}, f32[320,768]{1,0:T(8,128)}, u32[]{:S(2)}) copy-start(f32[320,768]{1,0:T(8,128)} %fusion.7) | copy-start | bytes 2949124
  79.0 1.0 %copy-start.5 = (f32[320,320]{1,0:T(8,128)S(1)}, f32[320,320]{1,0:T(8,128)}, u32[]{:S(2)}) copy-start(f32[320,320]{1,0:T(8,128)} %fusion.6) | copy-start | bytes 1228804
  80.3 16.0 %collective-permute-start.4 = (f32[64,448]{1,0:T(8,128)S(1)}, f32[64,448]{1,0:T(8,128)S(1)}, u32[]{:S(2)}, u32[]{:S(2)}) collective-permute-start(f32[64,448]{1,0:T(8,128)S(1)} %get-tuple-element.12), channel_id=1, source_target_pairs={{0,1},{1,2},{2,3},{3,4},{4,5},{5,6},{6,7},{7,8},{8,9},{9,10},{10,1... | collective-permute-start | bytes 344072 | tf_op jit(solution)/shard_map/ppermute | solution.py:14
  82.2 14.1 %collective-permute-start.5 = (f32[64,448]{1,0:T(8,128)S(1)}, f32[64,448]{1,0:T(8,128)S(1)}, u32[]{:S(2)}, u32[]{:S(2)}) collective-permute-start(f32[64,448]{1,0:T(8,128)S(1)} %get-tuple-element.11), channel_id=1, source_target_pairs={{0,2},{1,3},{2,4},{3,5},{4,6},{5,7},{6,8},{7,9},{8,10},{9,11},{10,... | collective-permute-start | bytes 344072 | tf_op jit(solution)/shard_map/ppermute | solution.py:14
  84.2 12.2 %collective-permute-start.6 = (f32[64,448]{1,0:T(8,128)S(1)}, f32[64,448]{1,0:T(8,128)S(1)}, u32[]{:S(2)}, u32[]{:S(2)}) collective-permute-start(f32[64,448]{1,0:T(8,128)S(1)} %get-tuple-element.10), channel_id=1, source_target_pairs={{1,0},{2,1},{3,2},{4,3},{5,4},{6,5},{7,6},{8,7},{9,8},{10,9},{11,1... | collective-permute-start | bytes 344072 | tf_op jit(solution)/shard_map/ppermute | solution.py:14
  92.0 7.9 %collective-permute-start.7 = (f32[64,448]{1,0:T(8,128)S(1)}, f32[64,448]{1,0:T(8,128)S(1)}, u32[]{:S(2)}, u32[]{:S(2)}) collective-permute-start(f32[64,448]{1,0:T(8,128)S(1)} %get-tuple-element.9), channel_id=1, source_target_pairs={{2,0},{3,1},{4,2},{5,3},{6,4},{7,5},{8,6},{9,7},{10,8},{11,9},{12,... | collective-permute-start | bytes 344072 | tf_op jit(solution)/shard_map/ppermute | solution.py:14

commit v5 on v4

--- a/solution.py
+++ b/solution.py
@@ -18,8 +18,9 @@
     return jnp.dot(a, b, precision=MATMUL_PRECISION, preferred_element_type=jnp.float32)
 
 
-def dense_kernel(slot_ref, a_ref, out_ref):
-    sides, rows_here, block_size, span = out_ref.shape
+def dense_kernel(slot_ref, a_ref, *out_refs):
+    sides = len(out_refs)
+    rows_here, block_size, span = out_refs[0].shape
     per_side = span // block_size
     lanes = 2 * block_size
     left = lax.broadcasted_iota(jnp.int32, (block_size, lanes), 1) < block_size
@@ -37,7 +38,7 @@
                     turn = (safe % 2) != h
                     picked = jnp.where(turn, rolled, tile)
                     halves.append(jnp.where(slot >= 0, picked, jnp.zeros_like(picked)))
-                out_ref[d, i, :, m * lanes : (m + 1) * lanes] = jnp.where(left, halves[0], halves[1])
+                out_refs[d][i, :, m * lanes : (m + 1) * lanes] = jnp.where(left, halves[0], halves[1])
         return carry
 
     lax.fori_loop(0, rows_here, one_row, 0)
@@ -48,12 +49,12 @@
     span = rows_here * block_size
     return pl.pallas_call(
         dense_kernel,
-        out_shape=jax.ShapeDtypeStruct((3, rows_here, block_size, span), jnp.float32),
+        out_shape=[jax.ShapeDtypeStruct((rows_here, block_size, span), jnp.float32)] * 3,
         in_specs=[
             pl.BlockSpec(memory_space=pltpu.SMEM),
             pl.BlockSpec(memory_space=pltpu.VMEM),
         ],
-        out_specs=pl.BlockSpec(memory_space=pltpu.VMEM),
+        out_specs=[pl.BlockSpec(memory_space=pltpu.VMEM)] * 3,
     )(slot_table, a_vals)
 
 
@@ -65,22 +66,16 @@
     group_total = lax.axis_size("rows") * lax.axis_size("cols")
     position = lax.axis_index("rows") * lax.axis_size("cols") + lax.axis_index("cols")
     flat_axis = ("rows", "cols")
-    lower_raw = from_behind(p_vals, flat_axis, 1)
-    upper_raw = from_behind(p_vals, flat_axis, -1)
-    lower_mask = from_behind(p_mask, flat_axis, 1)
-    upper_mask = from_behind(p_mask, flat_axis, -1)
     slot_ids = jnp.arange(prol_slots, dtype=jnp.int32)
+    target = position + slot_ids - 2
+    inside = ((target >= 0) & (target < group_total)).astype(jnp.float32)
+    keep = jnp.repeat(p_mask.astype(jnp.float32) * inside[None, :], block_size, axis=1)
+    pflat = p_vals * keep[:, None, :]
+    lower_rows = from_behind(pflat, flat_axis, 1)
+    upper_rows = from_behind(pflat, flat_axis, -1)
     span = rows_here * block_size
     width = prol_slots * block_size
-
-    def masked(values, mask, owner):
-        target = owner + slot_ids - 2
-        inside = ((target >= 0) & (target < group_total)).astype(jnp.float32)
-        keep = mask.astype(jnp.float32) * inside[None, :]
-        blocks = values.reshape(rows_here, block_size, prol_slots, block_size) * keep[:, None, :, None]
-        return blocks.reshape(span, width)
-
-    p_own = masked(p_vals, p_mask, position)
+    p_own = pflat.reshape(span, width)
 
     local_cols = a_cols - (position - 1) * rows_here
     live_mask = jnp.arange(slot_count, dtype=jnp.int32)[None, :] < a_count[:, None]
@@ -88,7 +83,7 @@
     hit = live_mask[:, :, None] & (local_cols[:, :, None] == col_ids[None, None, :])
     slot_numbers = jnp.arange(1, slot_count + 1, dtype=jnp.int32)[None, :, None]
     slot_table = (jnp.sum(jnp.where(hit, slot_numbers, 0), axis=1) - 1).reshape(-1)
-    dense = dense_sides(slot_table, a_vals).reshape(3, span, span)
+    dense = [side.reshape(span, span) for side in dense_sides(slot_table, a_vals)]
 
     def pt_times(side):
         return lax.dot_general(
@@ -100,8 +95,8 @@
         )
 
     t_own = mm(pt_times(1), p_own)
-    t_low = mm(pt_times(0), masked(lower_raw, lower_mask, position - 1))
-    t_high = mm(pt_times(2), masked(upper_raw, upper_mask, position + 1))
+    t_low = mm(pt_times(0), lower_rows.reshape(span, width))
+    t_high = mm(pt_times(2), upper_rows.reshape(span, width))
     terms = (
         jnp.pad(t_low, ((0, 0), (0, 2 * block_size)))
         + jnp.pad(t_own, ((0, 0), (block_size, block_size)))

time: 101 us -> 87.9 us (0.87)
  the two profiles are of different devices: /device:TPU:24 before, /device:TPU:1 now
where the time goes in v5:
time: 87.9 us; the launch traced here: 87.5 us
  waiting for transfers between devices  35 us (40%)
  starting transfers between devices  27.2 us (31%)
  matrix products  9.64 us (11%)
  Pallas kernels  9.14 us (10%)
  other arithmetic  4.63 us (5%)
  local copies, waits for them, and re-layouts  1.66 us (2%)
    ppermute x6, waiting for transfers between devices, from_behind(): return lax.ppermute(array, axis, pairs)  35 us
    ppermute x6, starting transfers between devices, from_behind(): return lax.ppermute(array, axis, pairs)  27.2 us
    pallas_call x1, Pallas kernels, dense_sides(): pl.pallas_call(dense_kernel, out_shape=[jax.ShapeDtypeStruct((rows_here,...  9.14 us
    dot_general x3, matrix products, pt_times(): lax.dot_general(p_own, dense[side], (((0,), (0,)), ((), ())), precision=M...  6.73 us
    dot_general x3, matrix products, mm(): jnp.dot(a, b, precision=MATMUL_PRECISION, preferred_element_type=jnp.floa...  2.91 us
  transfers between devices with their start and end apart: 6, of which 4 were waited for; matrix products, arithmetic and copies ran while one was open for 12% of the time, Pallas kernels for 10%

profile of v5, /device:TPU:1, one launch (start us, length us, event | category | flops | bytes accessed | tf_op | source)
XLA Modules:
  0.0 87.5 jit_solution(11455617912297822966)
XLA Ops:
  0.0 0.8 convert_multiply_fusion
  0.8 0.1 copy.8
  0.9 0.1 broadcast_in_dim.10
  0.9 0.1 mul.27
  1.0 1.4 %broadcast_multiply_fusion = f32[12,64,320]{2,1,0:T(8,128)S(1)} fusion(f32[12,64,320]{2,1,0:T(8,128)} %param.8, f32[12,320]{1,0:T(8,128)S(1)} %mul.27), kind=kLoop, calls=%fused_computation.4 | loop fusion | flops 245760 | bytes 1981440 | tf_op jit(solution)/shard_map/mul | solution.py:73
  2.4 4.4 %collective-permute-start = (f32[12,64,320]{2,1,0:T(8,128)S(1)}, f32[12,64,320]{2,1,0:T(8,128)S(1)}, u32[]{:S(2)}, u32[]{:S(2)}) collective-permute-start(f32[12,64,320]{2,1,0:T(8,128)S(1)} %broadcast_multiply_fusion), channel_id=1, source_target_pairs={{0,1},{1,2},{2,3},{3,4},{4,5},{5,6},{6,7},{7,8},{8,9},{9,10},{10,1... | collective-permute-start | bytes 2949128 | tf_op jit(solution)/shard_map/ppermute | solution.py:14
  6.8 7.4 %collective-permute-start.1 = (f32[12,64,320]{2,1,0:T(8,128)S(1)}, f32[12,64,320]{2,1,0:T(8,128)S(1)}, u32[]{:S(2)}, u32[]{:S(2)}) collective-permute-start(f32[12,64,320]{2,1,0:T(8,128)S(1)} %broadcast_multiply_fusion), channel_id=1, source_target_pairs={{1,0},{2,1},{3,2},{4,3},{5,4},{6,5},{7,6},{8,7},{9,8},{10,9},{11,1... | collective-permute-start | bytes 2949128 | tf_op jit(solution)/shard_map/ppermute | solution.py:14
  14.2 0.5 iota_add_fusion
  14.7 0.1 iota_compare_fusion.1
  14.8 0.8 select_reduce_fusion
  15.6 0.7 sub.23.slot_ref
  16.3 9.1 %shard_map.55 = (f32[12,64,768]{2,1,0:T(8,128)}, f32[12,64,768]{2,1,0:T(8,128)}, f32[12,64,768]{2,1,0:T(8,128)}) custom-call(s32[432]{0:T(512)} %sub.23.slot_ref, f32[12,64,896]{2,1,0:T(8,128)} %a_ref.1), custom_call_target="tpu_custom_call" | custom-call | tf_op jit(solution)/shard_map/pallas_call | solution.py:50
  25.4 3.3 %convolution_bitcast_fusion.1 = f32[320,768]{1,0:T(8,128)S(1)} fusion(f32[12,64,320]{2,1,0:T(8,128)S(1)} %broadcast_multiply_fusion, f32[12,64,768]{2,1,0:T(8,128)} %get-tuple-element.9), kind=kOutput, calls=%fused_computation.1 | convolution fusion | flops 1132462080 | bytes 4325376 | tf_op jit(solution)/shard_map/dot_general | solution.py:89
  28.7 1.0 %fusion.3 = f32[320,320]{1,0:T(8,128)S(1)} fusion(f32[320,768]{1,0:T(8,128)S(1)} %convolution_bitcast_fusion.1, f32[768,320]{1,0:T(8,128)S(1)} %bitcast.23), kind=kOutput, calls=%fused_computation.17 | convolution fusion | flops 471859200 | bytes 2375680 | tf_op jit(solution)/shard_map/dot_general | solution.py:18
  29.7 0.7 copy-done.3
  30.4 1.7 %convolution_bitcast_fusion.2 = f32[320,768]{1,0:T(8,128)S(1)} fusion(f32[12,64,320]{2,1,0:T(8,128)S(1)} %broadcast_multiply_fusion, f32[12,64,768]{2,1,0:T(8,128)S(1)} %copy-done.3), kind=kOutput, calls=%fused_computation.2 | convolution fusion | flops 1132462080 | bytes 4325376 | tf_op jit(solution)/shard_map/dot_general | solution.py:89
  32.1 1.7 %convolution_bitcast_fusion = f32[320,768]{1,0:T(8,128)S(1)} fusion(f32[12,64,320]{2,1,0:T(8,128)S(1)} %broadcast_multiply_fusion, f32[12,64,768]{2,1,0:T(8,128)S(1)} %copy-done.2), kind=kOutput, calls=%fused_computation | convolution fusion | flops 1132462080 | bytes 4325376 | tf_op jit(solution)/shard_map/dot_general | solution.py:89
  33.9 3.6 %collective-permute-done = f32[12,64,320]{2,1,0:T(8,128)S(1)} collective-permute-done((f32[12,64,320]{2,1,0:T(8,128)S(1)}, f32[12,64,320]{2,1,0:T(8,128)S(1)}, u32[]{:S(2)}, u32[]{:S(2)}) %collective-permute-start) | collective-permute-done | bytes 983072 | tf_op jit(solution)/shard_map/ppermute | solution.py:14
  37.4 1.0 %fusion.2 = f32[320,320]{1,0:T(8,128)S(1)} fusion(f32[320,768]{1,0:T(8,128)S(1)} %convolution_bitcast_fusion.2, f32[768,320]{1,0:T(8,128)S(1)} %bitcast.25), kind=kOutput, calls=%fused_computation.16 | convolution fusion | flops 471859200 | bytes 2375680 | tf_op jit(solution)/shard_map/dot_general | solution.py:18
  38.4 22.8 %collective-permute-done.1 = f32[12,64,320]{2,1,0:T(8,128)S(1)} collective-permute-done((f32[12,64,320]{2,1,0:T(8,128)S(1)}, f32[12,64,320]{2,1,0:T(8,128)S(1)}, u32[]{:S(2)}, u32[]{:S(2)}) %collective-permute-start.1) | collective-permute-done | bytes 983072 | tf_op jit(solution)/shard_map/ppermute | solution.py:14
  61.2 1.0 %fusion.4 = f32[320,320]{1,0:T(8,128)S(1)} fusion(f32[320,768]{1,0:T(8,128)S(1)} %convolution_bitcast_fusion, f32[768,320]{1,0:T(8,128)S(1)} %bitcast.24), kind=kOutput, calls=%fused_computation.18 | convolution fusion | flops 471859200 | bytes 2375680 | tf_op jit(solution)/shard_map/dot_general | solution.py:18
  62.1 0.2 pad_add_fusion
  62.4 0.1 fusion.1
  62.4 2.2 %collective-permute-start.2 = (f32[64,448]{1,0:T(8,128)S(1)}, f32[64,448]{1,0:T(8,128)S(1)}, u32[]{:S(2)}, u32[]{:S(2)}) collective-permute-start(f32[64,448]{1,0:T(8,128)S(1)} %get-tuple-element.15), channel_id=1, source_target_pairs={{0,1},{1,2},{2,3},{3,4},{4,5},{5,6},{6,7},{7,8},{8,9},{9,10},{10,1... | collective-permute-start | bytes 344072 | tf_op jit(solution)/shard_map/ppermute | solution.py:14
  64.7 2.4 %collective-permute-start.3 = (f32[64,448]{1,0:T(8,128)S(1)}, f32[64,448]{1,0:T(8,128)S(1)}, u32[]{:S(2)}, u32[]{:S(2)}) collective-permute-start(f32[64,448]{1,0:T(8,128)S(1)} %get-tuple-element.14), channel_id=1, source_target_pairs={{0,2},{1,3},{2,4},{3,5},{4,6},{5,7},{6,8},{7,9},{8,10},{9,11},{10,... | collective-permute-start | bytes 344072 | tf_op jit(solution)/shard_map/ppermute | solution.py:14
  67.1 6.9 %collective-permute-start.4 = (f32[64,448]{1,0:T(8,128)S(1)}, f32[64,448]{1,0:T(8,128)S(1)}, u32[]{:S(2)}, u32[]{:S(2)}) collective-permute-start(f32[64,448]{1,0:T(8,128)S(1)} %get-tuple-element.13), channel_id=1, source_target_pairs={{1,0},{2,1},{3,2},{4,3},{5,4},{6,5},{7,6},{8,7},{9,8},{10,9},{11,1... | collective-permute-start | bytes 344072 | tf_op jit(solution)/shard_map/ppermute | solution.py:14
  74.0 3.9 %collective-permute-start.5 = (f32[64,448]{1,0:T(8,128)S(1)}, f32[64,448]{1,0:T(8,128)S(1)}, u32[]{:S(2)}, u32[]{:S(2)}) collective-permute-start(f32[64,448]{1,0:T(8,128)S(1)} %get-tuple-element.12), channel_id=1, source_target_pairs={{2,0},{3,1},{4,2},{5,3},{6,4},{7,5},{8,6},{9,7},{10,8},{11,9},{12,... | collective-permute-start | bytes 344072 | tf_op jit(solution)/shard_map/ppermute | solution.py:14
  77.9 0.0 collective-permute-done.2
  77.9 0.0 collective-permute-done.3
  77.9 0.4 collective-permute-done.4
  78.3 8.3 %collective-permute-done.5 = f32[64,448]{1,0:T(8,128)S(1)} collective-permute-done((f32[64,448]{1,0:T(8,128)S(1)}, f32[64,448]{1,0:T(8,128)S(1)}, u32[]{:S(2)}, u32[]{:S(2)}) %collective-permute-start.5) | collective-permute-done | bytes 114720 | tf_op jit(solution)/shard_map/ppermute | solution.py:14
  86.6 0.8 add_bitcast_fusion
  (10 shorter events, 0.0 us)
Async XLA Ops:
  1.0 13.7 %copy-start.1 = (s32[12]{0:T(128)S(1)}, s32[12]{0:T(128)}, u32[]{:S(2)}) copy-start(s32[12]{0:T(128)} %param.7) | copy-start | bytes 148
  1.0 13.8 %copy-start = (s32[12,14]{1,0:T(8,128)S(1)}, s32[12,14]{1,0:T(8,128)}, u32[]{:S(2)}) copy-start(s32[12,14]{1,0:T(8,128)} %param.6) | copy-start | bytes 2020
  2.4 35.0 %collective-permute-start = (f32[12,64,320]{2,1,0:T(8,128)S(1)}, f32[12,64,320]{2,1,0:T(8,128)S(1)}, u32[]{:S(2)}, u32[]{:S(2)}) collective-permute-start(f32[12,64,320]{2,1,0:T(8,128)S(1)} %broadcast_multiply_fusion), channel_id=1, source_target_pairs={{0,1},{1,2},{2,3},{3,4},{4,5},{5,6},{6,7},{7,8},{8,9},{9,10},{10,1... | collective-permute-start | bytes 2949128 | tf_op jit(solution)/shard_map/ppermute | solution.py:14
  6.8 54.3 %collective-permute-start.1 = (f32[12,64,320]{2,1,0:T(8,128)S(1)}, f32[12,64,320]{2,1,0:T(8,128)S(1)}, u32[]{:S(2)}, u32[]{:S(2)}) collective-permute-start(f32[12,64,320]{2,1,0:T(8,128)S(1)} %broadcast_multiply_fusion), channel_id=1, source_target_pairs={{1,0},{2,1},{3,2},{4,3},{5,4},{6,5},{7,6},{8,7},{9,8},{10,9},{11,1... | collective-permute-start | bytes 2949128 | tf_op jit(solution)/shard_map/ppermute | solution.py:14
  28.7 1.7 %copy-start.3 = (f32[12,64,768]{2,1,0:T(8,128)S(1)}, f32[12,64,768]{2,1,0:T(8,128)}, u32[]{:S(2)}) copy-start(f32[12,64,768]{2,1,0:T(8,128)} %get-tuple-element.8) | copy-start | bytes 7077892
  30.4 1.8 %copy-start.2 = (f32[12,64,768]{2,1,0:T(8,128)S(1)}, f32[12,64,768]{2,1,0:T(8,128)}, u32[]{:S(2)}) copy-start(f32[12,64,768]{2,1,0:T(8,128)} %get-tuple-element.10) | copy-start | bytes 7077892
  62.4 15.5 %collective-permute-start.2 = (f32[64,448]{1,0:T(8,128)S(1)}, f32[64,448]{1,0:T(8,128)S(1)}, u32[]{:S(2)}, u32[]{:S(2)}) collective-permute-start(f32[64,448]{1,0:T(8,128)S(1)} %get-tuple-element.15), channel_id=1, source_target_pairs={{0,1},{1,2},{2,3},{3,4},{4,5},{5,6},{6,7},{7,8},{8,9},{9,10},{10,1... | collective-permute-start | bytes 344072 | tf_op jit(solution)/shard_map/ppermute | solution.py:14
  64.7 13.2 %collective-permute-start.3 = (f32[64,448]{1,0:T(8,128)S(1)}, f32[64,448]{1,0:T(8,128)S(1)}, u32[]{:S(2)}, u32[]{:S(2)}) collective-permute-start(f32[64,448]{1,0:T(8,128)S(1)} %get-tuple-element.14), channel_id=1, source_target_pairs={{0,2},{1,3},{2,4},{3,5},{4,6},{5,7},{6,8},{7,9},{8,10},{9,11},{10,... | collective-permute-start | bytes 344072 | tf_op jit(solution)/shard_map/ppermute | solution.py:14
  67.1 11.2 %collective-permute-start.4 = (f32[64,448]{1,0:T(8,128)S(1)}, f32[64,448]{1,0:T(8,128)S(1)}, u32[]{:S(2)}, u32[]{:S(2)}) collective-permute-start(f32[64,448]{1,0:T(8,128)S(1)} %get-tuple-element.13), channel_id=1, source_target_pairs={{1,0},{2,1},{3,2},{4,3},{5,4},{6,5},{7,6},{8,7},{9,8},{10,9},{11,1... | collective-permute-start | bytes 344072 | tf_op jit(solution)/shard_map/ppermute | solution.py:14
  74.0 12.7 %collective-permute-start.5 = (f32[64,448]{1,0:T(8,128)S(1)}, f32[64,448]{1,0:T(8,128)S(1)}, u32[]{:S(2)}, u32[]{:S(2)}) collective-permute-start(f32[64,448]{1,0:T(8,128)S(1)} %get-tuple-element.12), channel_id=1, source_target_pairs={{2,0},{3,1},{4,2},{5,3},{6,4},{7,5},{8,6},{9,7},{10,8},{11,9},{12,... | collective-permute-start | bytes 344072 | tf_op jit(solution)/shard_map/ppermute | solution.py:14

commit v6 on v5

--- a/solution.py
+++ b/solution.py
@@ -58,6 +58,79 @@
     )(slot_table, a_vals)
 
 
+def exchange_kernel(terms_ref, out_ref, recv, send_sem, recv_sem):
+    col_count = lax.axis_size("cols")
+    total = lax.axis_size("rows") * col_count
+    me = lax.axis_index("rows") * col_count + lax.axis_index("cols")
+    centre = terms_ref.shape[0] // 2
+    shifts = [s - centre for s in range(terms_ref.shape[0]) if s != centre]
+
+    def mesh_id(pos):
+        return (pos // col_count, pos % col_count)
+
+    barrier = pltpu.get_barrier_semaphore()
+    for shift in shifts:
+        @pl.when((me + shift >= 0) & (me + shift < total))
+        def _():
+            pl.semaphore_signal(
+                barrier, 1, device_id=mesh_id(me + shift), device_id_type=pl.DeviceIdType.MESH
+            )
+
+    peers = 0
+    for shift in shifts:
+        peers = peers + ((me + shift >= 0) & (me + shift < total)).astype(jnp.int32)
+    pl.semaphore_wait(barrier, peers)
+
+    copies = []
+    for u, shift in enumerate(shifts):
+        copy = pltpu.make_async_remote_copy(
+            src_ref=terms_ref.at[shift + centre],
+            dst_ref=recv.at[u],
+            send_sem=send_sem.at[u],
+            recv_sem=recv_sem.at[u],
+            device_id=mesh_id(me + shift),
+            device_id_type=pl.DeviceIdType.MESH,
+        )
+        copies.append(copy)
+
+        @pl.when((me + shift >= 0) & (me + shift < total))
+        def _():
+            copy.start()
+
+    for u, shift in enumerate(shifts):
+        sends = (me + shift >= 0) & (me + shift < total)
+        gets = (me - shift >= 0) & (me - shift < total)
+
+        @pl.when(sends)
+        def _():
+            copies[u].wait_send()
+
+        @pl.when(gets)
+        def _():
+            copies[u].wait_recv()
+            out_ref[u] = recv[u]
+
+        @pl.when(jnp.logical_not(gets))
+        def _():
+            out_ref[u] = jnp.zeros(out_ref.shape[1:], out_ref.dtype)
+
+
+def exchange(terms):
+    parts, block_size, wide = terms.shape
+    return pl.pallas_call(
+        exchange_kernel,
+        out_shape=jax.ShapeDtypeStruct((parts - 1, block_size, wide), jnp.float32),
+        in_specs=[pl.BlockSpec(memory_space=pltpu.VMEM)],
+        out_specs=pl.BlockSpec(memory_space=pltpu.VMEM),
+        scratch_shapes=[
+            pltpu.VMEM((parts - 1, block_size, wide), jnp.float32),
+            pltpu.SemaphoreType.DMA((parts - 1,)),
+            pltpu.SemaphoreType.DMA((parts - 1,)),
+        ],
+        compiler_params=pltpu.CompilerParams(collective_id=0, has_side_effects=True),
+    )(terms)
+
+
 def shards(a_vals, a_cols, a_count, p_vals, p_mask):
     rows_here = a_cols.shape[0]
     slot_count = a_cols.shape[1]
@@ -106,11 +179,10 @@
     def spread(s, block):
         return jnp.pad(block, ((0, 0), ((prol_slots - 1 - s) * block_size, s * block_size)))
 
+    arrived = exchange(terms)
     result = spread(2, terms[2])
-    result = result + spread(3, from_behind(terms[3], flat_axis, 1))
-    result = result + spread(4, from_behind(terms[4], flat_axis, 2))
-    result = result + spread(1, from_behind(terms[1], flat_axis, -1))
-    result = result + spread(0, from_behind(terms[0], flat_axis, -2))
+    for u, s in enumerate([0, 1, 3, 4]):
+        result = result + spread(s, arrived[u])
     return result.reshape(1, block_size, (prol_slots + 6) * block_size)
 
 

time: 87.9 us -> 88.5 us (level)
  Pallas kernels: 9.14 us -> 31.2 us
  starting transfers between devices: 27.2 us -> 11.8 us
  waiting for transfers between devices: 35 us -> 26.3 us
  local copies, waits for them, and re-layouts: 1.66 us -> 3.56 us
    pallas_call x0 -> x1, Pallas kernels: none -> 22 us  [exchange(): pl.pallas_call(exchange_kernel, out_shape=jax.ShapeDtypeStruct((parts - 1...]
    ppermute x6 -> x2, starting transfers between devices: 27.2 us -> 11.8 us  [from_behind(): return lax.ppermute(array, axis, pairs)]
    ppermute x6 -> x2, waiting for transfers between devices: 35 us -> 26.3 us  [from_behind(): return lax.ppermute(array, axis, pairs)]
    squeeze x0 -> x1, local copies, waits for them, and re-layouts: none -> 1.13 us  [shards(): result = result + spread(s, arrived[u])]
  transfers between devices with their start and end apart: 6 -> 2, of which waited for: 4 -> 2; matrix products, arithmetic and copies ran while one was open for 12% -> 12% of each run, Pallas kernels for 10% -> 10%
where the time goes in v6:
time: 88.5 us; the launch traced here: 87.2 us
  Pallas kernels  31.2 us (35%)
  waiting for transfers between devices  26.3 us (30%)
  starting transfers between devices  11.8 us (13%)
  matrix products  9.64 us (11%)
  other arithmetic  4.63 us (5%)
  local copies, waits for them, and re-layouts  3.56 us (4%)
    ppermute x2, waiting for transfers between devices, from_behind(): return lax.ppermute(array, axis, pairs)  26.3 us
    pallas_call x1, Pallas kernels, exchange(): pl.pallas_call(exchange_kernel, out_shape=jax.ShapeDtypeStruct((parts - 1...  22 us
    ppermute x2, starting transfers between devices, from_behind(): return lax.ppermute(array, axis, pairs)  11.8 us
    pallas_call x1, Pallas kernels, dense_sides(): pl.pallas_call(dense_kernel, out_shape=[jax.ShapeDtypeStruct((rows_here,...  9.14 us
    dot_general x3, matrix products, pt_times(): lax.dot_general(p_own, dense[side], (((0,), (0,)), ((), ())), precision=M...  6.73 us
    dot_general x3, matrix products, mm(): jnp.dot(a, b, precision=MATMUL_PRECISION, preferred_element_type=jnp.floa...  2.9 us
  transfers between devices with their start and end apart: 2, of which 2 were waited for; matrix products, arithmetic and copies ran while one was open for 12% of the time, Pallas kernels for 10%

profile of v6, /device:TPU:1, one launch (start us, length us, event | category | flops | bytes accessed | tf_op | source)
XLA Modules:
  0.0 87.2 jit_solution(9977622579393890925)
XLA Ops:
  0.0 0.8 convert_multiply_fusion
  0.8 0.1 copy.8
  0.9 0.1 broadcast_in_dim.10
  0.9 0.1 mul.27
  1.0 0.0 copy-start.2
  1.0 1.4 %broadcast_multiply_fusion = f32[12,64,320]{2,1,0:T(8,128)S(1)} fusion(f32[12,64,320]{2,1,0:T(8,128)} %param.8, f32[12,320]{1,0:T(8,128)S(1)} %mul.27), kind=kLoop, calls=%fused_computation.4 | loop fusion | flops 245760 | bytes 1981440 | tf_op jit(solution)/shard_map/mul | solution.py:146
  2.4 4.4 %collective-permute-start = (f32[12,64,320]{2,1,0:T(8,128)S(1)}, f32[12,64,320]{2,1,0:T(8,128)S(1)}, u32[]{:S(2)}, u32[]{:S(2)}) collective-permute-start(f32[12,64,320]{2,1,0:T(8,128)S(1)} %broadcast_multiply_fusion), channel_id=1, source_target_pairs={{0,1},{1,2},{2,3},{3,4},{4,5},{5,6},{6,7},{7,8},{8,9},{9,10},{10,1... | collective-permute-start | bytes 2949128 | tf_op jit(solution)/shard_map/ppermute | solution.py:14
  6.8 7.4 %collective-permute-start.1 = (f32[12,64,320]{2,1,0:T(8,128)S(1)}, f32[12,64,320]{2,1,0:T(8,128)S(1)}, u32[]{:S(2)}, u32[]{:S(2)}) collective-permute-start(f32[12,64,320]{2,1,0:T(8,128)S(1)} %broadcast_multiply_fusion), channel_id=1, source_target_pairs={{1,0},{2,1},{3,2},{4,3},{5,4},{6,5},{7,6},{8,7},{9,8},{10,9},{11,1... | collective-permute-start | bytes 2949128 | tf_op jit(solution)/shard_map/ppermute | solution.py:14
  14.2 0.5 iota_add_fusion
  14.7 0.0 copy-done.2
  14.7 0.1 iota_compare_fusion.1
  14.8 0.0 copy-done.1
  14.8 0.8 select_reduce_fusion
  15.6 0.7 sub.23.slot_ref
  16.3 9.1 %shard_map.55 = (f32[12,64,768]{2,1,0:T(8,128)}, f32[12,64,768]{2,1,0:T(8,128)}, f32[12,64,768]{2,1,0:T(8,128)}) custom-call(s32[432]{0:T(512)} %sub.23.slot_ref, f32[12,64,896]{2,1,0:T(8,128)} %a_ref.1), custom_call_target="tpu_custom_call" | custom-call | tf_op jit(solution)/shard_map/pallas_call | solution.py:50
  25.4 3.3 %convolution_bitcast_fusion.1 = f32[320,768]{1,0:T(8,128)S(1)} fusion(f32[12,64,320]{2,1,0:T(8,128)S(1)} %broadcast_multiply_fusion, f32[12,64,768]{2,1,0:T(8,128)} %get-tuple-element.9), kind=kOutput, calls=%fused_computation.1 | convolution fusion | flops 1132462080 | bytes 4325376 | tf_op jit(solution)/shard_map/dot_general | solution.py:162
  28.7 0.0 copy-start.4
  28.7 1.0 %fusion.2 = f32[320,320]{1,0:T(8,128)S(1)} fusion(f32[320,768]{1,0:T(8,128)S(1)} %convolution_bitcast_fusion.1, f32[768,320]{1,0:T(8,128)S(1)} %bitcast.32), kind=kOutput, calls=%fused_computation.20 | convolution fusion | flops 471859200 | bytes 2375680 | tf_op jit(solution)/shard_map/dot_general | solution.py:18
  29.7 0.7 copy-done.4
  30.4 1.7 %convolution_bitcast_fusion.2 = f32[320,768]{1,0:T(8,128)S(1)} fusion(f32[12,64,320]{2,1,0:T(8,128)S(1)} %broadcast_multiply_fusion, f32[12,64,768]{2,1,0:T(8,128)S(1)} %copy-done.4), kind=kOutput, calls=%fused_computation.2 | convolution fusion | flops 1132462080 | bytes 4325376 | tf_op jit(solution)/shard_map/dot_general | solution.py:162
  32.1 0.0 copy-done.3
  32.1 1.7 %convolution_bitcast_fusion = f32[320,768]{1,0:T(8,128)S(1)} fusion(f32[12,64,320]{2,1,0:T(8,128)S(1)} %broadcast_multiply_fusion, f32[12,64,768]{2,1,0:T(8,128)S(1)} %copy-done.3), kind=kOutput, calls=%fused_computation | convolution fusion | flops 1132462080 | bytes 4325376 | tf_op jit(solution)/shard_map/dot_general | solution.py:162
  33.9 3.6 %collective-permute-done = f32[12,64,320]{2,1,0:T(8,128)S(1)} collective-permute-done((f32[12,64,320]{2,1,0:T(8,128)S(1)}, f32[12,64,320]{2,1,0:T(8,128)S(1)}, u32[]{:S(2)}, u32[]{:S(2)}) %collective-permute-start) | collective-permute-done | bytes 983072 | tf_op jit(solution)/shard_map/ppermute | solution.py:14
  37.4 1.0 %fusion.1 = f32[320,320]{1,0:T(8,128)S(1)} fusion(f32[320,768]{1,0:T(8,128)S(1)} %convolution_bitcast_fusion.2, f32[768,320]{1,0:T(8,128)S(1)} %bitcast.35), kind=kOutput, calls=%fused_computation.19 | convolution fusion | flops 471859200 | bytes 2375680 | tf_op jit(solution)/shard_map/dot_general | solution.py:18
  38.4 22.8 %collective-permute-done.1 = f32[12,64,320]{2,1,0:T(8,128)S(1)} collective-permute-done((f32[12,64,320]{2,1,0:T(8,128)S(1)}, f32[12,64,320]{2,1,0:T(8,128)S(1)}, u32[]{:S(2)}, u32[]{:S(2)}) %collective-permute-start.1) | collective-permute-done | bytes 983072 | tf_op jit(solution)/shard_map/ppermute | solution.py:14
  61.2 1.0 %fusion.3 = f32[320,320]{1,0:T(8,128)S(1)} fusion(f32[320,768]{1,0:T(8,128)S(1)} %convolution_bitcast_fusion, f32[768,320]{1,0:T(8,128)S(1)} %bitcast.34), kind=kOutput, calls=%fused_computation.21 | convolution fusion | flops 471859200 | bytes 2375680 | tf_op jit(solution)/shard_map/dot_general | solution.py:18
  62.1 0.2 pad_add_fusion
  62.4 0.0 copy-start
  62.4 0.8 copy-done
  63.2 22.0 %shard_map.56 = f32[4,64,448]{2,1,0:T(8,128)} custom-call(f32[5,64,448]{2,1,0:T(8,128)} %bitcast.33), custom_call_target="tpu_custom_call" | custom-call | tf_op jit(solution)/shard_map/pallas_call | solution.py:120
  85.3 1.1 %slice_bitcast_fusion.3 = (f32[64,448]{1,0:T(8,128)S(1)}, f32[64,448]{1,0:T(8,128)S(1)}, f32[64,448]{1,0:T(8,128)S(1)}, f32[64,448]{1,0:T(8,128)S(1)}) fusion(f32[4,64,448]{2,1,0:T(8,128)} %shard_map.56), kind=kLoop, calls=%fused_computation.9 | loop fusion | bytes 917504 | tf_op jit(solution)/shard_map/squeeze | solution.py:185
  86.4 0.8 add_bitcast_fusion
  (6 shorter events, 0.0 us)
Async XLA Ops:
  1.0 13.7 %copy-start.2 = (s32[12]{0:T(128)S(1)}, s32[12]{0:T(128)}, u32[]{:S(2)}) copy-start(s32[12]{0:T(128)} %param.7) | copy-start | bytes 148
  1.0 13.8 %copy-start.1 = (s32[12,14]{1,0:T(8,128)S(1)}, s32[12,14]{1,0:T(8,128)}, u32[]{:S(2)}) copy-start(s32[12,14]{1,0:T(8,128)} %param.6) | copy-start | bytes 2020
  2.4 35.0 %collective-permute-start = (f32[12,64,320]{2,1,0:T(8,128)S(1)}, f32[12,64,320]{2,1,0:T(8,128)S(1)}, u32[]{:S(2)}, u32[]{:S(2)}) collective-permute-start(f32[12,64,320]{2,1,0:T(8,128)S(1)} %broadcast_multiply_fusion), channel_id=1, source_target_pairs={{0,1},{1,2},{2,3},{3,4},{4,5},{5,6},{6,7},{7,8},{8,9},{9,10},{10,1... | collective-permute-start | bytes 2949128 | tf_op jit(solution)/shard_map/ppermute | solution.py:14
  6.8 54.3 %collective-permute-start.1 = (f32[12,64,320]{2,1,0:T(8,128)S(1)}, f32[12,64,320]{2,1,0:T(8,128)S(1)}, u32[]{:S(2)}, u32[]{:S(2)}) collective-permute-start(f32[12,64,320]{2,1,0:T(8,128)S(1)} %broadcast_multiply_fusion), channel_id=1, source_target_pairs={{1,0},{2,1},{3,2},{4,3},{5,4},{6,5},{7,6},{8,7},{9,8},{10,9},{11,1... | collective-permute-start | bytes 2949128 | tf_op jit(solution)/shard_map/ppermute | solution.py:14
  28.7 1.7 %copy-start.4 = (f32[12,64,768]{2,1,0:T(8,128)S(1)}, f32[12,64,768]{2,1,0:T(8,128)}, u32[]{:S(2)}) copy-start(f32[12,64,768]{2,1,0:T(8,128)} %get-tuple-element.8) | copy-start | bytes 7077892
  30.4 1.7 %copy-start.3 = (f32[12,64,768]{2,1,0:T(8,128)S(1)}, f32[12,64,768]{2,1,0:T(8,128)}, u32[]{:S(2)}) copy-start(f32[12,64,768]{2,1,0:T(8,128)} %get-tuple-element.10) | copy-start | bytes 7077892
  62.4 0.8 copy-start

commit v7 on v6

--- a/solution.py
+++ b/solution.py
@@ -16,6 +16,12 @@
 
 def mm(a, b):
     return jnp.dot(a, b, precision=MATMUL_PRECISION, preferred_element_type=jnp.float32)
+
+
+CHUNKS = 4
+
+
+CHUNKS = 4
 
 
 def dense_kernel(slot_ref, a_ref, *out_refs):
@@ -58,6 +64,82 @@
     )(slot_table, a_vals)
 
 
+def neighbour_kernel(p_ref, lower_ref, upper_ref, landed, send_sem, recv_sem):
+    col_count = lax.axis_size("cols")
+    total = lax.axis_size("rows") * col_count
+    me = lax.axis_index("rows") * col_count + lax.axis_index("cols")
+    chunk = p_ref.shape[0] // CHUNKS
+    routes = [(1, 0), (-1, 1)]
+    barrier = pltpu.get_barrier_semaphore()
+    peers = 0
+    for shift, _ in routes:
+        there = (me + shift >= 0) & (me + shift < total)
+        peers = peers + there.astype(jnp.int32)
+
+        @pl.when(there)
+        def _():
+            pl.semaphore_signal(
+                barrier,
+                1,
+                device_id=((me + shift) // col_count, (me + shift) % col_count),
+                device_id_type=pl.DeviceIdType.MESH,
+            )
+
+    pl.semaphore_wait(barrier, peers)
+    copies = []
+    for c in range(CHUNKS):
+        for shift, slot in routes:
+            there = (me + shift >= 0) & (me + shift < total)
+            rows = pl.ds(c * chunk, chunk)
+            copy = pltpu.make_async_remote_copy(
+                src_ref=p_ref.at[rows],
+                dst_ref=landed.at[slot, rows],
+                send_sem=send_sem.at[slot * CHUNKS + c],
+                recv_sem=recv_sem.at[slot * CHUNKS + c],
+                device_id=((me + shift) // col_count, (me + shift) % col_count),
+                device_id_type=pl.DeviceIdType.MESH,
+            )
+            copies.append((shift, slot, c, copy))
+
+            @pl.when(there)
+            def _():
+                copy.start()
+
+    for shift, slot, c, copy in copies:
+        sends = (me + shift >= 0) & (me + shift < total)
+        gets = (me - shift >= 0) & (me - shift < total)
+        target = (lower_ref, upper_ref)[slot]
+        rows = pl.ds(c * chunk, chunk)
+
+        @pl.when(sends)
+        def _():
+            copy.wait_send()
+
+        @pl.when(gets)
+        def _():
+            copy.wait_recv()
+            target[rows] = landed[slot, rows]
+
+        @pl.when(jnp.logical_not(gets))
+        def _():
+            target[rows] = jnp.zeros(target[rows].shape, target.dtype)
+
+
+def neighbours(p_rows):
+    return pl.pallas_call(
+        neighbour_kernel,
+        out_shape=[jax.ShapeDtypeStruct(p_rows.shape, jnp.float32)] * 2,
+        in_specs=[pl.BlockSpec(memory_space=pltpu.VMEM)],
+        out_specs=[pl.BlockSpec(memory_space=pltpu.VMEM)] * 2,
+        scratch_shapes=[
+            pltpu.VMEM((2,) + p_rows.shape, jnp.float32),
+            pltpu.SemaphoreType.DMA((2 * CHUNKS,)),
+            pltpu.SemaphoreType.DMA((2 * CHUNKS,)),
+        ],
+        compiler_params=pltpu.CompilerParams(collective_id=1, has_side_effects=True),
+    )(p_rows)
+
+
 def exchange_kernel(terms_ref, out_ref, recv, send_sem, recv_sem):
     col_count = lax.axis_size("cols")
     total = lax.axis_size("rows") * col_count
@@ -144,8 +226,6 @@
     inside = ((target >= 0) & (target < group_total)).astype(jnp.float32)
     keep = jnp.repeat(p_mask.astype(jnp.float32) * inside[None, :], block_size, axis=1)
     pflat = p_vals * keep[:, None, :]
-    lower_rows = from_behind(pflat, flat_axis, 1)
-    upper_rows = from_behind(pflat, flat_axis, -1)
     span = rows_here * block_size
     width = prol_slots * block_size
     p_own = pflat.reshape(span, width)
@@ -157,6 +237,7 @@
     slot_numbers = jnp.arange(1, slot_count + 1, dtype=jnp.int32)[None, :, None]
     slot_table = (jnp.sum(jnp.where(hit, slot_numbers, 0), axis=1) - 1).reshape(-1)
     dense = [side.reshape(span, span) for side in dense_sides(slot_table, a_vals)]
+    lower_rows, upper_rows = neighbours(pflat)
 
     def pt_times(side):
         return lax.dot_general(

time: 88.5 us -> 114 us (1.29)
  the two profiles are of different devices: /device:TPU:1 before, /device:TPU:30 now
where the time goes in v7:
time: 114 us
  Pallas kernels  92.8 us (81%)
  matrix products  12.7 us (11%)
  other arithmetic  4.31 us (4%)
  local copies, waits for them, and re-layouts  3.65 us (3%)
    pallas_call x1, Pallas kernels, neighbours(): pl.pallas_call(neighbour_kernel, out_shape=[jax.ShapeDtypeStruct(p_rows.s...  59.1 us
    pallas_call x1, Pallas kernels, exchange(): pl.pallas_call(exchange_kernel, out_shape=jax.ShapeDtypeStruct((parts - 1...  24.5 us
    pallas_call x1, Pallas kernels, dense_sides(): pl.pallas_call(dense_kernel, out_shape=[jax.ShapeDtypeStruct((rows_here,...  9.18 us
    dot_general x3, matrix products, pt_times(): lax.dot_general(p_own, dense[side], (((0,), (0,)), ((), ())), precision=M...  8.41 us
    dot_general x3, matrix products, mm(): jnp.dot(a, b, precision=MATMUL_PRECISION, preferred_element_type=jnp.floa...  4.31 us

profile of v7, /device:TPU:30, one launch (start us, length us, event | category | flops | bytes accessed | tf_op | source)
XLA Modules:
  0.0 113.6 jit_solution(17046083328948041903)
XLA Ops:
  0.0 0.8 convert_multiply_fusion
  0.8 0.1 copy.8
  0.9 0.1 broadcast_in_dim.10
  0.9 0.1 mul.27
  1.0 0.0 copy-start.3
  1.0 1.4 %broadcast_multiply_fusion.p_ref = f32[12,64,320]{2,1,0:T(8,128)S(1)} fusion(f32[12,64,320]{2,1,0:T(8,128)} %param.8, f32[12,320]{1,0:T(8,128)S(1)} %mul.27), kind=kLoop, calls=%fused_computation.4 | loop fusion | flops 245760 | bytes 1981440 | tf_op jit(solution)/shard_map/mul | solution.py:228
  2.4 0.0 copy-start
  2.4 0.0 copy-done.3
  2.5 0.0 copy-done.4
  2.5 0.1 iota_compare_fusion.1
  2.6 0.1 select_reduce_fusion
  2.7 0.7 sub.23.slot_ref
  3.4 9.2 %shard_map.55 = (f32[12,64,768]{2,1,0:T(8,128)}, f32[12,64,768]{2,1,0:T(8,128)}, f32[12,64,768]{2,1,0:T(8,128)}) custom-call(s32[432]{0:T(512)} %sub.23.slot_ref, f32[12,64,896]{2,1,0:T(8,128)} %a_ref.1), custom_call_target="tpu_custom_call" | custom-call | tf_op jit(solution)/shard_map/pallas_call | solution.py:56
  12.6 0.0 copy-done
  12.6 3.2 %convolution_bitcast_fusion.2 = f32[320,768]{1,0:T(8,128)S(1)} fusion(f32[12,64,320]{2,1,0:T(8,128)S(1)} %broadcast_multiply_fusion.p_ref, f32[12,64,768]{2,1,0:T(8,128)} %get-tuple-element.10), kind=kOutput, calls=%fused_computation.2 | convolution fusion | flops 1132462080 | bytes 4325376 | tf_op jit(solution)/shard_map/dot_general | solution.py:243
  15.8 59.1 %shard_map.56 = (f32[12,64,320]{2,1,0:T(8,128)}, f32[12,64,320]{2,1,0:T(8,128)}) custom-call(f32[12,64,320]{2,1,0:T(8,128)} %copy-done), custom_call_target="tpu_custom_call" | custom-call | tf_op jit(solution)/shard_map/pallas_call | solution.py:129
  74.9 0.0 copy-start.1
  75.0 2.3 %fusion.1 = f32[320,320]{1,0:T(8,128)S(1)} fusion(f32[320,768]{1,0:T(8,128)S(1)} %convolution_bitcast_fusion.2, f32[768,320]{1,0:T(8,128)} %bitcast.35), kind=kOutput, calls=%fused_computation.19 | convolution fusion | flops 471859200 | bytes 2375680 | tf_op jit(solution)/shard_map/dot_general | solution.py:18
  77.3 0.0 copy-done.1
  77.3 0.0 copy-start.2
  77.3 3.4 %convolution_bitcast_fusion = f32[320,768]{1,0:T(8,128)S(1)} fusion(f32[12,64,320]{2,1,0:T(8,128)S(1)} %copy-done.1, f32[12,64,768]{2,1,0:T(8,128)} %get-tuple-element.13), kind=kOutput, calls=%fused_computation | convolution fusion | flops 1132462080 | bytes 4325376 | tf_op jit(solution)/shard_map/dot_general | solution.py:243
  80.7 0.0 copy-done.2
  80.7 0.0 copy-start.5
  80.7 1.0 fusion.3
  81.8 0.6 copy-done.5
  82.4 1.7 %convolution_bitcast_fusion.1 = f32[320,768]{1,0:T(8,128)S(1)} fusion(f32[12,64,320]{2,1,0:T(8,128)S(1)} %copy-done.1, f32[12,64,768]{2,1,0:T(8,128)S(1)} %copy-done.5), kind=kOutput, calls=%fused_computation.1 | convolution fusion | flops 1132462080 | bytes 4325376 | tf_op jit(solution)/shard_map/dot_general | solution.py:243
  84.2 1.0 fusion.2
  85.2 1.1 pad_add_fusion
  86.2 24.5 %shard_map.57 = f32[4,64,448]{2,1,0:T(8,128)} custom-call(f32[5,64,448]{2,1,0:T(8,128)} %bitcast.33), custom_call_target="tpu_custom_call" | custom-call | tf_op jit(solution)/shard_map/pallas_call | solution.py:202
  110.8 1.1 slice_bitcast_fusion.3
  111.9 0.9 slice.21
  112.8 0.8 add_bitcast_fusion
  (5 shorter events, 0.0 us)
Async XLA Ops:
  1.0 1.4 %copy-start.3 = (s32[12,14]{1,0:T(8,128)S(1)}, s32[12,14]{1,0:T(8,128)}, u32[]{:S(2)}) copy-start(s32[12,14]{1,0:T(8,128)} %param.6) | copy-start | bytes 2020
  1.0 1.5 %copy-start.4 = (s32[12]{0:T(128)S(1)}, s32[12]{0:T(128)}, u32[]{:S(2)}) copy-start(s32[12]{0:T(128)} %param.7) | copy-start | bytes 148
  2.4 10.1 %copy-start = (f32[12,64,320]{2,1,0:T(8,128)}, f32[12,64,320]{2,1,0:T(8,128)S(1)}, u32[]{:S(2)}) copy-start(f32[12,64,320]{2,1,0:T(8,128)S(1)} %broadcast_multiply_fusion.p_ref) | copy-start | bytes 2949124
  74.9 2.3 %copy-start.1 = (f32[12,64,320]{2,1,0:T(8,128)S(1)}, f32[12,64,320]{2,1,0:T(8,128)}, u32[]{:S(2)}) copy-start(f32[12,64,320]{2,1,0:T(8,128)} %copy-done) | copy-start | bytes 2949124
  77.3 3.4 %copy-start.2 = (f32[12,64,320]{2,1,0:T(8,128)S(1)}, f32[12,64,320]{2,1,0:T(8,128)}, u32[]{:S(2)}) copy-start(f32[12,64,320]{2,1,0:T(8,128)} %get-tuple-element.14) | copy-start | bytes 2949124
  80.7 1.7 %copy-start.5 = (f32[12,64,768]{2,1,0:T(8,128)S(1)}, f32[12,64,768]{2,1,0:T(8,128)}, u32[]{:S(2)}) copy-start(f32[12,64,768]{2,1,0:T(8,128)} %get-tuple-element.12) | copy-start | bytes 7077892

commit v8 on v5

--- a/solution.py
+++ b/solution.py
@@ -107,10 +107,10 @@
         return jnp.pad(block, ((0, 0), ((prol_slots - 1 - s) * block_size, s * block_size)))
 
     result = spread(2, terms[2])
+    result = result + spread(0, from_behind(terms[0], flat_axis, -2))
+    result = result + spread(1, from_behind(terms[1], flat_axis, -1))
+    result = result + spread(4, from_behind(terms[4], flat_axis, 2))
     result = result + spread(3, from_behind(terms[3], flat_axis, 1))
-    result = result + spread(4, from_behind(terms[4], flat_axis, 2))
-    result = result + spread(1, from_behind(terms[1], flat_axis, -1))
-    result = result + spread(0, from_behind(terms[0], flat_axis, -2))
     return result.reshape(1, block_size, (prol_slots + 6) * block_size)
 
 

time: 87.9 us -> 88.9 us (1.011)
  the two profiles are of different devices: /device:TPU:1 before, /device:TPU:24 now
where the time goes in v8:
time: 88.9 us; the launch traced here: 88.5 us
  waiting for transfers between devices  35.5 us (40%)
  starting transfers between devices  27.7 us (31%)
  matrix products  9.64 us (11%)
  Pallas kernels  9.13 us (10%)
  other arithmetic  4.63 us (5%)
  local copies, waits for them, and re-layouts  1.66 us (2%)
    ppermute x6, waiting for transfers between devices, from_behind(): return lax.ppermute(array, axis, pairs)  35.5 us
    ppermute x6, starting transfers between devices, from_behind(): return lax.ppermute(array, axis, pairs)  27.7 us
    pallas_call x1, Pallas kernels, dense_sides(): pl.pallas_call(dense_kernel, out_shape=[jax.ShapeDtypeStruct((rows_here,...  9.13 us
    dot_general x3, matrix products, pt_times(): lax.dot_general(p_own, dense[side], (((0,), (0,)), ((), ())), precision=M...  6.73 us
    dot_general x3, matrix products, mm(): jnp.dot(a, b, precision=MATMUL_PRECISION, preferred_element_type=jnp.floa...  2.9 us
  transfers between devices with their start and end apart: 6, of which 3 were waited for; matrix products, arithmetic and copies ran while one was open for 12% of the time, Pallas kernels for 10%

profile of v8, /device:TPU:24, one launch (start us, length us, event | category | flops | bytes accessed | tf_op | source)
XLA Modules:
  0.0 88.5 jit_solution(7444881190194947433)
XLA Ops:
  0.0 0.8 convert_multiply_fusion
  0.8 0.1 copy.8
  0.9 0.1 broadcast_in_dim.10
  0.9 0.1 mul.27
  1.0 1.4 %broadcast_multiply_fusion = f32[12,64,320]{2,1,0:T(8,128)S(1)} fusion(f32[12,64,320]{2,1,0:T(8,128)} %param.8, f32[12,320]{1,0:T(8,128)S(1)} %mul.27), kind=kLoop, calls=%fused_computation.4 | loop fusion | flops 245760 | bytes 1981440 | tf_op jit(solution)/shard_map/mul | solution.py:73
  2.4 3.8 %collective-permute-start = (f32[12,64,320]{2,1,0:T(8,128)S(1)}, f32[12,64,320]{2,1,0:T(8,128)S(1)}, u32[]{:S(2)}, u32[]{:S(2)}) collective-permute-start(f32[12,64,320]{2,1,0:T(8,128)S(1)} %broadcast_multiply_fusion), channel_id=1, source_target_pairs={{0,1},{1,2},{2,3},{3,4},{4,5},{5,6},{6,7},{7,8},{8,9},{9,10},{10,1... | collective-permute-start | bytes 2949128 | tf_op jit(solution)/shard_map/ppermute | solution.py:14
  6.3 11.3 %collective-permute-start.1 = (f32[12,64,320]{2,1,0:T(8,128)S(1)}, f32[12,64,320]{2,1,0:T(8,128)S(1)}, u32[]{:S(2)}, u32[]{:S(2)}) collective-permute-start(f32[12,64,320]{2,1,0:T(8,128)S(1)} %broadcast_multiply_fusion), channel_id=1, source_target_pairs={{1,0},{2,1},{3,2},{4,3},{5,4},{6,5},{7,6},{8,7},{9,8},{10,9},{11,1... | collective-permute-start | bytes 2949128 | tf_op jit(solution)/shard_map/ppermute | solution.py:14
  17.6 0.5 iota_add_fusion
  18.1 0.1 iota_compare_fusion.1
  18.2 0.8 select_reduce_fusion
  19.0 0.7 sub.23.slot_ref
  19.7 9.1 %shard_map.55 = (f32[12,64,768]{2,1,0:T(8,128)}, f32[12,64,768]{2,1,0:T(8,128)}, f32[12,64,768]{2,1,0:T(8,128)}) custom-call(s32[432]{0:T(512)} %sub.23.slot_ref, f32[12,64,896]{2,1,0:T(8,128)} %a_ref.1), custom_call_target="tpu_custom_call" | custom-call | tf_op jit(solution)/shard_map/pallas_call | solution.py:50
  28.8 3.3 %convolution_bitcast_fusion.1 = f32[320,768]{1,0:T(8,128)S(1)} fusion(f32[12,64,320]{2,1,0:T(8,128)S(1)} %broadcast_multiply_fusion, f32[12,64,768]{2,1,0:T(8,128)} %get-tuple-element.9), kind=kOutput, calls=%fused_computation.1 | convolution fusion | flops 1132462080 | bytes 4325376 | tf_op jit(solution)/shard_map/dot_general | solution.py:89
  32.1 1.0 %fusion.3 = f32[320,320]{1,0:T(8,128)S(1)} fusion(f32[320,768]{1,0:T(8,128)S(1)} %convolution_bitcast_fusion.1, f32[768,320]{1,0:T(8,128)S(1)} %bitcast.23), kind=kOutput, calls=%fused_computation.17 | convolution fusion | flops 471859200 | bytes 2375680 | tf_op jit(solution)/shard_map/dot_general | solution.py:18
  33.0 0.7 copy-done.3
  33.7 1.7 %convolution_bitcast_fusion.2 = f32[320,768]{1,0:T(8,128)S(1)} fusion(f32[12,64,320]{2,1,0:T(8,128)S(1)} %broadcast_multiply_fusion, f32[12,64,768]{2,1,0:T(8,128)S(1)} %copy-done.3), kind=kOutput, calls=%fused_computation.2 | convolution fusion | flops 1132462080 | bytes 4325376 | tf_op jit(solution)/shard_map/dot_general | solution.py:89
  35.5 1.7 %convolution_bitcast_fusion = f32[320,768]{1,0:T(8,128)S(1)} fusion(f32[12,64,320]{2,1,0:T(8,128)S(1)} %broadcast_multiply_fusion, f32[12,64,768]{2,1,0:T(8,128)S(1)} %copy-done.2), kind=kOutput, calls=%fused_computation | convolution fusion | flops 1132462080 | bytes 4325376 | tf_op jit(solution)/shard_map/dot_general | solution.py:89
  37.2 1.1 %collective-permute-done = f32[12,64,320]{2,1,0:T(8,128)S(1)} collective-permute-done((f32[12,64,320]{2,1,0:T(8,128)S(1)}, f32[12,64,320]{2,1,0:T(8,128)S(1)}, u32[]{:S(2)}, u32[]{:S(2)}) %collective-permute-start) | collective-permute-done | bytes 983072 | tf_op jit(solution)/shard_map/ppermute | solution.py:14
  38.3 1.0 %fusion.2 = f32[320,320]{1,0:T(8,128)S(1)} fusion(f32[320,768]{1,0:T(8,128)S(1)} %convolution_bitcast_fusion.2, f32[768,320]{1,0:T(8,128)S(1)} %bitcast.25), kind=kOutput, calls=%fused_computation.16 | convolution fusion | flops 471859200 | bytes 2375680 | tf_op jit(solution)/shard_map/dot_general | solution.py:18
  39.3 20.9 %collective-permute-done.1 = f32[12,64,320]{2,1,0:T(8,128)S(1)} collective-permute-done((f32[12,64,320]{2,1,0:T(8,128)S(1)}, f32[12,64,320]{2,1,0:T(8,128)S(1)}, u32[]{:S(2)}, u32[]{:S(2)}) %collective-permute-start.1) | collective-permute-done | bytes 983072 | tf_op jit(solution)/shard_map/ppermute | solution.py:14
  60.2 1.0 %fusion.4 = f32[320,320]{1,0:T(8,128)S(1)} fusion(f32[320,768]{1,0:T(8,128)S(1)} %convolution_bitcast_fusion, f32[768,320]{1,0:T(8,128)S(1)} %bitcast.24), kind=kOutput, calls=%fused_computation.18 | convolution fusion | flops 471859200 | bytes 2375680 | tf_op jit(solution)/shard_map/dot_general | solution.py:18
  61.2 0.2 pad_add_fusion
  61.4 0.1 fusion.1
  61.5 1.9 %collective-permute-start.2 = (f32[64,448]{1,0:T(8,128)S(1)}, f32[64,448]{1,0:T(8,128)S(1)}, u32[]{:S(2)}, u32[]{:S(2)}) collective-permute-start(f32[64,448]{1,0:T(8,128)S(1)} %get-tuple-element.15), channel_id=1, source_target_pairs={{2,0},{3,1},{4,2},{5,3},{6,4},{7,5},{8,6},{9,7},{10,8},{11,9},{12,... | collective-permute-start | bytes 344072 | tf_op jit(solution)/shard_map/ppermute | solution.py:14
  63.4 1.9 %collective-permute-start.3 = (f32[64,448]{1,0:T(8,128)S(1)}, f32[64,448]{1,0:T(8,128)S(1)}, u32[]{:S(2)}, u32[]{:S(2)}) collective-permute-start(f32[64,448]{1,0:T(8,128)S(1)} %get-tuple-element.14), channel_id=1, source_target_pairs={{1,0},{2,1},{3,2},{4,3},{5,4},{6,5},{7,6},{8,7},{9,8},{10,9},{11,1... | collective-permute-start | bytes 344072 | tf_op jit(solution)/shard_map/ppermute | solution.py:14
  65.3 4.8 %collective-permute-start.4 = (f32[64,448]{1,0:T(8,128)S(1)}, f32[64,448]{1,0:T(8,128)S(1)}, u32[]{:S(2)}, u32[]{:S(2)}) collective-permute-start(f32[64,448]{1,0:T(8,128)S(1)} %get-tuple-element.13), channel_id=1, source_target_pairs={{0,2},{1,3},{2,4},{3,5},{4,6},{5,7},{6,8},{7,9},{8,10},{9,11},{10,... | collective-permute-start | bytes 344072 | tf_op jit(solution)/shard_map/ppermute | solution.py:14
  70.2 3.9 %collective-permute-start.5 = (f32[64,448]{1,0:T(8,128)S(1)}, f32[64,448]{1,0:T(8,128)S(1)}, u32[]{:S(2)}, u32[]{:S(2)}) collective-permute-start(f32[64,448]{1,0:T(8,128)S(1)} %get-tuple-element.12), channel_id=1, source_target_pairs={{0,1},{1,2},{2,3},{3,4},{4,5},{5,6},{6,7},{7,8},{8,9},{9,10},{10,1... | collective-permute-start | bytes 344072 | tf_op jit(solution)/shard_map/ppermute | solution.py:14
  74.1 0.0 collective-permute-done.2
  74.1 0.0 collective-permute-done.3
  74.1 13.5 %collective-permute-done.4 = f32[64,448]{1,0:T(8,128)S(1)} collective-permute-done((f32[64,448]{1,0:T(8,128)S(1)}, f32[64,448]{1,0:T(8,128)S(1)}, u32[]{:S(2)}, u32[]{:S(2)}) %collective-permute-start.4) | collective-permute-done | bytes 114720 | tf_op jit(solution)/shard_map/ppermute | solution.py:14
  87.6 0.0 collective-permute-done.5
  87.6 0.8 add_bitcast_fusion
  (10 shorter events, 0.0 us)
Async XLA Ops:
  1.0 17.1 %copy-start.1 = (s32[12]{0:T(128)S(1)}, s32[12]{0:T(128)}, u32[]{:S(2)}) copy-start(s32[12]{0:T(128)} %param.7) | copy-start | bytes 148
  1.0 17.2 %copy-start = (s32[12,14]{1,0:T(8,128)S(1)}, s32[12,14]{1,0:T(8,128)}, u32[]{:S(2)}) copy-start(s32[12,14]{1,0:T(8,128)} %param.6) | copy-start | bytes 2020
  2.4 35.9 %collective-permute-start = (f32[12,64,320]{2,1,0:T(8,128)S(1)}, f32[12,64,320]{2,1,0:T(8,128)S(1)}, u32[]{:S(2)}, u32[]{:S(2)}) collective-permute-start(f32[12,64,320]{2,1,0:T(8,128)S(1)} %broadcast_multiply_fusion), channel_id=1, source_target_pairs={{0,1},{1,2},{2,3},{3,4},{4,5},{5,6},{6,7},{7,8},{8,9},{9,10},{10,1... | collective-permute-start | bytes 2949128 | tf_op jit(solution)/shard_map/ppermute | solution.py:14
  6.3 53.9 %collective-permute-start.1 = (f32[12,64,320]{2,1,0:T(8,128)S(1)}, f32[12,64,320]{2,1,0:T(8,128)S(1)}, u32[]{:S(2)}, u32[]{:S(2)}) collective-permute-start(f32[12,64,320]{2,1,0:T(8,128)S(1)} %broadcast_multiply_fusion), channel_id=1, source_target_pairs={{1,0},{2,1},{3,2},{4,3},{5,4},{6,5},{7,6},{8,7},{9,8},{10,9},{11,1... | collective-permute-start | bytes 2949128 | tf_op jit(solution)/shard_map/ppermute | solution.py:14
  32.1 1.7 %copy-start.3 = (f32[12,64,768]{2,1,0:T(8,128)S(1)}, f32[12,64,768]{2,1,0:T(8,128)}, u32[]{:S(2)}) copy-start(f32[12,64,768]{2,1,0:T(8,128)} %get-tuple-element.8) | copy-start | bytes 7077892
  33.7 1.7 %copy-start.2 = (f32[12,64,768]{2,1,0:T(8,128)S(1)}, f32[12,64,768]{2,1,0:T(8,128)}, u32[]{:S(2)}) copy-start(f32[12,64,768]{2,1,0:T(8,128)} %get-tuple-element.10) | copy-start | bytes 7077892
  61.5 12.6 %collective-permute-start.2 = (f32[64,448]{1,0:T(8,128)S(1)}, f32[64,448]{1,0:T(8,128)S(1)}, u32[]{:S(2)}, u32[]{:S(2)}) collective-permute-start(f32[64,448]{1,0:T(8,128)S(1)} %get-tuple-element.15), channel_id=1, source_target_pairs={{2,0},{3,1},{4,2},{5,3},{6,4},{7,5},{8,6},{9,7},{10,8},{11,9},{12,... | collective-permute-start | bytes 344072 | tf_op jit(solution)/shard_map/ppermute | solution.py:14
  63.4 10.7 %collective-permute-start.3 = (f32[64,448]{1,0:T(8,128)S(1)}, f32[64,448]{1,0:T(8,128)S(1)}, u32[]{:S(2)}, u32[]{:S(2)}) collective-permute-start(f32[64,448]{1,0:T(8,128)S(1)} %get-tuple-element.14), channel_id=1, source_target_pairs={{1,0},{2,1},{3,2},{4,3},{5,4},{6,5},{7,6},{8,7},{9,8},{10,9},{11,1... | collective-permute-start | bytes 344072 | tf_op jit(solution)/shard_map/ppermute | solution.py:14
  65.3 22.3 %collective-permute-start.4 = (f32[64,448]{1,0:T(8,128)S(1)}, f32[64,448]{1,0:T(8,128)S(1)}, u32[]{:S(2)}, u32[]{:S(2)}) collective-permute-start(f32[64,448]{1,0:T(8,128)S(1)} %get-tuple-element.13), channel_id=1, source_target_pairs={{0,2},{1,3},{2,4},{3,5},{4,6},{5,7},{6,8},{7,9},{8,10},{9,11},{10,... | collective-permute-start | bytes 344072 | tf_op jit(solution)/shard_map/ppermute | solution.py:14
  70.2 17.5 %collective-permute-start.5 = (f32[64,448]{1,0:T(8,128)S(1)}, f32[64,448]{1,0:T(8,128)S(1)}, u32[]{:S(2)}, u32[]{:S(2)}) collective-permute-start(f32[64,448]{1,0:T(8,128)S(1)} %get-tuple-element.12), channel_id=1, source_target_pairs={{0,1},{1,2},{2,3},{3,4},{4,5},{5,6},{6,7},{7,8},{8,9},{9,10},{10,1... | collective-permute-start | bytes 344072 | tf_op jit(solution)/shard_map/ppermute | solution.py:14

commit v9 on v8

--- a/solution.py
+++ b/solution.py
@@ -95,22 +95,25 @@
         )
 
     t_own = mm(pt_times(1), p_own)
-    t_low = mm(pt_times(0), lower_rows.reshape(span, width))
     t_high = mm(pt_times(2), upper_rows.reshape(span, width))
-    terms = (
-        jnp.pad(t_low, ((0, 0), (0, 2 * block_size)))
-        + jnp.pad(t_own, ((0, 0), (block_size, block_size)))
+    early = (
+        jnp.pad(t_own, ((0, 0), (block_size, block_size)))
         + jnp.pad(t_high, ((0, 0), (2 * block_size, 0)))
     ).reshape(prol_slots, block_size, (prol_slots + 2) * block_size)
+    sent = [from_behind(early[s], flat_axis, s - 2) for s in (3, 4, 1, 0)]
+    lower_rows, sent, early = lax.optimization_barrier((lower_rows, sent, early))
+    late = mm(pt_times(0), lower_rows.reshape(span, width)).reshape(prol_slots, block_size, width)
 
     def spread(s, block):
-        return jnp.pad(block, ((0, 0), ((prol_slots - 1 - s) * block_size, s * block_size)))
+        left = (prol_slots - 1 - s) * block_size
+        right = (prol_slots + 6) * block_size - left - block.shape[1]
+        return jnp.pad(block, ((0, 0), (left, right)))
 
-    result = spread(2, terms[2])
-    result = result + spread(0, from_behind(terms[0], flat_axis, -2))
-    result = result + spread(1, from_behind(terms[1], flat_axis, -1))
-    result = result + spread(4, from_behind(terms[4], flat_axis, 2))
-    result = result + spread(3, from_behind(terms[3], flat_axis, 1))
+    result = spread(2, early[2]) + spread(2, late[2])
+    for s, arrived in zip((3, 4, 1, 0), sent):
+        result = result + spread(s, arrived)
+    for s in (3, 4, 1, 0):
+        result = result + spread(s, from_behind(late[s], flat_axis, s - 2))
     return result.reshape(1, block_size, (prol_slots + 6) * block_size)
 
 

time: 88.9 us -> 102 us (1.15)
  the two profiles are of different devices: /device:TPU:24 before, /device:TPU:1 now
where the time goes in v9:
time: 102 us; the launch traced here: 100 us
  starting transfers between devices  44.8 us (44%)
  waiting for transfers between devices  29.8 us (29%)
  matrix products  9.79 us (10%)
  Pallas kernels  9.16 us (9%)
  other arithmetic  4.89 us (5%)
  local copies, waits for them, and re-layouts  1.65 us (2%)
    ppermute x10, starting transfers between devices, from_behind(): return lax.ppermute(array, axis, pairs)  44.8 us
    ppermute x10, waiting for transfers between devices, from_behind(): return lax.ppermute(array, axis, pairs)  29.8 us
    pallas_call x1, Pallas kernels, dense_sides(): pl.pallas_call(dense_kernel, out_shape=[jax.ShapeDtypeStruct((rows_here,...  9.16 us
    dot_general x3, matrix products, pt_times(): lax.dot_general(p_own, dense[side], (((0,), (0,)), ((), ())), precision=M...  6.89 us
    dot_general x3, matrix products, mm(): jnp.dot(a, b, precision=MATMUL_PRECISION, preferred_element_type=jnp.floa...  2.9 us
  transfers between devices with their start and end apart: 10, of which 6 were waited for; matrix products, arithmetic and copies ran while one was open for 11% of the time, Pallas kernels for 9%

profile of v9, /device:TPU:1, one launch (start us, length us, event | category | flops | bytes accessed | tf_op | source)
XLA Modules:
  0.0 100.4 jit_solution(12371387297047662125)
XLA Ops:
  0.0 0.8 convert_multiply_fusion
  1.0 1.4 %broadcast_multiply_fusion = f32[12,64,320]{2,1,0:T(8,128)S(1)} fusion(f32[12,64,320]{2,1,0:T(8,128)} %param.8, f32[12,320]{1,0:T(8,128)S(1)} %mul.27), kind=kLoop, calls=%fused_computation.12 | loop fusion | flops 245760 | bytes 1981440 | tf_op jit(solution)/shard_map/mul | solution.py:73
  2.4 9.8 %collective-permute-start.1 = (f32[12,64,320]{2,1,0:T(8,128)S(1)}, f32[12,64,320]{2,1,0:T(8,128)S(1)}, u32[]{:S(2)}, u32[]{:S(2)}) collective-permute-start(f32[12,64,320]{2,1,0:T(8,128)S(1)} %broadcast_multiply_fusion), channel_id=1, source_target_pairs={{1,0},{2,1},{3,2},{4,3},{5,4},{6,5},{7,6},{8,7},{9,8},{10,9},{11,1... | collective-permute-start | bytes 2949128 | tf_op jit(solution)/shard_map/ppermute | solution.py:14
  12.3 1.9 %collective-permute-start = (f32[12,64,320]{2,1,0:T(8,128)S(1)}, f32[12,64,320]{2,1,0:T(8,128)S(1)}, u32[]{:S(2)}, u32[]{:S(2)}) collective-permute-start(f32[12,64,320]{2,1,0:T(8,128)S(1)} %broadcast_multiply_fusion), channel_id=1, source_target_pairs={{0,1},{1,2},{2,3},{3,4},{4,5},{5,6},{6,7},{7,8},{8,9},{9,10},{10,1... | collective-permute-start | bytes 2949128 | tf_op jit(solution)/shard_map/ppermute | solution.py:14
  14.2 0.5 iota_add_fusion
  14.8 0.8 select_reduce_fusion
  15.6 0.7 sub.23.slot_ref
  16.3 9.2 %shard_map.55 = (f32[12,64,768]{2,1,0:T(8,128)}, f32[12,64,768]{2,1,0:T(8,128)}, f32[12,64,768]{2,1,0:T(8,128)}) custom-call(s32[432]{0:T(512)} %sub.23.slot_ref, f32[12,64,896]{2,1,0:T(8,128)} %a_ref.1), custom_call_target="tpu_custom_call" | custom-call | tf_op jit(solution)/shard_map/pallas_call | solution.py:50
  25.4 3.4 %convolution_bitcast_fusion.1 = f32[320,768]{1,0:T(8,128)S(1)} fusion(f32[12,64,320]{2,1,0:T(8,128)S(1)} %broadcast_multiply_fusion, f32[12,64,768]{2,1,0:T(8,128)} %get-tuple-element.15), kind=kOutput, calls=%fused_computation.1 | convolution fusion | flops 1132462080 | bytes 4325376 | tf_op jit(solution)/shard_map/dot_general | solution.py:89
  28.9 1.7 %convolution_bitcast_fusion.2 = f32[320,768]{1,0:T(8,128)S(1)} fusion(f32[12,64,320]{2,1,0:T(8,128)S(1)} %broadcast_multiply_fusion, f32[12,64,768]{2,1,0:T(8,128)S(1)} %copy-done.3), kind=kOutput, calls=%fused_computation.2 | convolution fusion | flops 1132462080 | bytes 4325376 | tf_op jit(solution)/shard_map/dot_general | solution.py:89
  30.6 1.0 fusion.6
  31.6 0.7 copy-done.2
  32.3 1.7 %convolution_bitcast_fusion = f32[320,768]{1,0:T(8,128)S(1)} fusion(f32[12,64,320]{2,1,0:T(8,128)S(1)} %broadcast_multiply_fusion, f32[12,64,768]{2,1,0:T(8,128)S(1)} %copy-done.2), kind=kOutput, calls=%fused_computation | convolution fusion | flops 1132462080 | bytes 4325376 | tf_op jit(solution)/shard_map/dot_general | solution.py:89
  34.0 1.7 %collective-permute-done.1 = f32[12,64,320]{2,1,0:T(8,128)S(1)} collective-permute-done((f32[12,64,320]{2,1,0:T(8,128)S(1)}, f32[12,64,320]{2,1,0:T(8,128)S(1)}, u32[]{:S(2)}, u32[]{:S(2)}) %collective-permute-start.1) | collective-permute-done | bytes 983072 | tf_op jit(solution)/shard_map/ppermute | solution.py:14
  35.8 1.0 fusion.7
  36.7 0.2 fusion.3
  36.9 1.9 %collective-permute-start.2 = (f32[64,448]{1,0:T(8,128)S(1)}, f32[64,448]{1,0:T(8,128)S(1)}, u32[]{:S(2)}, u32[]{:S(2)}) collective-permute-start(f32[64,448]{1,0:T(8,128)S(1)} %get-tuple-element.24), channel_id=1, source_target_pairs={{0,1},{1,2},{2,3},{3,4},{4,5},{5,6},{6,7},{7,8},{8,9},{9,10},{10,1... | collective-permute-start | bytes 344072 | tf_op jit(solution)/shard_map/ppermute | solution.py:14
  38.9 5.6 %collective-permute-start.3 = (f32[64,448]{1,0:T(8,128)S(1)}, f32[64,448]{1,0:T(8,128)S(1)}, u32[]{:S(2)}, u32[]{:S(2)}) collective-permute-start(f32[64,448]{1,0:T(8,128)S(1)} %get-tuple-element.25), channel_id=1, source_target_pairs={{0,2},{1,3},{2,4},{3,5},{4,6},{5,7},{6,8},{7,9},{8,10},{9,11},{10,... | collective-permute-start | bytes 344072 | tf_op jit(solution)/shard_map/ppermute | solution.py:14
  44.5 6.3 %collective-permute-start.4 = (f32[64,448]{1,0:T(8,128)S(1)}, f32[64,448]{1,0:T(8,128)S(1)}, u32[]{:S(2)}, u32[]{:S(2)}) collective-permute-start(f32[64,448]{1,0:T(8,128)S(1)} %get-tuple-element.26), channel_id=1, source_target_pairs={{1,0},{2,1},{3,2},{4,3},{5,4},{6,5},{7,6},{8,7},{9,8},{10,9},{11,1... | collective-permute-start | bytes 344072 | tf_op jit(solution)/shard_map/ppermute | solution.py:14
  50.8 3.9 %collective-permute-start.5 = (f32[64,448]{1,0:T(8,128)S(1)}, f32[64,448]{1,0:T(8,128)S(1)}, u32[]{:S(2)}, u32[]{:S(2)}) collective-permute-start(f32[64,448]{1,0:T(8,128)S(1)} %get-tuple-element.23), channel_id=1, source_target_pairs={{2,0},{3,1},{4,2},{5,3},{6,4},{7,5},{8,6},{9,7},{10,8},{11,9},{12,... | collective-permute-start | bytes 344072 | tf_op jit(solution)/shard_map/ppermute | solution.py:14
  54.7 0.2 pad_add_fusion
  55.0 0.7 collective-permute-done.2
  55.7 1.4 %collective-permute-done.3 = f32[64,448]{1,0:T(8,128)S(1)} collective-permute-done((f32[64,448]{1,0:T(8,128)S(1)}, f32[64,448]{1,0:T(8,128)S(1)}, u32[]{:S(2)}, u32[]{:S(2)}) %collective-permute-start.3) | collective-permute-done | bytes 114720 | tf_op jit(solution)/shard_map/ppermute | solution.py:14
  57.2 12.0 %collective-permute-done.4 = f32[64,448]{1,0:T(8,128)S(1)} collective-permute-done((f32[64,448]{1,0:T(8,128)S(1)}, f32[64,448]{1,0:T(8,128)S(1)}, u32[]{:S(2)}, u32[]{:S(2)}) %collective-permute-start.4) | collective-permute-done | bytes 114720 | tf_op jit(solution)/shard_map/ppermute | solution.py:14
  69.1 9.0 %collective-permute-done.5 = f32[64,448]{1,0:T(8,128)S(1)} collective-permute-done((f32[64,448]{1,0:T(8,128)S(1)}, f32[64,448]{1,0:T(8,128)S(1)}, u32[]{:S(2)}, u32[]{:S(2)}) %collective-permute-start.5) | collective-permute-done | bytes 114720 | tf_op jit(solution)/shard_map/ppermute | solution.py:14
  78.1 1.0 fusion.8
  79.1 1.9 %collective-permute-start.6 = (f32[64,320]{1,0:T(8,128)S(1)}, f32[64,320]{1,0:T(8,128)S(1)}, u32[]{:S(2)}, u32[]{:S(2)}) collective-permute-start(f32[64,320]{1,0:T(8,128)S(1)} %get-tuple-element.31), channel_id=1, source_target_pairs={{0,1},{1,2},{2,3},{3,4},{4,5},{5,6},{6,7},{7,8},{8,9},{9,10},{10,1... | collective-permute-start | bytes 245768 | tf_op jit(solution)/shard_map/ppermute | solution.py:14
  81.1 5.7 %collective-permute-start.7 = (f32[64,320]{1,0:T(8,128)S(1)}, f32[64,320]{1,0:T(8,128)S(1)}, u32[]{:S(2)}, u32[]{:S(2)}) collective-permute-start(f32[64,320]{1,0:T(8,128)S(1)} %get-tuple-element.30), channel_id=1, source_target_pairs={{0,2},{1,3},{2,4},{3,5},{4,6},{5,7},{6,8},{7,9},{8,10},{9,11},{10,... | collective-permute-start | bytes 245768 | tf_op jit(solution)/shard_map/ppermute | solution.py:14
  86.7 3.8 %collective-permute-start.8 = (f32[64,320]{1,0:T(8,128)S(1)}, f32[64,320]{1,0:T(8,128)S(1)}, u32[]{:S(2)}, u32[]{:S(2)}) collective-permute-start(f32[64,320]{1,0:T(8,128)S(1)} %get-tuple-element.29), channel_id=1, source_target_pairs={{1,0},{2,1},{3,2},{4,3},{5,4},{6,5},{7,6},{8,7},{9,8},{10,9},{11,1... | collective-permute-start | bytes 245768 | tf_op jit(solution)/shard_map/ppermute | solution.py:14
  90.5 3.9 %collective-permute-start.9 = (f32[64,320]{1,0:T(8,128)S(1)}, f32[64,320]{1,0:T(8,128)S(1)}, u32[]{:S(2)}, u32[]{:S(2)}) collective-permute-start(f32[64,320]{1,0:T(8,128)S(1)} %get-tuple-element.28), channel_id=1, source_target_pairs={{2,0},{3,1},{4,2},{5,3},{6,4},{7,5},{8,6},{9,7},{10,8},{11,9},{12,... | collective-permute-start | bytes 245768 | tf_op jit(solution)/shard_map/ppermute | solution.py:14
  94.5 5.0 %collective-permute-done.9 = f32[64,320]{1,0:T(8,128)S(1)} collective-permute-done((f32[64,320]{1,0:T(8,128)S(1)}, f32[64,320]{1,0:T(8,128)S(1)}, u32[]{:S(2)}, u32[]{:S(2)}) %collective-permute-start.9) | collective-permute-done | bytes 81952 | tf_op jit(solution)/shard_map/ppermute | solution.py:14
  99.5 0.9 add_bitcast_fusion
  (20 shorter events, 0.4 us)
Async XLA Ops:
  1.0 13.7 %copy-start.1 = (s32[12]{0:T(128)S(1)}, s32[12]{0:T(128)}, u32[]{:S(2)}) copy-start(s32[12]{0:T(128)} %param.7) | copy-start | bytes 148
  1.0 13.8 %copy-start = (s32[12,14]{1,0:T(8,128)S(1)}, s32[12,14]{1,0:T(8,128)}, u32[]{:S(2)}) copy-start(s32[12,14]{1,0:T(8,128)} %param.6) | copy-start | bytes 2020
  2.4 33.3 %collective-permute-start.1 = (f32[12,64,320]{2,1,0:T(8,128)S(1)}, f32[12,64,320]{2,1,0:T(8,128)S(1)}, u32[]{:S(2)}, u32[]{:S(2)}) collective-permute-start(f32[12,64,320]{2,1,0:T(8,128)S(1)} %broadcast_multiply_fusion), channel_id=1, source_target_pairs={{1,0},{2,1},{3,2},{4,3},{5,4},{6,5},{7,6},{8,7},{9,8},{10,9},{11,1... | collective-permute-start | bytes 2949128 | tf_op jit(solution)/shard_map/ppermute | solution.py:14
  12.3 42.7 %collective-permute-start = (f32[12,64,320]{2,1,0:T(8,128)S(1)}, f32[12,64,320]{2,1,0:T(8,128)S(1)}, u32[]{:S(2)}, u32[]{:S(2)}) collective-permute-start(f32[12,64,320]{2,1,0:T(8,128)S(1)} %broadcast_multiply_fusion), channel_id=1, source_target_pairs={{0,1},{1,2},{2,3},{3,4},{4,5},{5,6},{6,7},{7,8},{8,9},{9,10},{10,1... | collective-permute-start | bytes 2949128 | tf_op jit(solution)/shard_map/ppermute | solution.py:14
  25.4 3.4 %copy-start.3 = (f32[12,64,768]{2,1,0:T(8,128)S(1)}, f32[12,64,768]{2,1,0:T(8,128)}, u32[]{:S(2)}) copy-start(f32[12,64,768]{2,1,0:T(8,128)} %get-tuple-element.14) | copy-start | bytes 7077892
  30.6 1.7 %copy-start.2 = (f32[12,64,768]{2,1,0:T(8,128)S(1)}, f32[12,64,768]{2,1,0:T(8,128)}, u32[]{:S(2)}) copy-start(f32[12,64,768]{2,1,0:T(8,128)} %get-tuple-element.17) | copy-start | bytes 7077892
  36.9 18.8 %collective-permute-start.2 = (f32[64,448]{1,0:T(8,128)S(1)}, f32[64,448]{1,0:T(8,128)S(1)}, u32[]{:S(2)}, u32[]{:S(2)}) collective-permute-start(f32[64,448]{1,0:T(8,128)S(1)} %get-tuple-element.24), channel_id=1, source_target_pairs={{0,1},{1,2},{2,3},{3,4},{4,5},{5,6},{6,7},{7,8},{8,9},{9,10},{10,1... | collective-permute-start | bytes 344072 | tf_op jit(solution)/shard_map/ppermute | solution.py:14
  38.9 18.3 %collective-permute-start.3 = (f32[64,448]{1,0:T(8,128)S(1)}, f32[64,448]{1,0:T(8,128)S(1)}, u32[]{:S(2)}, u32[]{:S(2)}) collective-permute-start(f32[64,448]{1,0:T(8,128)S(1)} %get-tuple-element.25), channel_id=1, source_target_pairs={{0,2},{1,3},{2,4},{3,5},{4,6},{5,7},{6,8},{7,9},{8,10},{9,11},{10,... | collective-permute-start | bytes 344072 | tf_op jit(solution)/shard_map/ppermute | solution.py:14
  44.5 24.7 %collective-permute-start.4 = (f32[64,448]{1,0:T(8,128)S(1)}, f32[64,448]{1,0:T(8,128)S(1)}, u32[]{:S(2)}, u32[]{:S(2)}) collective-permute-start(f32[64,448]{1,0:T(8,128)S(1)} %get-tuple-element.26), channel_id=1, source_target_pairs={{1,0},{2,1},{3,2},{4,3},{5,4},{6,5},{7,6},{8,7},{9,8},{10,9},{11,1... | collective-permute-start | bytes 344072 | tf_op jit(solution)/shard_map/ppermute | solution.py:14
  50.8 27.3 %collective-permute-start.5 = (f32[64,448]{1,0:T(8,128)S(1)}, f32[64,448]{1,0:T(8,128)S(1)}, u32[]{:S(2)}, u32[]{:S(2)}) collective-permute-start(f32[64,448]{1,0:T(8,128)S(1)} %get-tuple-element.23), channel_id=1, source_target_pairs={{2,0},{3,1},{4,2},{5,3},{6,4},{7,5},{8,6},{9,7},{10,8},{11,9},{12,... | collective-permute-start | bytes 344072 | tf_op jit(solution)/shard_map/ppermute | solution.py:14
  79.1 15.4 %collective-permute-start.6 = (f32[64,320]{1,0:T(8,128)S(1)}, f32[64,320]{1,0:T(8,128)S(1)}, u32[]{:S(2)}, u32[]{:S(2)}) collective-permute-start(f32[64,320]{1,0:T(8,128)S(1)} %get-tuple-element.31), channel_id=1, source_target_pairs={{0,1},{1,2},{2,3},{3,4},{4,5},{5,6},{6,7},{7,8},{8,9},{9,10},{10,1... | collective-permute-start | bytes 245768 | tf_op jit(solution)/shard_map/ppermute | solution.py:14
  81.1 13.4 %collective-permute-start.7 = (f32[64,320]{1,0:T(8,128)S(1)}, f32[64,320]{1,0:T(8,128)S(1)}, u32[]{:S(2)}, u32[]{:S(2)}) collective-permute-start(f32[64,320]{1,0:T(8,128)S(1)} %get-tuple-element.30), channel_id=1, source_target_pairs={{0,2},{1,3},{2,4},{3,5},{4,6},{5,7},{6,8},{7,9},{8,10},{9,11},{10,... | collective-permute-start | bytes 245768 | tf_op jit(solution)/shard_map/ppermute | solution.py:14
  86.7 7.8 %collective-permute-start.8 = (f32[64,320]{1,0:T(8,128)S(1)}, f32[64,320]{1,0:T(8,128)S(1)}, u32[]{:S(2)}, u32[]{:S(2)}) collective-permute-start(f32[64,320]{1,0:T(8,128)S(1)} %get-tuple-element.29), channel_id=1, source_target_pairs={{1,0},{2,1},{3,2},{4,3},{5,4},{6,5},{7,6},{8,7},{9,8},{10,9},{11,1... | collective-permute-start | bytes 245768 | tf_op jit(solution)/shard_map/ppermute | solution.py:14
  90.5 8.9 %collective-permute-start.9 = (f32[64,320]{1,0:T(8,128)S(1)}, f32[64,320]{1,0:T(8,128)S(1)}, u32[]{:S(2)}, u32[]{:S(2)}) collective-permute-start(f32[64,320]{1,0:T(8,128)S(1)} %get-tuple-element.28), channel_id=1, source_target_pairs={{2,0},{3,1},{4,2},{5,3},{6,4},{7,5},{8,6},{9,7},{10,8},{11,9},{12,... | collective-permute-start | bytes 245768 | tf_op jit(solution)/shard_map/ppermute | solution.py:14

commit v10 on v6

--- a/solution.py
+++ b/solution.py
@@ -58,7 +58,7 @@
     )(slot_table, a_vals)
 
 
-def exchange_kernel(terms_ref, out_ref, recv, send_sem, recv_sem):
+def exchange_kernel(terms_ref, out_ref, recv, acc, padded, send_sem, recv_sem):
     col_count = lax.axis_size("cols")
     total = lax.axis_size("rows") * col_count
     me = lax.axis_index("rows") * col_count + lax.axis_index("cols")
@@ -97,6 +97,21 @@
         def _():
             copy.start()
 
+    block_size = terms_ref.shape[1]
+    lanes = 2 * block_size
+    acc[...] = jnp.zeros(acc.shape, acc.dtype)
+
+    def place(part_ref, offset):
+        wide = part_ref.shape[-1]
+        if offset % lanes == 0:
+            acc[:, offset : offset + wide] += part_ref[...]
+        else:
+            padded[...] = jnp.zeros(padded.shape, padded.dtype)
+            padded[:, :wide] = part_ref[...]
+            base = offset - block_size
+            acc[:, base : base + padded.shape[1]] += pltpu.roll(padded[...], block_size, 1)
+
+    place(terms_ref.at[centre], centre * block_size)
     for u, shift in enumerate(shifts):
         sends = (me + shift >= 0) & (me + shift < total)
         gets = (me - shift >= 0) & (me - shift < total)
@@ -108,22 +123,24 @@
         @pl.when(gets)
         def _():
             copies[u].wait_recv()
-            out_ref[u] = recv[u]
-
-        @pl.when(jnp.logical_not(gets))
-        def _():
-            out_ref[u] = jnp.zeros(out_ref.shape[1:], out_ref.dtype)
+            place(recv.at[u], (centre - shift) * block_size)
+
+    out_ref[...] = acc[:, : out_ref.shape[1]]
 
 
 def exchange(terms):
     parts, block_size, wide = terms.shape
+    lanes = 2 * block_size
+    full = wide + (parts - 1) * block_size
     return pl.pallas_call(
         exchange_kernel,
-        out_shape=jax.ShapeDtypeStruct((parts - 1, block_size, wide), jnp.float32),
+        out_shape=jax.ShapeDtypeStruct((block_size, full), jnp.float32),
         in_specs=[pl.BlockSpec(memory_space=pltpu.VMEM)],
         out_specs=pl.BlockSpec(memory_space=pltpu.VMEM),
         scratch_shapes=[
             pltpu.VMEM((parts - 1, block_size, wide), jnp.float32),
+            pltpu.VMEM((block_size, -(-full // lanes) * lanes), jnp.float32),
+            pltpu.VMEM((block_size, -(-wide // lanes) * lanes), jnp.float32),
             pltpu.SemaphoreType.DMA((parts - 1,)),
             pltpu.SemaphoreType.DMA((parts - 1,)),
         ],
@@ -176,13 +193,7 @@
         + jnp.pad(t_high, ((0, 0), (2 * block_size, 0)))
     ).reshape(prol_slots, block_size, (prol_slots + 2) * block_size)
 
-    def spread(s, block):
-        return jnp.pad(block, ((0, 0), ((prol_slots - 1 - s) * block_size, s * block_size)))
-
-    arrived = exchange(terms)
-    result = spread(2, terms[2])
-    for u, s in enumerate([0, 1, 3, 4]):
-        result = result + spread(s, arrived[u])
+    result = exchange(terms)
     return result.reshape(1, block_size, (prol_slots + 6) * block_size)
 
 

time: 88.5 us -> 88.1 us (level)
    squeeze x1 -> x0, local copies, waits for them, and re-layouts: 1.13 us -> none  [shards(): result = result + spread(s, arrived[u])]
    unnamed x10 -> x9, local copies, waits for them, and re-layouts: 1.51 us -> 2.31 us
  transfers between devices with their start and end apart: 2 -> 2, of which waited for: 2 -> 2; matrix products, arithmetic and copies ran while one was open for 12% -> 12% of each run, Pallas kernels for 10% -> 11%
where the time goes in v10:
time: 88.1 us; the launch traced here: 86.8 us
  Pallas kernels  31.1 us (35%)
  waiting for transfers between devices  26.3 us (30%)
  starting transfers between devices  11.8 us (13%)
  matrix products  9.64 us (11%)
  other arithmetic  4.64 us (5%)
  local copies, waits for them, and re-layouts  3.22 us (4%)
    ppermute x2, waiting for transfers between devices, from_behind(): return lax.ppermute(array, axis, pairs)  26.3 us
    pallas_call x1, Pallas kernels, exchange(): pl.pallas_call(exchange_kernel, out_shape=jax.ShapeDtypeStruct((block_siz...  21.9 us
    ppermute x2, starting transfers between devices, from_behind(): return lax.ppermute(array, axis, pairs)  11.8 us
    pallas_call x1, Pallas kernels, dense_sides(): pl.pallas_call(dense_kernel, out_shape=[jax.ShapeDtypeStruct((rows_here,...  9.15 us
    dot_general x3, matrix products, pt_times(): lax.dot_general(p_own, dense[side], (((0,), (0,)), ((), ())), precision=M...  6.73 us
    dot_general x3, matrix products, mm(): jnp.dot(a, b, precision=MATMUL_PRECISION, preferred_element_type=jnp.floa...  2.91 us
    unnamed x9, local copies, waits for them, and re-layouts  2.31 us
  transfers between devices with their start and end apart: 2, of which 2 were waited for; matrix products, arithmetic and copies ran while one was open for 12% of the time, Pallas kernels for 11%

profile of v10, /device:TPU:1, one launch (start us, length us, event | category | flops | bytes accessed | tf_op | source)
XLA Modules:
  0.0 86.8 jit_solution(14989134552606026051)
XLA Ops:
  0.0 0.8 convert_multiply_fusion
  0.8 0.1 copy.8
  0.9 0.1 broadcast_in_dim.10
  0.9 0.1 mul.27
  1.0 0.0 copy-start.1
  1.0 0.0 copy-start
  1.0 1.4 %broadcast_multiply_fusion = f32[12,64,320]{2,1,0:T(8,128)S(1)} fusion(f32[12,64,320]{2,1,0:T(8,128)} %param.8, f32[12,320]{1,0:T(8,128)S(1)} %mul.27), kind=kLoop, calls=%fused_computation.4 | loop fusion | flops 245760 | bytes 1981440 | tf_op jit(solution)/shard_map/mul | solution.py:163
  2.4 4.4 %collective-permute-start = (f32[12,64,320]{2,1,0:T(8,128)S(1)}, f32[12,64,320]{2,1,0:T(8,128)S(1)}, u32[]{:S(2)}, u32[]{:S(2)}) collective-permute-start(f32[12,64,320]{2,1,0:T(8,128)S(1)} %broadcast_multiply_fusion), channel_id=1, source_target_pairs={{0,1},{1,2},{2,3},{3,4},{4,5},{5,6},{6,7},{7,8},{8,9},{9,10},{10,1... | collective-permute-start | bytes 2949128 | tf_op jit(solution)/shard_map/ppermute | solution.py:14
  6.8 7.4 %collective-permute-start.1 = (f32[12,64,320]{2,1,0:T(8,128)S(1)}, f32[12,64,320]{2,1,0:T(8,128)S(1)}, u32[]{:S(2)}, u32[]{:S(2)}) collective-permute-start(f32[12,64,320]{2,1,0:T(8,128)S(1)} %broadcast_multiply_fusion), channel_id=1, source_target_pairs={{1,0},{2,1},{3,2},{4,3},{5,4},{6,5},{7,6},{8,7},{9,8},{10,9},{11,1... | collective-permute-start | bytes 2949128 | tf_op jit(solution)/shard_map/ppermute | solution.py:14
  14.2 0.5 iota_add_fusion
  14.7 0.0 copy-done.1
  14.7 0.1 iota_compare_fusion.1
  14.8 0.0 copy-done
  14.8 0.8 select_reduce_fusion
  15.6 0.7 sub.23.slot_ref
  16.3 9.1 %shard_map.55 = (f32[12,64,768]{2,1,0:T(8,128)}, f32[12,64,768]{2,1,0:T(8,128)}, f32[12,64,768]{2,1,0:T(8,128)}) custom-call(s32[432]{0:T(512)} %sub.23.slot_ref, f32[12,64,896]{2,1,0:T(8,128)} %a_ref.1), custom_call_target="tpu_custom_call" | custom-call | tf_op jit(solution)/shard_map/pallas_call | solution.py:50
  25.4 3.3 %convolution_bitcast_fusion.1 = f32[320,768]{1,0:T(8,128)S(1)} fusion(f32[12,64,320]{2,1,0:T(8,128)S(1)} %broadcast_multiply_fusion, f32[12,64,768]{2,1,0:T(8,128)} %get-tuple-element.9), kind=kOutput, calls=%fused_computation.1 | convolution fusion | flops 1132462080 | bytes 4325376 | tf_op jit(solution)/shard_map/dot_general | solution.py:179
  28.7 0.0 copy-start.3
  28.7 1.0 %fusion.2 = f32[320,320]{1,0:T(8,128)S(1)} fusion(f32[320,768]{1,0:T(8,128)S(1)} %convolution_bitcast_fusion.1, f32[768,320]{1,0:T(8,128)S(1)} %bitcast.23), kind=kOutput, calls=%fused_computation.15 | convolution fusion | flops 471859200 | bytes 2375680 | tf_op jit(solution)/shard_map/dot_general | solution.py:18
  29.7 0.7 copy-done.3
  30.4 0.0 copy-start.2
  30.4 1.7 %convolution_bitcast_fusion.2 = f32[320,768]{1,0:T(8,128)S(1)} fusion(f32[12,64,320]{2,1,0:T(8,128)S(1)} %broadcast_multiply_fusion, f32[12,64,768]{2,1,0:T(8,128)S(1)} %copy-done.3), kind=kOutput, calls=%fused_computation.2 | convolution fusion | flops 1132462080 | bytes 4325376 | tf_op jit(solution)/shard_map/dot_general | solution.py:179
  32.1 0.0 copy-done.2
  32.1 1.7 %convolution_bitcast_fusion = f32[320,768]{1,0:T(8,128)S(1)} fusion(f32[12,64,320]{2,1,0:T(8,128)S(1)} %broadcast_multiply_fusion, f32[12,64,768]{2,1,0:T(8,128)S(1)} %copy-done.2), kind=kOutput, calls=%fused_computation | convolution fusion | flops 1132462080 | bytes 4325376 | tf_op jit(solution)/shard_map/dot_general | solution.py:179
  33.9 3.6 %collective-permute-done = f32[12,64,320]{2,1,0:T(8,128)S(1)} collective-permute-done((f32[12,64,320]{2,1,0:T(8,128)S(1)}, f32[12,64,320]{2,1,0:T(8,128)S(1)}, u32[]{:S(2)}, u32[]{:S(2)}) %collective-permute-start) | collective-permute-done | bytes 983072 | tf_op jit(solution)/shard_map/ppermute | solution.py:14
  37.4 1.0 %fusion.1 = f32[320,320]{1,0:T(8,128)S(1)} fusion(f32[320,768]{1,0:T(8,128)S(1)} %convolution_bitcast_fusion.2, f32[768,320]{1,0:T(8,128)S(1)} %bitcast.26), kind=kOutput, calls=%fused_computation.14 | convolution fusion | flops 471859200 | bytes 2375680 | tf_op jit(solution)/shard_map/dot_general | solution.py:18
  38.4 22.8 %collective-permute-done.1 = f32[12,64,320]{2,1,0:T(8,128)S(1)} collective-permute-done((f32[12,64,320]{2,1,0:T(8,128)S(1)}, f32[12,64,320]{2,1,0:T(8,128)S(1)}, u32[]{:S(2)}, u32[]{:S(2)}) %collective-permute-start.1) | collective-permute-done | bytes 983072 | tf_op jit(solution)/shard_map/ppermute | solution.py:14
  61.2 1.0 %fusion.3 = f32[320,320]{1,0:T(8,128)S(1)} fusion(f32[320,768]{1,0:T(8,128)S(1)} %convolution_bitcast_fusion, f32[768,320]{1,0:T(8,128)S(1)} %bitcast.25), kind=kOutput, calls=%fused_computation.16 | convolution fusion | flops 471859200 | bytes 2375680 | tf_op jit(solution)/shard_map/dot_general | solution.py:18
  62.1 1.1 %pad_add_fusion = f32[320,448]{1,0:T(8,128)} fusion(f32[320,320]{1,0:T(8,128)S(1)} %fusion.3, f32[320,320]{1,0:T(8,128)S(1)} %fusion.2, f32[320,320]{1,0:T(8,128)S(1)} %fusion.1), kind=kLoop, calls=%fused_computation.3 | loop fusion | flops 286720 | bytes 1802240 | tf_op jit(solution)/shard_map/add | solution.py:191
  63.2 21.9 %shard_map.56 = f32[64,704]{1,0:T(8,128)} custom-call(f32[5,64,448]{2,1,0:T(8,128)} %bitcast.24), custom_call_target="tpu_custom_call" | custom-call | tf_op jit(solution)/shard_map/pallas_call | solution.py:135
  85.2 1.6 %copy.10 = f32[1,64,704]{2,1,0:T(8,128)} copy(f32[1,64,704]{2,1,0:T(8,128)} %bitcast.27) | data formatting | bytes 360448
  (3 shorter events, 0.0 us)
Async XLA Ops:
  1.0 13.7 %copy-start.1 = (s32[12]{0:T(128)S(1)}, s32[12]{0:T(128)}, u32[]{:S(2)}) copy-start(s32[12]{0:T(128)} %param.7) | copy-start | bytes 148
  1.0 13.8 %copy-start = (s32[12,14]{1,0:T(8,128)S(1)}, s32[12,14]{1,0:T(8,128)}, u32[]{:S(2)}) copy-start(s32[12,14]{1,0:T(8,128)} %param.6) | copy-start | bytes 2020
  2.4 35.0 %collective-permute-start = (f32[12,64,320]{2,1,0:T(8,128)S(1)}, f32[12,64,320]{2,1,0:T(8,128)S(1)}, u32[]{:S(2)}, u32[]{:S(2)}) collective-permute-start(f32[12,64,320]{2,1,0:T(8,128)S(1)} %broadcast_multiply_fusion), channel_id=1, source_target_pairs={{0,1},{1,2},{2,3},{3,4},{4,5},{5,6},{6,7},{7,8},{8,9},{9,10},{10,1... | collective-permute-start | bytes 2949128 | tf_op jit(solution)/shard_map/ppermute | solution.py:14
  6.8 54.3 %collective-permute-start.1 = (f32[12,64,320]{2,1,0:T(8,128)S(1)}, f32[12,64,320]{2,1,0:T(8,128)S(1)}, u32[]{:S(2)}, u32[]{:S(2)}) collective-permute-start(f32[12,64,320]{2,1,0:T(8,128)S(1)} %broadcast_multiply_fusion), channel_id=1, source_target_pairs={{1,0},{2,1},{3,2},{4,3},{5,4},{6,5},{7,6},{8,7},{9,8},{10,9},{11,1... | collective-permute-start | bytes 2949128 | tf_op jit(solution)/shard_map/ppermute | solution.py:14
  28.7 1.7 %copy-start.3 = (f32[12,64,768]{2,1,0:T(8,128)S(1)}, f32[12,64,768]{2,1,0:T(8,128)}, u32[]{:S(2)}) copy-start(f32[12,64,768]{2,1,0:T(8,128)} %get-tuple-element.8) | copy-start | bytes 7077892
  30.4 1.8 %copy-start.2 = (f32[12,64,768]{2,1,0:T(8,128)S(1)}, f32[12,64,768]{2,1,0:T(8,128)}, u32[]{:S(2)}) copy-start(f32[12,64,768]{2,1,0:T(8,128)} %get-tuple-element.10) | copy-start | bytes 7077892

commit v11 on v8

--- a/solution.py
+++ b/solution.py
@@ -56,6 +56,117 @@
         ],
         out_specs=[pl.BlockSpec(memory_space=pltpu.VMEM)] * 3,
     )(slot_table, a_vals)
+
+
+def exchange_kernel(terms_ref, out_ref, land1, bufs_r, bufs_l, land_r, land_l, acc, padded, sems):
+    col_count = lax.axis_size("cols")
+    total = lax.axis_size("rows") * col_count
+    me = lax.axis_index("rows") * col_count + lax.axis_index("cols")
+    block_size = terms_ref.shape[1]
+    lanes = 2 * block_size
+    has = {1: me + 1 < total, -1: me - 1 >= 0}
+
+    def mesh_id(pos):
+        return (pos // col_count, pos % col_count)
+
+    def place(target, part, offset):
+        wide = part.shape[-1]
+        if offset % lanes == 0:
+            target[:, offset : offset + wide] += part
+        else:
+            padded[...] = jnp.zeros(padded.shape, padded.dtype)
+            padded[:, :wide] = part
+            base = offset - block_size
+            target[:, base : base + padded.shape[1]] += pltpu.roll(padded[...], block_size, 1)
+
+    barrier = pltpu.get_barrier_semaphore()
+    for shift in (1, -1):
+        @pl.when(has[shift])
+        def _():
+            pl.semaphore_signal(
+                barrier, 1, device_id=mesh_id(me + shift), device_id_type=pl.DeviceIdType.MESH
+            )
+
+    pl.semaphore_wait(barrier, has[1].astype(jnp.int32) + has[-1].astype(jnp.int32))
+
+    def remote(src, dst, k, shift):
+        return pltpu.make_async_remote_copy(
+            src_ref=src,
+            dst_ref=dst,
+            send_sem=sems.at[0, k],
+            recv_sem=sems.at[1, k],
+            device_id=mesh_id(me + shift),
+            device_id_type=pl.DeviceIdType.MESH,
+        )
+
+    first = [remote(terms_ref.at[4], land1.at[0], 0, 1), remote(terms_ref.at[0], land1.at[1], 1, -1)]
+    for copy, shift in zip(first, (1, -1)):
+        @pl.when(has[shift])
+        def _():
+            copy.start()
+
+    bufs_r[...] = jnp.zeros(bufs_r.shape, bufs_r.dtype)
+    bufs_l[...] = jnp.zeros(bufs_l.shape, bufs_l.dtype)
+    place(bufs_r, terms_ref[3], block_size)
+    place(bufs_l, terms_ref[1], block_size)
+    for copy, shift, k in zip(first, (1, -1), (0, 1)):
+        @pl.when(has[shift])
+        def _():
+            copy.wait_send()
+
+        @pl.when(has[-shift])
+        def _():
+            copy.wait_recv()
+            if k == 0:
+                place(bufs_r, land1[0], 0)
+            else:
+                place(bufs_l, land1[1], lanes)
+
+    second = [remote(bufs_r, land_r, 2, 1), remote(bufs_l, land_l, 3, -1)]
+    for copy, shift in zip(second, (1, -1)):
+        @pl.when(has[shift])
+        def _():
+            copy.start()
+
+    acc[...] = jnp.zeros(acc.shape, acc.dtype)
+    place(acc, terms_ref[2], lanes)
+    for copy, shift, k in zip(second, (1, -1), (0, 1)):
+        @pl.when(has[shift])
+        def _():
+            copy.wait_send()
+
+        @pl.when(has[-shift])
+        def _():
+            copy.wait_recv()
+            if k == 0:
+                acc[:, : land_r.shape[1]] += land_r[...]
+            else:
+                acc[:, lanes : lanes + land_l.shape[1]] += land_l[...]
+
+    out_ref[...] = acc[:, : out_ref.shape[1]]
+
+
+def exchange(terms):
+    parts, block_size, wide = terms.shape
+    lanes = 2 * block_size
+    full = wide + (parts - 1) * block_size
+    return pl.pallas_call(
+        exchange_kernel,
+        out_shape=jax.ShapeDtypeStruct((block_size, full), jnp.float32),
+        in_specs=[pl.BlockSpec(memory_space=pltpu.VMEM)],
+        out_specs=pl.BlockSpec(memory_space=pltpu.VMEM),
+        scratch_shapes=[
+            pltpu.VMEM((2, block_size, wide), jnp.float32),
+            pltpu.VMEM((block_size, wide + block_size), jnp.float32),
+            pltpu.VMEM((block_size, wide + lanes), jnp.float32),
+            pltpu.VMEM((block_size, wide + block_size), jnp.float32),
+            pltpu.VMEM((block_size, wide + lanes), jnp.float32),
+            pltpu.VMEM((block_size, -(-full // lanes) * lanes), jnp.float32),
+            pltpu.VMEM((block_size, -(-wide // lanes) * lanes), jnp.float32),
+            pltpu.SemaphoreType.DMA((2, 4)),
+        ],
+        compiler_params=pltpu.CompilerParams(collective_id=0, has_side_effects=True),
+    )(terms)
 
 
 def shards(a_vals, a_cols, a_count, p_vals, p_mask):
@@ -103,14 +214,7 @@
         + jnp.pad(t_high, ((0, 0), (2 * block_size, 0)))
     ).reshape(prol_slots, block_size, (prol_slots + 2) * block_size)
 
-    def spread(s, block):
-        return jnp.pad(block, ((0, 0), ((prol_slots - 1 - s) * block_size, s * block_size)))
-
-    result = spread(2, terms[2])
-    result = result + spread(0, from_behind(terms[0], flat_axis, -2))
-    result = result + spread(1, from_behind(terms[1], flat_axis, -1))
-    result = result + spread(4, from_behind(terms[4], flat_axis, 2))
-    result = result + spread(3, from_behind(terms[3], flat_axis, 1))
+    result = exchange(terms)
     return result.reshape(1, block_size, (prol_slots + 6) * block_size)
 
 

time: 88.9 us -> 87.5 us (0.984)
  the two profiles are of different devices: /device:TPU:24 before, /device:TPU:1 now
where the time goes in v11:
time: 87.5 us; the launch traced here: 87.1 us
  Pallas kernels  31.4 us (36%)
  waiting for transfers between devices  26.3 us (30%)
  starting transfers between devices  11.8 us (13%)
  matrix products  9.64 us (11%)
  other arithmetic  4.64 us (5%)
  local copies, waits for them, and re-layouts  3.22 us (4%)
    ppermute x2, waiting for transfers between devices, from_behind(): return lax.ppermute(array, axis, pairs)  26.3 us
    pallas_call x1, Pallas kernels, exchange(): pl.pallas_call(exchange_kernel, out_shape=jax.ShapeDtypeStruct((block_siz...  22.3 us
    ppermute x2, starting transfers between devices, from_behind(): return lax.ppermute(array, axis, pairs)  11.8 us
    pallas_call x1, Pallas kernels, dense_sides(): pl.pallas_call(dense_kernel, out_shape=[jax.ShapeDtypeStruct((rows_here,...  9.16 us
    dot_general x3, matrix products, pt_times(): lax.dot_general(p_own, dense[side], (((0,), (0,)), ((), ())), precision=M...  6.74 us
    dot_general x3, matrix products, mm(): jnp.dot(a, b, precision=MATMUL_PRECISION, preferred_element_type=jnp.floa...  2.91 us
    unnamed x9, local copies, waits for them, and re-layouts  2.31 us
  transfers between devices with their start and end apart: 2, of which 2 were waited for; matrix products, arithmetic and copies ran while one was open for 12% of the time, Pallas kernels for 11%

profile of v11, /device:TPU:1, one launch (start us, length us, event | category | flops | bytes accessed | tf_op | source)
XLA Modules:
  0.0 87.1 jit_solution(16632808540175661525)
XLA Ops:
  0.0 0.8 convert_multiply_fusion
  0.8 0.1 copy.8
  0.9 0.1 broadcast_in_dim.10
  0.9 0.1 mul.27
  1.0 0.0 copy-start.1
  1.0 0.0 copy-start
  1.0 1.4 %broadcast_multiply_fusion = f32[12,64,320]{2,1,0:T(8,128)S(1)} fusion(f32[12,64,320]{2,1,0:T(8,128)} %param.8, f32[12,320]{1,0:T(8,128)S(1)} %mul.27), kind=kLoop, calls=%fused_computation.4 | loop fusion | flops 245760 | bytes 1981440 | tf_op jit(solution)/shard_map/mul | solution.py:184
  2.4 4.4 %collective-permute-start = (f32[12,64,320]{2,1,0:T(8,128)S(1)}, f32[12,64,320]{2,1,0:T(8,128)S(1)}, u32[]{:S(2)}, u32[]{:S(2)}) collective-permute-start(f32[12,64,320]{2,1,0:T(8,128)S(1)} %broadcast_multiply_fusion), channel_id=1, source_target_pairs={{0,1},{1,2},{2,3},{3,4},{4,5},{5,6},{6,7},{7,8},{8,9},{9,10},{10,1... | collective-permute-start | bytes 2949128 | tf_op jit(solution)/shard_map/ppermute | solution.py:14
  6.8 7.4 %collective-permute-start.1 = (f32[12,64,320]{2,1,0:T(8,128)S(1)}, f32[12,64,320]{2,1,0:T(8,128)S(1)}, u32[]{:S(2)}, u32[]{:S(2)}) collective-permute-start(f32[12,64,320]{2,1,0:T(8,128)S(1)} %broadcast_multiply_fusion), channel_id=1, source_target_pairs={{1,0},{2,1},{3,2},{4,3},{5,4},{6,5},{7,6},{8,7},{9,8},{10,9},{11,1... | collective-permute-start | bytes 2949128 | tf_op jit(solution)/shard_map/ppermute | solution.py:14
  14.2 0.5 iota_add_fusion
  14.7 0.0 copy-done.1
  14.7 0.1 iota_compare_fusion.1
  14.8 0.0 copy-done
  14.8 0.8 select_reduce_fusion
  15.6 0.7 sub.23.slot_ref
  16.3 9.2 %shard_map.55 = (f32[12,64,768]{2,1,0:T(8,128)}, f32[12,64,768]{2,1,0:T(8,128)}, f32[12,64,768]{2,1,0:T(8,128)}) custom-call(s32[432]{0:T(512)} %sub.23.slot_ref, f32[12,64,896]{2,1,0:T(8,128)} %a_ref.1), custom_call_target="tpu_custom_call" | custom-call | tf_op jit(solution)/shard_map/pallas_call | solution.py:50
  25.4 3.3 %convolution_bitcast_fusion.1 = f32[320,768]{1,0:T(8,128)S(1)} fusion(f32[12,64,320]{2,1,0:T(8,128)S(1)} %broadcast_multiply_fusion, f32[12,64,768]{2,1,0:T(8,128)} %get-tuple-element.9), kind=kOutput, calls=%fused_computation.1 | convolution fusion | flops 1132462080 | bytes 4325376 | tf_op jit(solution)/shard_map/dot_general | solution.py:200
  28.7 0.0 copy-start.3
  28.7 1.0 %fusion.2 = f32[320,320]{1,0:T(8,128)S(1)} fusion(f32[320,768]{1,0:T(8,128)S(1)} %convolution_bitcast_fusion.1, f32[768,320]{1,0:T(8,128)S(1)} %bitcast.23), kind=kOutput, calls=%fused_computation.15 | convolution fusion | flops 471859200 | bytes 2375680 | tf_op jit(solution)/shard_map/dot_general | solution.py:18
  29.7 0.7 copy-done.3
  30.4 0.0 copy-start.2
  30.4 1.7 %convolution_bitcast_fusion.2 = f32[320,768]{1,0:T(8,128)S(1)} fusion(f32[12,64,320]{2,1,0:T(8,128)S(1)} %broadcast_multiply_fusion, f32[12,64,768]{2,1,0:T(8,128)S(1)} %copy-done.3), kind=kOutput, calls=%fused_computation.2 | convolution fusion | flops 1132462080 | bytes 4325376 | tf_op jit(solution)/shard_map/dot_general | solution.py:200
  32.1 0.0 copy-done.2
  32.1 1.7 %convolution_bitcast_fusion = f32[320,768]{1,0:T(8,128)S(1)} fusion(f32[12,64,320]{2,1,0:T(8,128)S(1)} %broadcast_multiply_fusion, f32[12,64,768]{2,1,0:T(8,128)S(1)} %copy-done.2), kind=kOutput, calls=%fused_computation | convolution fusion | flops 1132462080 | bytes 4325376 | tf_op jit(solution)/shard_map/dot_general | solution.py:200
  33.9 3.5 %collective-permute-done = f32[12,64,320]{2,1,0:T(8,128)S(1)} collective-permute-done((f32[12,64,320]{2,1,0:T(8,128)S(1)}, f32[12,64,320]{2,1,0:T(8,128)S(1)}, u32[]{:S(2)}, u32[]{:S(2)}) %collective-permute-start) | collective-permute-done | bytes 983072 | tf_op jit(solution)/shard_map/ppermute | solution.py:14
  37.4 1.0 %fusion.1 = f32[320,320]{1,0:T(8,128)S(1)} fusion(f32[320,768]{1,0:T(8,128)S(1)} %convolution_bitcast_fusion.2, f32[768,320]{1,0:T(8,128)S(1)} %bitcast.26), kind=kOutput, calls=%fused_computation.14 | convolution fusion | flops 471859200 | bytes 2375680 | tf_op jit(solution)/shard_map/dot_general | solution.py:18
  38.4 22.8 %collective-permute-done.1 = f32[12,64,320]{2,1,0:T(8,128)S(1)} collective-permute-done((f32[12,64,320]{2,1,0:T(8,128)S(1)}, f32[12,64,320]{2,1,0:T(8,128)S(1)}, u32[]{:S(2)}, u32[]{:S(2)}) %collective-permute-start.1) | collective-permute-done | bytes 983072 | tf_op jit(solution)/shard_map/ppermute | solution.py:14
  61.2 1.0 %fusion.3 = f32[320,320]{1,0:T(8,128)S(1)} fusion(f32[320,768]{1,0:T(8,128)S(1)} %convolution_bitcast_fusion, f32[768,320]{1,0:T(8,128)S(1)} %bitcast.25), kind=kOutput, calls=%fused_computation.16 | convolution fusion | flops 471859200 | bytes 2375680 | tf_op jit(solution)/shard_map/dot_general | solution.py:18
  62.1 1.1 %pad_add_fusion = f32[320,448]{1,0:T(8,128)} fusion(f32[320,320]{1,0:T(8,128)S(1)} %fusion.3, f32[320,320]{1,0:T(8,128)S(1)} %fusion.2, f32[320,320]{1,0:T(8,128)S(1)} %fusion.1), kind=kLoop, calls=%fused_computation.3 | loop fusion | flops 286720 | bytes 1802240 | tf_op jit(solution)/shard_map/add | solution.py:212
  63.2 22.3 %shard_map.56 = f32[64,704]{1,0:T(8,128)} custom-call(f32[5,64,448]{2,1,0:T(8,128)} %bitcast.24), custom_call_target="tpu_custom_call" | custom-call | tf_op jit(solution)/shard_map/pallas_call | solution.py:153
  85.5 1.6 %copy.10 = f32[1,64,704]{2,1,0:T(8,128)} copy(f32[1,64,704]{2,1,0:T(8,128)} %bitcast.27) | data formatting | bytes 360448
  (3 shorter events, 0.0 us)
Async XLA Ops:
  1.0 13.7 %copy-start.1 = (s32[12]{0:T(128)S(1)}, s32[12]{0:T(128)}, u32[]{:S(2)}) copy-start(s32[12]{0:T(128)} %param.7) | copy-start | bytes 148
  1.0 13.8 %copy-start = (s32[12,14]{1,0:T(8,128)S(1)}, s32[12,14]{1,0:T(8,128)}, u32[]{:S(2)}) copy-start(s32[12,14]{1,0:T(8,128)} %param.6) | copy-start | bytes 2020
  2.4 35.0 %collective-permute-start = (f32[12,64,320]{2,1,0:T(8,128)S(1)}, f32[12,64,320]{2,1,0:T(8,128)S(1)}, u32[]{:S(2)}, u32[]{:S(2)}) collective-permute-start(f32[12,64,320]{2,1,0:T(8,128)S(1)} %broadcast_multiply_fusion), channel_id=1, source_target_pairs={{0,1},{1,2},{2,3},{3,4},{4,5},{5,6},{6,7},{7,8},{8,9},{9,10},{10,1... | collective-permute-start | bytes 2949128 | tf_op jit(solution)/shard_map/ppermute | solution.py:14
  6.8 54.3 %collective-permute-start.1 = (f32[12,64,320]{2,1,0:T(8,128)S(1)}, f32[12,64,320]{2,1,0:T(8,128)S(1)}, u32[]{:S(2)}, u32[]{:S(2)}) collective-permute-start(f32[12,64,320]{2,1,0:T(8,128)S(1)} %broadcast_multiply_fusion), channel_id=1, source_target_pairs={{1,0},{2,1},{3,2},{4,3},{5,4},{6,5},{7,6},{8,7},{9,8},{10,9},{11,1... | collective-permute-start | bytes 2949128 | tf_op jit(solution)/shard_map/ppermute | solution.py:14
  28.7 1.7 %copy-start.3 = (f32[12,64,768]{2,1,0:T(8,128)S(1)}, f32[12,64,768]{2,1,0:T(8,128)}, u32[]{:S(2)}) copy-start(f32[12,64,768]{2,1,0:T(8,128)} %get-tuple-element.8) | copy-start | bytes 7077892
  30.4 1.8 %copy-start.2 = (f32[12,64,768]{2,1,0:T(8,128)S(1)}, f32[12,64,768]{2,1,0:T(8,128)}, u32[]{:S(2)}) copy-start(f32[12,64,768]{2,1,0:T(8,128)} %get-tuple-element.10) | copy-start | bytes 7077892

commit v12 on v5

--- a/solution.py
+++ b/solution.py
@@ -66,13 +66,18 @@
     group_total = lax.axis_size("rows") * lax.axis_size("cols")
     position = lax.axis_index("rows") * lax.axis_size("cols") + lax.axis_index("cols")
     flat_axis = ("rows", "cols")
+    lower_raw, lower_mask = from_behind((p_vals, p_mask), flat_axis, 1)
+    upper_raw, upper_mask = from_behind((p_vals, p_mask), flat_axis, -1)
     slot_ids = jnp.arange(prol_slots, dtype=jnp.int32)
-    target = position + slot_ids - 2
-    inside = ((target >= 0) & (target < group_total)).astype(jnp.float32)
-    keep = jnp.repeat(p_mask.astype(jnp.float32) * inside[None, :], block_size, axis=1)
-    pflat = p_vals * keep[:, None, :]
-    lower_rows = from_behind(pflat, flat_axis, 1)
-    upper_rows = from_behind(pflat, flat_axis, -1)
+
+    def keep_of(mask, owner):
+        target = owner + slot_ids - 2
+        inside = ((target >= 0) & (target < group_total)).astype(jnp.float32)
+        return jnp.repeat(mask.astype(jnp.float32) * inside[None, :], block_size, axis=1)[:, None, :]
+
+    pflat = p_vals * keep_of(p_mask, position)
+    lower_rows = lower_raw * keep_of(lower_mask, position - 1)
+    upper_rows = upper_raw * keep_of(upper_mask, position + 1)
     span = rows_here * block_size
     width = prol_slots * block_size
     p_own = pflat.reshape(span, width)

time: 87.9 us -> 92.6 us (1.053)
  waiting for transfers between devices: 35 us -> 23.2 us
  starting transfers between devices: 27.2 us -> 37.2 us
  matrix products: 9.64 us -> 14.3 us
  other arithmetic: 4.63 us -> 6.51 us
    ppermute x6 -> x8, waiting for transfers between devices: 35 us -> 23.2 us  [from_behind(): return lax.ppermute(array, axis, pairs)]
    ppermute x6 -> x8, starting transfers between devices: 27.2 us -> 37.2 us  [from_behind(): return lax.ppermute(array, axis, pairs)]
    dot_general x3, matrix products: 6.73 us -> 9.93 us  [pt_times(): lax.dot_general(p_own, dense[side], (((0,), (0,)), ((), ())), precision=M...]
    mul x2 -> x6, other arithmetic: 2.16 us -> 3.83 us  [the longest x1 1.47 us: shards(): lower_rows = lower_raw * keep_of(lower_mask, position - 1)]
    dot_general x3, matrix products: 2.91 us -> 4.34 us  [mm(): jnp.dot(a, b, precision=MATMUL_PRECISION, preferred_element_type=jnp.floa...]
  transfers between devices with their start and end apart: 6 -> 8, of which waited for: 4 -> 2; matrix products, arithmetic and copies ran while one was open for 12% -> 22% of each run, Pallas kernels for 10% -> 10%
where the time goes in v12:
time: 92.6 us; the launch traced here: 92.1 us
  starting transfers between devices  37.2 us (40%)
  waiting for transfers between devices  23.2 us (25%)
  matrix products  14.3 us (15%)
  Pallas kernels  9.13 us (10%)
  other arithmetic  6.51 us (7%)
  local copies, waits for them, and re-layouts  1.56 us (2%)
    ppermute x8, starting transfers between devices, from_behind(): return lax.ppermute(array, axis, pairs)  37.2 us
    ppermute x8, waiting for transfers between devices, from_behind(): return lax.ppermute(array, axis, pairs)  23.2 us
    dot_general x3, matrix products, pt_times(): lax.dot_general(p_own, dense[side], (((0,), (0,)), ((), ())), precision=M...  9.93 us
    pallas_call x1, Pallas kernels, dense_sides(): pl.pallas_call(dense_kernel, out_shape=[jax.ShapeDtypeStruct((rows_here,...  9.13 us
    dot_general x3, matrix products, mm(): jnp.dot(a, b, precision=MATMUL_PRECISION, preferred_element_type=jnp.floa...  4.34 us
  transfers between devices with their start and end apart: 8, of which 2 were waited for; matrix products, arithmetic and copies ran while one was open for 22% of the time, Pallas kernels for 10%

profile of v12, /device:TPU:1, one launch (start us, length us, event | category | flops | bytes accessed | tf_op | source)
XLA Modules:
  0.0 92.1 jit_solution(15773685570034510041)
XLA Ops:
  0.0 4.4 %collective-permute-start.1 = (s32[12,5]{0,1:T(8,128)}, s32[12,5]{0,1:T(8,128)S(1)}, u32[]{:S(2)}, u32[]{:S(2)}) collective-permute-start(s32[12,5]{0,1:T(8,128)} %param.9), channel_id=1, source_target_pairs={{0,1},{1,2},{2,3},{3,4},{4,5},{5,6},{6,7},{7,8},{8,9},{9,10},{10,1... | collective-permute-start | bytes 728 | tf_op jit(solution)/shard_map/ppermute | solution.py:14
  4.4 7.4 %collective-permute-start.3 = (s32[12,5]{0,1:T(8,128)}, s32[12,5]{0,1:T(8,128)S(1)}, u32[]{:S(2)}, u32[]{:S(2)}) collective-permute-start(s32[12,5]{0,1:T(8,128)} %param.9), channel_id=1, source_target_pairs={{1,0},{2,1},{3,2},{4,3},{5,4},{6,5},{7,6},{8,7},{9,8},{10,9},{11,1... | collective-permute-start | bytes 728 | tf_op jit(solution)/shard_map/ppermute | solution.py:14
  11.8 1.9 %collective-permute-start = (f32[12,64,320]{2,1,0:T(8,128)}, f32[12,64,320]{2,1,0:T(8,128)}, u32[]{:S(2)}, u32[]{:S(2)}) collective-permute-start(f32[12,64,320]{2,1,0:T(8,128)} %param.8), channel_id=1, source_target_pairs={{0,1},{1,2},{2,3},{3,4},{4,5},{5,6},{6,7},{7,8},{8,9},{9,10},{10,1... | collective-permute-start | bytes 2949128 | tf_op jit(solution)/shard_map/ppermute | solution.py:14
  13.7 7.6 %collective-permute-start.2 = (f32[12,64,320]{2,1,0:T(8,128)}, f32[12,64,320]{2,1,0:T(8,128)S(1)}, u32[]{:S(2)}, u32[]{:S(2)}) collective-permute-start(f32[12,64,320]{2,1,0:T(8,128)} %param.8), channel_id=1, source_target_pairs={{1,0},{2,1},{3,2},{4,3},{5,4},{6,5},{7,6},{8,7},{9,8},{10,9},{11,1... | collective-permute-start | bytes 2949128 | tf_op jit(solution)/shard_map/ppermute | solution.py:14
  21.3 0.7 iota_compare_fusion.1
  22.0 0.7 broadcast_subtract_fusion
  22.7 0.1 select_reduce_fusion
  22.9 0.7 sub.30.slot_ref
  23.5 0.8 convert_multiply_fusion.2
  24.3 0.1 copy.12
  24.6 1.4 %broadcast_multiply_fusion.2 = f32[12,64,320]{2,1,0:T(8,128)S(1)} fusion(f32[12,64,320]{2,1,0:T(8,128)} %param.8, f32[12,320]{1,0:T(8,128)S(1)} %mul.63), kind=kLoop, calls=%fused_computation.6 | loop fusion | flops 245760 | bytes 1981440 | tf_op jit(solution)/shard_map/mul | solution.py:78
  25.9 9.1 %shard_map.55 = (f32[12,64,768]{2,1,0:T(8,128)}, f32[12,64,768]{2,1,0:T(8,128)}, f32[12,64,768]{2,1,0:T(8,128)}) custom-call(s32[432]{0:T(512)} %sub.30.slot_ref, f32[12,64,896]{2,1,0:T(8,128)} %a_ref.1), custom_call_target="tpu_custom_call" | custom-call | tf_op jit(solution)/shard_map/pallas_call | solution.py:50
  35.1 4.5 %convolution_bitcast_fusion.1 = f32[320,768]{1,0:T(8,128)} fusion(f32[12,64,320]{2,1,0:T(8,128)S(1)} %broadcast_multiply_fusion.2, f32[12,64,768]{2,1,0:T(8,128)} %get-tuple-element.9), kind=kOutput, calls=%fused_computation.1 | convolution fusion | flops 1132462080 | bytes 4325376 | tf_op jit(solution)/shard_map/dot_general | solution.py:94
  39.6 2.7 %convolution_bitcast_fusion.2 = f32[320,768]{1,0:T(8,128)} fusion(f32[12,64,320]{2,1,0:T(8,128)S(1)} %broadcast_multiply_fusion.2, f32[12,64,768]{2,1,0:T(8,128)S(1)} %copy-done.3), kind=kOutput, calls=%fused_computation.2 | convolution fusion | flops 1132462080 | bytes 4325376 | tf_op jit(solution)/shard_map/dot_general | solution.py:94
  42.2 2.4 %fusion.3 = f32[320,320]{1,0:T(8,128)S(1)} fusion(f32[320,768]{1,0:T(8,128)} %convolution_bitcast_fusion.1, f32[768,320]{1,0:T(8,128)S(1)} %bitcast.23), kind=kOutput, calls=%fused_computation.23 | convolution fusion | flops 471859200 | bytes 2375680 | tf_op jit(solution)/shard_map/dot_general | solution.py:18
  44.6 2.8 %convolution_bitcast_fusion = f32[320,768]{1,0:T(8,128)} fusion(f32[12,64,320]{2,1,0:T(8,128)S(1)} %broadcast_multiply_fusion.2, f32[12,64,768]{2,1,0:T(8,128)S(1)} %copy-done.2), kind=kOutput, calls=%fused_computation | convolution fusion | flops 1132462080 | bytes 4325376 | tf_op jit(solution)/shard_map/dot_general | solution.py:94
  47.5 0.1 copy.13
  47.8 0.1 copy.14
  48.0 0.1 mul.74
  48.0 1.5 %broadcast_multiply_fusion.1 = f32[12,64,320]{2,1,0:T(8,128)S(1)} fusion(f32[12,64,320]{2,1,0:T(8,128)} %collective-permute-done, f32[12,320]{1,0:T(8,128)S(1)} %mul.69), kind=kLoop, calls=%fused_computation.5 | loop fusion | flops 245760 | bytes 1981440 | tf_op jit(solution)/shard_map/mul | solution.py:79
  49.5 0.1 copy-done
  49.6 1.0 %fusion.2 = f32[320,320]{1,0:T(8,128)S(1)} fusion(f32[320,768]{1,0:T(8,128)S(1)} %copy-done, f32[768,320]{1,0:T(8,128)S(1)} %bitcast.24), kind=kOutput, calls=%fused_computation.22 | convolution fusion | flops 471859200 | bytes 2375680 | tf_op jit(solution)/shard_map/dot_general | solution.py:18
  50.6 16.5 %collective-permute-done.2 = f32[12,64,320]{2,1,0:T(8,128)S(1)} collective-permute-done((f32[12,64,320]{2,1,0:T(8,128)}, f32[12,64,320]{2,1,0:T(8,128)S(1)}, u32[]{:S(2)}, u32[]{:S(2)}) %collective-permute-start.2) | collective-permute-done | bytes 983072 | tf_op jit(solution)/shard_map/ppermute | solution.py:14
  67.1 0.1 broadcast_multiply_fusion
  67.2 1.0 %fusion.4 = f32[320,320]{1,0:T(8,128)S(1)} fusion(f32[320,768]{1,0:T(8,128)S(1)} %copy-done.1, f32[768,320]{1,0:T(8,128)S(1)} %bitcast.25), kind=kOutput, calls=%fused_computation.24 | convolution fusion | flops 471859200 | bytes 2375680 | tf_op jit(solution)/shard_map/dot_general | solution.py:18
  68.2 0.2 pad_add_fusion
  68.5 1.9 %collective-permute-start.4 = (f32[64,448]{1,0:T(8,128)S(1)}, f32[64,448]{1,0:T(8,128)S(1)}, u32[]{:S(2)}, u32[]{:S(2)}) collective-permute-start(f32[64,448]{1,0:T(8,128)S(1)} %get-tuple-element.15), channel_id=1, source_target_pairs={{0,1},{1,2},{2,3},{3,4},{4,5},{5,6},{6,7},{7,8},{8,9},{9,10},{10,1... | collective-permute-start | bytes 344072 | tf_op jit(solution)/shard_map/ppermute | solution.py:14
  70.4 1.9 %collective-permute-start.5 = (f32[64,448]{1,0:T(8,128)S(1)}, f32[64,448]{1,0:T(8,128)S(1)}, u32[]{:S(2)}, u32[]{:S(2)}) collective-permute-start(f32[64,448]{1,0:T(8,128)S(1)} %get-tuple-element.14), channel_id=1, source_target_pairs={{0,2},{1,3},{2,4},{3,5},{4,6},{5,7},{6,8},{7,9},{8,10},{9,11},{10,... | collective-permute-start | bytes 344072 | tf_op jit(solution)/shard_map/ppermute | solution.py:14
  72.4 8.2 %collective-permute-start.6 = (f32[64,448]{1,0:T(8,128)S(1)}, f32[64,448]{1,0:T(8,128)S(1)}, u32[]{:S(2)}, u32[]{:S(2)}) collective-permute-start(f32[64,448]{1,0:T(8,128)S(1)} %get-tuple-element.13), channel_id=1, source_target_pairs={{1,0},{2,1},{3,2},{4,3},{5,4},{6,5},{7,6},{8,7},{9,8},{10,9},{11,1... | collective-permute-start | bytes 344072 | tf_op jit(solution)/shard_map/ppermute | solution.py:14
  80.6 3.9 %collective-permute-start.7 = (f32[64,448]{1,0:T(8,128)S(1)}, f32[64,448]{1,0:T(8,128)S(1)}, u32[]{:S(2)}, u32[]{:S(2)}) collective-permute-start(f32[64,448]{1,0:T(8,128)S(1)} %get-tuple-element.12), channel_id=1, source_target_pairs={{2,0},{3,1},{4,2},{5,3},{6,4},{7,5},{8,6},{9,7},{10,8},{11,9},{12,... | collective-permute-start | bytes 344072 | tf_op jit(solution)/shard_map/ppermute | solution.py:14
  84.6 6.7 %collective-permute-done.7 = f32[64,448]{1,0:T(8,128)S(1)} collective-permute-done((f32[64,448]{1,0:T(8,128)S(1)}, f32[64,448]{1,0:T(8,128)S(1)}, u32[]{:S(2)}, u32[]{:S(2)}) %collective-permute-start.7) | collective-permute-done | bytes 114720 | tf_op jit(solution)/shard_map/ppermute | solution.py:14
  91.3 0.8 add_bitcast_fusion
  (26 shorter events, 0.6 us)
Async XLA Ops:
  0.0 47.4 %collective-permute-start.1 = (s32[12,5]{0,1:T(8,128)}, s32[12,5]{0,1:T(8,128)S(1)}, u32[]{:S(2)}, u32[]{:S(2)}) collective-permute-start(s32[12,5]{0,1:T(8,128)} %param.9), channel_id=1, source_target_pairs={{0,1},{1,2},{2,3},{3,4},{4,5},{5,6},{6,7},{7,8},{8,9},{9,10},{10,1... | collective-permute-start | bytes 728 | tf_op jit(solution)/shard_map/ppermute | solution.py:14
  4.4 43.3 %collective-permute-start.3 = (s32[12,5]{0,1:T(8,128)}, s32[12,5]{0,1:T(8,128)S(1)}, u32[]{:S(2)}, u32[]{:S(2)}) collective-permute-start(s32[12,5]{0,1:T(8,128)} %param.9), channel_id=1, source_target_pairs={{1,0},{2,1},{3,2},{4,3},{5,4},{6,5},{7,6},{8,7},{9,8},{10,9},{11,1... | collective-permute-start | bytes 728 | tf_op jit(solution)/shard_map/ppermute | solution.py:14
  11.8 36.3 %collective-permute-start = (f32[12,64,320]{2,1,0:T(8,128)}, f32[12,64,320]{2,1,0:T(8,128)}, u32[]{:S(2)}, u32[]{:S(2)}) collective-permute-start(f32[12,64,320]{2,1,0:T(8,128)} %param.8), channel_id=1, source_target_pairs={{0,1},{1,2},{2,3},{3,4},{4,5},{5,6},{6,7},{7,8},{8,9},{9,10},{10,1... | collective-permute-start | bytes 2949128 | tf_op jit(solution)/shard_map/ppermute | solution.py:14
  13.7 53.4 %collective-permute-start.2 = (f32[12,64,320]{2,1,0:T(8,128)}, f32[12,64,320]{2,1,0:T(8,128)S(1)}, u32[]{:S(2)}, u32[]{:S(2)}) collective-permute-start(f32[12,64,320]{2,1,0:T(8,128)} %param.8), channel_id=1, source_target_pairs={{1,0},{2,1},{3,2},{4,3},{5,4},{6,5},{7,6},{8,7},{9,8},{10,9},{11,1... | collective-permute-start | bytes 2949128 | tf_op jit(solution)/shard_map/ppermute | solution.py:14
  35.1 4.5 %copy-start.3 = (f32[12,64,768]{2,1,0:T(8,128)S(1)}, f32[12,64,768]{2,1,0:T(8,128)}, u32[]{:S(2)}) copy-start(f32[12,64,768]{2,1,0:T(8,128)} %get-tuple-element.8) | copy-start | bytes 7077892
  42.2 2.4 %copy-start.2 = (f32[12,64,768]{2,1,0:T(8,128)S(1)}, f32[12,64,768]{2,1,0:T(8,128)}, u32[]{:S(2)}) copy-start(f32[12,64,768]{2,1,0:T(8,128)} %get-tuple-element.10) | copy-start | bytes 7077892
  48.0 1.6 %copy-start = (f32[320,768]{1,0:T(8,128)S(1)}, f32[320,768]{1,0:T(8,128)}, u32[]{:S(2)}) copy-start(f32[320,768]{1,0:T(8,128)} %convolution_bitcast_fusion.2) | copy-start | bytes 2949124
  50.6 16.6 %copy-start.1 = (f32[320,768]{1,0:T(8,128)S(1)}, f32[320,768]{1,0:T(8,128)}, u32[]{:S(2)}) copy-start(f32[320,768]{1,0:T(8,128)} %convolution_bitcast_fusion) | copy-start | bytes 2949124
  68.5 16.0 %collective-permute-start.4 = (f32[64,448]{1,0:T(8,128)S(1)}, f32[64,448]{1,0:T(8,128)S(1)}, u32[]{:S(2)}, u32[]{:S(2)}) collective-permute-start(f32[64,448]{1,0:T(8,128)S(1)} %get-tuple-element.15), channel_id=1, source_target_pairs={{0,1},{1,2},{2,3},{3,4},{4,5},{5,6},{6,7},{7,8},{8,9},{9,10},{10,1... | collective-permute-start | bytes 344072 | tf_op jit(solution)/shard_map/ppermute | solution.py:14
  70.4 14.1 %collective-permute-start.5 = (f32[64,448]{1,0:T(8,128)S(1)}, f32[64,448]{1,0:T(8,128)S(1)}, u32[]{:S(2)}, u32[]{:S(2)}) collective-permute-start(f32[64,448]{1,0:T(8,128)S(1)} %get-tuple-element.14), channel_id=1, source_target_pairs={{0,2},{1,3},{2,4},{3,5},{4,6},{5,7},{6,8},{7,9},{8,10},{9,11},{10,... | collective-permute-start | bytes 344072 | tf_op jit(solution)/shard_map/ppermute | solution.py:14
  72.4 12.2 %collective-permute-start.6 = (f32[64,448]{1,0:T(8,128)S(1)}, f32[64,448]{1,0:T(8,128)S(1)}, u32[]{:S(2)}, u32[]{:S(2)}) collective-permute-start(f32[64,448]{1,0:T(8,128)S(1)} %get-tuple-element.13), channel_id=1, source_target_pairs={{1,0},{2,1},{3,2},{4,3},{5,4},{6,5},{7,6},{8,7},{9,8},{10,9},{11,1... | collective-permute-start | bytes 344072 | tf_op jit(solution)/shard_map/ppermute | solution.py:14
  80.6 10.7 %collective-permute-start.7 = (f32[64,448]{1,0:T(8,128)S(1)}, f32[64,448]{1,0:T(8,128)S(1)}, u32[]{:S(2)}, u32[]{:S(2)}) collective-permute-start(f32[64,448]{1,0:T(8,128)S(1)} %get-tuple-element.12), channel_id=1, source_target_pairs={{2,0},{3,1},{4,2},{5,3},{6,4},{7,5},{8,6},{9,7},{10,8},{11,9},{12,... | collective-permute-start | bytes 344072 | tf_op jit(solution)/shard_map/ppermute | solution.py:14

commit v13 on v11

--- a/solution.py
+++ b/solution.py
@@ -129,7 +129,6 @@
             copy.start()
 
     acc[...] = jnp.zeros(acc.shape, acc.dtype)
-    place(acc, terms_ref[2], lanes)
     for copy, shift, k in zip(second, (1, -1), (0, 1)):
         @pl.when(has[shift])
         def _():
@@ -214,7 +213,7 @@
         + jnp.pad(t_high, ((0, 0), (2 * block_size, 0)))
     ).reshape(prol_slots, block_size, (prol_slots + 2) * block_size)
 
-    result = exchange(terms)
+    result = exchange(terms) + jnp.pad(terms[2], ((0, 0), (2 * block_size, 2 * block_size)))
     return result.reshape(1, block_size, (prol_slots + 6) * block_size)
 
 

time: 87.5 us -> 87.5 us (level)
    reshape x0 -> x1, other arithmetic: none -> 1.62 us  [shards(): return result.reshape(1, block_size, (prol_slots + 6) * block_size)]
    unnamed x9 -> x10, local copies, waits for them, and re-layouts: 2.31 us -> 1.51 us
  transfers between devices with their start and end apart: 2 -> 2, of which waited for: 2 -> 2; matrix products, arithmetic and copies ran while one was open for 12% -> 12% of each run, Pallas kernels for 11% -> 10%
where the time goes in v13:
time: 87.5 us; the launch traced here: 87.1 us
  Pallas kernels  31.4 us (36%)
  waiting for transfers between devices  26.3 us (30%)
  starting transfers between devices  11.8 us (13%)
  matrix products  9.64 us (11%)
  other arithmetic  5.42 us (6%)
  local copies, waits for them, and re-layouts  2.43 us (3%)
    ppermute x2, waiting for transfers between devices, from_behind(): return lax.ppermute(array, axis, pairs)  26.3 us
    pallas_call x1, Pallas kernels, exchange(): pl.pallas_call(exchange_kernel, out_shape=jax.ShapeDtypeStruct((block_siz...  22.3 us
    ppermute x2, starting transfers between devices, from_behind(): return lax.ppermute(array, axis, pairs)  11.8 us
    pallas_call x1, Pallas kernels, dense_sides(): pl.pallas_call(dense_kernel, out_shape=[jax.ShapeDtypeStruct((rows_here,...  9.13 us
    dot_general x3, matrix products, pt_times(): lax.dot_general(p_own, dense[side], (((0,), (0,)), ((), ())), precision=M...  6.74 us
    dot_general x3, matrix products, mm(): jnp.dot(a, b, precision=MATMUL_PRECISION, preferred_element_type=jnp.floa...  2.9 us
  transfers between devices with their start and end apart: 2, of which 2 were waited for; matrix products, arithmetic and copies ran while one was open for 12% of the time, Pallas kernels for 10%

profile of v13, /device:TPU:1, one launch (start us, length us, event | category | flops | bytes accessed | tf_op | source)
XLA Modules:
  0.0 87.1 jit_solution(15894697942575924685)
XLA Ops:
  0.0 0.8 convert_multiply_fusion
  0.8 0.1 copy.8
  0.9 0.1 broadcast_in_dim.10
  0.9 0.1 mul.27
  1.0 0.0 copy-start.2
  1.0 1.4 %broadcast_multiply_fusion = f32[12,64,320]{2,1,0:T(8,128)S(1)} fusion(f32[12,64,320]{2,1,0:T(8,128)} %param.8, f32[12,320]{1,0:T(8,128)S(1)} %mul.27), kind=kLoop, calls=%fused_computation.4 | loop fusion | flops 245760 | bytes 1981440 | tf_op jit(solution)/shard_map/mul | solution.py:183
  2.4 4.4 %collective-permute-start = (f32[12,64,320]{2,1,0:T(8,128)S(1)}, f32[12,64,320]{2,1,0:T(8,128)S(1)}, u32[]{:S(2)}, u32[]{:S(2)}) collective-permute-start(f32[12,64,320]{2,1,0:T(8,128)S(1)} %broadcast_multiply_fusion), channel_id=1, source_target_pairs={{0,1},{1,2},{2,3},{3,4},{4,5},{5,6},{6,7},{7,8},{8,9},{9,10},{10,1... | collective-permute-start | bytes 2949128 | tf_op jit(solution)/shard_map/ppermute | solution.py:14
  6.8 7.4 %collective-permute-start.1 = (f32[12,64,320]{2,1,0:T(8,128)S(1)}, f32[12,64,320]{2,1,0:T(8,128)S(1)}, u32[]{:S(2)}, u32[]{:S(2)}) collective-permute-start(f32[12,64,320]{2,1,0:T(8,128)S(1)} %broadcast_multiply_fusion), channel_id=1, source_target_pairs={{1,0},{2,1},{3,2},{4,3},{5,4},{6,5},{7,6},{8,7},{9,8},{10,9},{11,1... | collective-permute-start | bytes 2949128 | tf_op jit(solution)/shard_map/ppermute | solution.py:14
  14.2 0.5 iota_add_fusion
  14.7 0.0 copy-done.2
  14.7 0.1 iota_compare_fusion.1
  14.8 0.0 copy-done.1
  14.8 0.8 select_reduce_fusion
  15.6 0.7 sub.23.slot_ref
  16.3 9.1 %shard_map.55 = (f32[12,64,768]{2,1,0:T(8,128)}, f32[12,64,768]{2,1,0:T(8,128)}, f32[12,64,768]{2,1,0:T(8,128)}) custom-call(s32[432]{0:T(512)} %sub.23.slot_ref, f32[12,64,896]{2,1,0:T(8,128)} %a_ref.1), custom_call_target="tpu_custom_call" | custom-call | tf_op jit(solution)/shard_map/pallas_call | solution.py:50
  25.4 3.3 %convolution_bitcast_fusion.1 = f32[320,768]{1,0:T(8,128)S(1)} fusion(f32[12,64,320]{2,1,0:T(8,128)S(1)} %broadcast_multiply_fusion, f32[12,64,768]{2,1,0:T(8,128)} %get-tuple-element.9), kind=kOutput, calls=%fused_computation.1 | convolution fusion | flops 1132462080 | bytes 4325376 | tf_op jit(solution)/shard_map/dot_general | solution.py:199
  28.7 0.0 copy-start.4
  28.7 1.0 %fusion.2 = f32[320,320]{1,0:T(8,128)S(1)} fusion(f32[320,768]{1,0:T(8,128)S(1)} %convolution_bitcast_fusion.1, f32[768,320]{1,0:T(8,128)S(1)} %bitcast.24), kind=kOutput, calls=%fused_computation.16 | convolution fusion | flops 471859200 | bytes 2375680 | tf_op jit(solution)/shard_map/dot_general | solution.py:18
  29.7 0.7 copy-done.4
  30.3 0.0 copy-start.3
  30.3 1.7 %convolution_bitcast_fusion.2 = f32[320,768]{1,0:T(8,128)S(1)} fusion(f32[12,64,320]{2,1,0:T(8,128)S(1)} %broadcast_multiply_fusion, f32[12,64,768]{2,1,0:T(8,128)S(1)} %copy-done.4), kind=kOutput, calls=%fused_computation.2 | convolution fusion | flops 1132462080 | bytes 4325376 | tf_op jit(solution)/shard_map/dot_general | solution.py:199
  32.1 0.0 copy-done.3
  32.1 1.7 %convolution_bitcast_fusion = f32[320,768]{1,0:T(8,128)S(1)} fusion(f32[12,64,320]{2,1,0:T(8,128)S(1)} %broadcast_multiply_fusion, f32[12,64,768]{2,1,0:T(8,128)S(1)} %copy-done.3), kind=kOutput, calls=%fused_computation | convolution fusion | flops 1132462080 | bytes 4325376 | tf_op jit(solution)/shard_map/dot_general | solution.py:199
  33.9 3.6 %collective-permute-done = f32[12,64,320]{2,1,0:T(8,128)S(1)} collective-permute-done((f32[12,64,320]{2,1,0:T(8,128)S(1)}, f32[12,64,320]{2,1,0:T(8,128)S(1)}, u32[]{:S(2)}, u32[]{:S(2)}) %collective-permute-start) | collective-permute-done | bytes 983072 | tf_op jit(solution)/shard_map/ppermute | solution.py:14
  37.4 1.0 %fusion.1 = f32[320,320]{1,0:T(8,128)S(1)} fusion(f32[320,768]{1,0:T(8,128)S(1)} %convolution_bitcast_fusion.2, f32[768,320]{1,0:T(8,128)S(1)} %bitcast.27), kind=kOutput, calls=%fused_computation.15 | convolution fusion | flops 471859200 | bytes 2375680 | tf_op jit(solution)/shard_map/dot_general | solution.py:18
  38.4 22.8 %collective-permute-done.1 = f32[12,64,320]{2,1,0:T(8,128)S(1)} collective-permute-done((f32[12,64,320]{2,1,0:T(8,128)S(1)}, f32[12,64,320]{2,1,0:T(8,128)S(1)}, u32[]{:S(2)}, u32[]{:S(2)}) %collective-permute-start.1) | collective-permute-done | bytes 983072 | tf_op jit(solution)/shard_map/ppermute | solution.py:14
  61.2 1.0 %fusion.3 = f32[320,320]{1,0:T(8,128)S(1)} fusion(f32[320,768]{1,0:T(8,128)S(1)} %convolution_bitcast_fusion, f32[768,320]{1,0:T(8,128)S(1)} %bitcast.26), kind=kOutput, calls=%fused_computation.17 | convolution fusion | flops 471859200 | bytes 2375680 | tf_op jit(solution)/shard_map/dot_general | solution.py:18
  62.1 0.2 pad_add_fusion
  62.4 0.0 copy-start
  62.4 0.8 copy-done
  63.2 22.3 %shard_map.56 = f32[64,704]{1,0:T(8,128)} custom-call(f32[5,64,448]{2,1,0:T(8,128)} %bitcast.25), custom_call_target="tpu_custom_call" | custom-call | tf_op jit(solution)/shard_map/pallas_call | solution.py:152
  85.5 1.6 %add_bitcast_fusion = f32[1,64,704]{2,1,0:T(8,128)} fusion(f32[64,704]{1,0:T(8,128)} %shard_map.56, f32[64,448]{1,0:T(8,128)S(1)} %slice.5), kind=kLoop, calls=%fused_computation.5 | loop fusion | flops 45056 | bytes 475136 | tf_op jit(solution)/shard_map/reshape | solution.py:217
  (5 shorter events, 0.0 us)
Async XLA Ops:
  1.0 13.7 %copy-start.2 = (s32[12]{0:T(128)S(1)}, s32[12]{0:T(128)}, u32[]{:S(2)}) copy-start(s32[12]{0:T(128)} %param.7) | copy-start | bytes 148
  1.0 13.8 %copy-start.1 = (s32[12,14]{1,0:T(8,128)S(1)}, s32[12,14]{1,0:T(8,128)}, u32[]{:S(2)}) copy-start(s32[12,14]{1,0:T(8,128)} %param.6) | copy-start | bytes 2020
  2.4 35.0 %collective-permute-start = (f32[12,64,320]{2,1,0:T(8,128)S(1)}, f32[12,64,320]{2,1,0:T(8,128)S(1)}, u32[]{:S(2)}, u32[]{:S(2)}) collective-permute-start(f32[12,64,320]{2,1,0:T(8,128)S(1)} %broadcast_multiply_fusion), channel_id=1, source_target_pairs={{0,1},{1,2},{2,3},{3,4},{4,5},{5,6},{6,7},{7,8},{8,9},{9,10},{10,1... | collective-permute-start | bytes 2949128 | tf_op jit(solution)/shard_map/ppermute | solution.py:14
  6.8 54.3 %collective-permute-start.1 = (f32[12,64,320]{2,1,0:T(8,128)S(1)}, f32[12,64,320]{2,1,0:T(8,128)S(1)}, u32[]{:S(2)}, u32[]{:S(2)}) collective-permute-start(f32[12,64,320]{2,1,0:T(8,128)S(1)} %broadcast_multiply_fusion), channel_id=1, source_target_pairs={{1,0},{2,1},{3,2},{4,3},{5,4},{6,5},{7,6},{8,7},{9,8},{10,9},{11,1... | collective-permute-start | bytes 2949128 | tf_op jit(solution)/shard_map/ppermute | solution.py:14
  28.7 1.7 %copy-start.4 = (f32[12,64,768]{2,1,0:T(8,128)S(1)}, f32[12,64,768]{2,1,0:T(8,128)}, u32[]{:S(2)}) copy-start(f32[12,64,768]{2,1,0:T(8,128)} %get-tuple-element.8) | copy-start | bytes 7077892
  30.3 1.8 %copy-start.3 = (f32[12,64,768]{2,1,0:T(8,128)S(1)}, f32[12,64,768]{2,1,0:T(8,128)}, u32[]{:S(2)}) copy-start(f32[12,64,768]{2,1,0:T(8,128)} %get-tuple-element.10) | copy-start | bytes 7077892
  62.4 0.8 copy-start

commit v14 on v13

--- a/solution.py
+++ b/solution.py
@@ -58,7 +58,9 @@
     )(slot_table, a_vals)
 
 
-def exchange_kernel(terms_ref, out_ref, land1, bufs_r, bufs_l, land_r, land_l, acc, padded, sems):
+def exchange_kernel(
+    terms_ref, out_ref, land1, bufs_r, bufs_l, send_r, send_l, land_r, land_l, acc, padded, sems, local_sems
+):
     col_count = lax.axis_size("cols")
     total = lax.axis_size("rows") * col_count
     me = lax.axis_index("rows") * col_count + lax.axis_index("cols")
@@ -122,7 +124,15 @@
             else:
                 place(bufs_l, land1[1], lanes)
 
-    second = [remote(bufs_r, land_r, 2, 1), remote(bufs_l, land_l, 3, -1)]
+    staged = [
+        pltpu.make_async_copy(bufs_r, send_r, local_sems.at[0]),
+        pltpu.make_async_copy(bufs_l, send_l, local_sems.at[1]),
+    ]
+    for copy in staged:
+        copy.start()
+    for copy in staged:
+        copy.wait()
+    second = [remote(send_r, land_r, 2, 1), remote(send_l, land_l, 3, -1)]
     for copy, shift in zip(second, (1, -1)):
         @pl.when(has[shift])
         def _():
@@ -160,9 +170,12 @@
             pltpu.VMEM((block_size, wide + lanes), jnp.float32),
             pltpu.VMEM((block_size, wide + block_size), jnp.float32),
             pltpu.VMEM((block_size, wide + lanes), jnp.float32),
+            pltpu.VMEM((block_size, wide + block_size), jnp.float32),
+            pltpu.VMEM((block_size, wide + lanes), jnp.float32),
             pltpu.VMEM((block_size, -(-full // lanes) * lanes), jnp.float32),
             pltpu.VMEM((block_size, -(-wide // lanes) * lanes), jnp.float32),
             pltpu.SemaphoreType.DMA((2, 4)),
+            pltpu.SemaphoreType.DMA((2,)),
         ],
         compiler_params=pltpu.CompilerParams(collective_id=0, has_side_effects=True),
     )(terms)

time: 87.5 us -> 87.8 us (level)
  no operation moved by 1% of the time
where the time goes in v14:
time: 87.8 us; the launch traced here: 87.5 us
  Pallas kernels  31.7 us (36%)
  waiting for transfers between devices  26.3 us (30%)
  starting transfers between devices  11.8 us (13%)
  matrix products  9.64 us (11%)
  other arithmetic  5.42 us (6%)
  local copies, waits for them, and re-layouts  2.43 us (3%)
    ppermute x2, waiting for transfers between devices, from_behind(): return lax.ppermute(array, axis, pairs)  26.3 us
    pallas_call x1, Pallas kernels, exchange(): pl.pallas_call(exchange_kernel, out_shape=jax.ShapeDtypeStruct((block_siz...  22.6 us
    ppermute x2, starting transfers between devices, from_behind(): return lax.ppermute(array, axis, pairs)  11.8 us
    pallas_call x1, Pallas kernels, dense_sides(): pl.pallas_call(dense_kernel, out_shape=[jax.ShapeDtypeStruct((rows_here,...  9.14 us
    dot_general x3, matrix products, pt_times(): lax.dot_general(p_own, dense[side], (((0,), (0,)), ((), ())), precision=M...  6.73 us
    dot_general x3, matrix products, mm(): jnp.dot(a, b, precision=MATMUL_PRECISION, preferred_element_type=jnp.floa...  2.9 us
  transfers between devices with their start and end apart: 2, of which 2 were waited for; matrix products, arithmetic and copies ran while one was open for 12% of the time, Pallas kernels for 10%

profile of v14, /device:TPU:1, one launch (start us, length us, event | category | flops | bytes accessed | tf_op | source)
XLA Modules:
  0.0 87.5 jit_solution(7181392114876730256)
XLA Ops:
  0.0 0.8 convert_multiply_fusion
  0.8 0.1 copy.8
  0.9 0.1 broadcast_in_dim.10
  0.9 0.1 mul.27
  1.0 0.0 copy-start.2
  1.0 1.4 %broadcast_multiply_fusion = f32[12,64,320]{2,1,0:T(8,128)S(1)} fusion(f32[12,64,320]{2,1,0:T(8,128)} %param.8, f32[12,320]{1,0:T(8,128)S(1)} %mul.27), kind=kLoop, calls=%fused_computation.4 | loop fusion | flops 245760 | bytes 1981440 | tf_op jit(solution)/shard_map/mul | solution.py:196
  2.4 4.4 %collective-permute-start = (f32[12,64,320]{2,1,0:T(8,128)S(1)}, f32[12,64,320]{2,1,0:T(8,128)S(1)}, u32[]{:S(2)}, u32[]{:S(2)}) collective-permute-start(f32[12,64,320]{2,1,0:T(8,128)S(1)} %broadcast_multiply_fusion), channel_id=1, source_target_pairs={{0,1},{1,2},{2,3},{3,4},{4,5},{5,6},{6,7},{7,8},{8,9},{9,10},{10,1... | collective-permute-start | bytes 2949128 | tf_op jit(solution)/shard_map/ppermute | solution.py:14
  6.8 7.4 %collective-permute-start.1 = (f32[12,64,320]{2,1,0:T(8,128)S(1)}, f32[12,64,320]{2,1,0:T(8,128)S(1)}, u32[]{:S(2)}, u32[]{:S(2)}) collective-permute-start(f32[12,64,320]{2,1,0:T(8,128)S(1)} %broadcast_multiply_fusion), channel_id=1, source_target_pairs={{1,0},{2,1},{3,2},{4,3},{5,4},{6,5},{7,6},{8,7},{9,8},{10,9},{11,1... | collective-permute-start | bytes 2949128 | tf_op jit(solution)/shard_map/ppermute | solution.py:14
  14.2 0.5 iota_add_fusion
  14.7 0.0 copy-done.2
  14.7 0.1 iota_compare_fusion.1
  14.8 0.0 copy-done.1
  14.8 0.8 select_reduce_fusion
  15.6 0.7 sub.23.slot_ref
  16.3 9.1 %shard_map.55 = (f32[12,64,768]{2,1,0:T(8,128)}, f32[12,64,768]{2,1,0:T(8,128)}, f32[12,64,768]{2,1,0:T(8,128)}) custom-call(s32[432]{0:T(512)} %sub.23.slot_ref, f32[12,64,896]{2,1,0:T(8,128)} %a_ref.1), custom_call_target="tpu_custom_call" | custom-call | tf_op jit(solution)/shard_map/pallas_call | solution.py:50
  25.4 3.3 %convolution_bitcast_fusion.1 = f32[320,768]{1,0:T(8,128)S(1)} fusion(f32[12,64,320]{2,1,0:T(8,128)S(1)} %broadcast_multiply_fusion, f32[12,64,768]{2,1,0:T(8,128)} %get-tuple-element.9), kind=kOutput, calls=%fused_computation.1 | convolution fusion | flops 1132462080 | bytes 4325376 | tf_op jit(solution)/shard_map/dot_general | solution.py:212
  28.7 0.0 copy-start.4
  28.7 1.0 %fusion.2 = f32[320,320]{1,0:T(8,128)S(1)} fusion(f32[320,768]{1,0:T(8,128)S(1)} %convolution_bitcast_fusion.1, f32[768,320]{1,0:T(8,128)S(1)} %bitcast.24), kind=kOutput, calls=%fused_computation.16 | convolution fusion | flops 471859200 | bytes 2375680 | tf_op jit(solution)/shard_map/dot_general | solution.py:18
  29.7 0.7 copy-done.4
  30.4 0.0 copy-start.3
  30.4 1.7 %convolution_bitcast_fusion.2 = f32[320,768]{1,0:T(8,128)S(1)} fusion(f32[12,64,320]{2,1,0:T(8,128)S(1)} %broadcast_multiply_fusion, f32[12,64,768]{2,1,0:T(8,128)S(1)} %copy-done.4), kind=kOutput, calls=%fused_computation.2 | convolution fusion | flops 1132462080 | bytes 4325376 | tf_op jit(solution)/shard_map/dot_general | solution.py:212
  32.1 0.0 copy-done.3
  32.1 1.7 %convolution_bitcast_fusion = f32[320,768]{1,0:T(8,128)S(1)} fusion(f32[12,64,320]{2,1,0:T(8,128)S(1)} %broadcast_multiply_fusion, f32[12,64,768]{2,1,0:T(8,128)S(1)} %copy-done.3), kind=kOutput, calls=%fused_computation | convolution fusion | flops 1132462080 | bytes 4325376 | tf_op jit(solution)/shard_map/dot_general | solution.py:212
  33.9 3.6 %collective-permute-done = f32[12,64,320]{2,1,0:T(8,128)S(1)} collective-permute-done((f32[12,64,320]{2,1,0:T(8,128)S(1)}, f32[12,64,320]{2,1,0:T(8,128)S(1)}, u32[]{:S(2)}, u32[]{:S(2)}) %collective-permute-start) | collective-permute-done | bytes 983072 | tf_op jit(solution)/shard_map/ppermute | solution.py:14
  37.4 1.0 %fusion.1 = f32[320,320]{1,0:T(8,128)S(1)} fusion(f32[320,768]{1,0:T(8,128)S(1)} %convolution_bitcast_fusion.2, f32[768,320]{1,0:T(8,128)S(1)} %bitcast.27), kind=kOutput, calls=%fused_computation.15 | convolution fusion | flops 471859200 | bytes 2375680 | tf_op jit(solution)/shard_map/dot_general | solution.py:18
  38.4 22.8 %collective-permute-done.1 = f32[12,64,320]{2,1,0:T(8,128)S(1)} collective-permute-done((f32[12,64,320]{2,1,0:T(8,128)S(1)}, f32[12,64,320]{2,1,0:T(8,128)S(1)}, u32[]{:S(2)}, u32[]{:S(2)}) %collective-permute-start.1) | collective-permute-done | bytes 983072 | tf_op jit(solution)/shard_map/ppermute | solution.py:14
  61.2 1.0 %fusion.3 = f32[320,320]{1,0:T(8,128)S(1)} fusion(f32[320,768]{1,0:T(8,128)S(1)} %convolution_bitcast_fusion, f32[768,320]{1,0:T(8,128)S(1)} %bitcast.26), kind=kOutput, calls=%fused_computation.17 | convolution fusion | flops 471859200 | bytes 2375680 | tf_op jit(solution)/shard_map/dot_general | solution.py:18
  62.1 0.2 pad_add_fusion
  62.4 0.0 copy-start
  62.4 0.8 copy-done
  63.2 22.6 %shard_map.56 = f32[64,704]{1,0:T(8,128)} custom-call(f32[5,64,448]{2,1,0:T(8,128)} %bitcast.25), custom_call_target="tpu_custom_call" | custom-call | tf_op jit(solution)/shard_map/pallas_call | solution.py:162
  85.8 1.6 %add_bitcast_fusion = f32[1,64,704]{2,1,0:T(8,128)} fusion(f32[64,704]{1,0:T(8,128)} %shard_map.56, f32[64,448]{1,0:T(8,128)S(1)} %slice.5), kind=kLoop, calls=%fused_computation.5 | loop fusion | flops 45056 | bytes 475136 | tf_op jit(solution)/shard_map/reshape | solution.py:230
  (5 shorter events, 0.0 us)
Async XLA Ops:
  1.0 13.7 %copy-start.2 = (s32[12]{0:T(128)S(1)}, s32[12]{0:T(128)}, u32[]{:S(2)}) copy-start(s32[12]{0:T(128)} %param.7) | copy-start | bytes 148
  1.0 13.8 %copy-start.1 = (s32[12,14]{1,0:T(8,128)S(1)}, s32[12,14]{1,0:T(8,128)}, u32[]{:S(2)}) copy-start(s32[12,14]{1,0:T(8,128)} %param.6) | copy-start | bytes 2020
  2.4 35.0 %collective-permute-start = (f32[12,64,320]{2,1,0:T(8,128)S(1)}, f32[12,64,320]{2,1,0:T(8,128)S(1)}, u32[]{:S(2)}, u32[]{:S(2)}) collective-permute-start(f32[12,64,320]{2,1,0:T(8,128)S(1)} %broadcast_multiply_fusion), channel_id=1, source_target_pairs={{0,1},{1,2},{2,3},{3,4},{4,5},{5,6},{6,7},{7,8},{8,9},{9,10},{10,1... | collective-permute-start | bytes 2949128 | tf_op jit(solution)/shard_map/ppermute | solution.py:14
  6.8 54.3 %collective-permute-start.1 = (f32[12,64,320]{2,1,0:T(8,128)S(1)}, f32[12,64,320]{2,1,0:T(8,128)S(1)}, u32[]{:S(2)}, u32[]{:S(2)}) collective-permute-start(f32[12,64,320]{2,1,0:T(8,128)S(1)} %broadcast_multiply_fusion), channel_id=1, source_target_pairs={{1,0},{2,1},{3,2},{4,3},{5,4},{6,5},{7,6},{8,7},{9,8},{10,9},{11,1... | collective-permute-start | bytes 2949128 | tf_op jit(solution)/shard_map/ppermute | solution.py:14
  28.7 1.7 %copy-start.4 = (f32[12,64,768]{2,1,0:T(8,128)S(1)}, f32[12,64,768]{2,1,0:T(8,128)}, u32[]{:S(2)}) copy-start(f32[12,64,768]{2,1,0:T(8,128)} %get-tuple-element.8) | copy-start | bytes 7077892
  30.4 1.7 %copy-start.3 = (f32[12,64,768]{2,1,0:T(8,128)S(1)}, f32[12,64,768]{2,1,0:T(8,128)}, u32[]{:S(2)}) copy-start(f32[12,64,768]{2,1,0:T(8,128)} %get-tuple-element.10) | copy-start | bytes 7077892
  62.4 0.8 copy-start

commit v15 on v5

--- a/solution.py
+++ b/solution.py
@@ -96,12 +96,12 @@
 
     t_own = mm(pt_times(1), p_own)
     t_low = mm(pt_times(0), lower_rows.reshape(span, width))
-    t_high = mm(pt_times(2), upper_rows.reshape(span, width))
-    terms = (
-        jnp.pad(t_low, ((0, 0), (0, 2 * block_size)))
-        + jnp.pad(t_own, ((0, 0), (block_size, block_size)))
-        + jnp.pad(t_high, ((0, 0), (2 * block_size, 0)))
-    ).reshape(prol_slots, block_size, (prol_slots + 2) * block_size)
+    partial = jnp.pad(t_low, ((0, 0), (0, 2 * block_size))) + jnp.pad(t_own, ((0, 0), (block_size, block_size)))
+    partial, high_w = lax.optimization_barrier((partial, pt_times(2)))
+    t_high = mm(high_w, upper_rows.reshape(span, width))
+    terms = (partial + jnp.pad(t_high, ((0, 0), (2 * block_size, 0)))).reshape(
+        prol_slots, block_size, (prol_slots + 2) * block_size
+    )
 
     def spread(s, block):
         return jnp.pad(block, ((0, 0), ((prol_slots - 1 - s) * block_size, s * block_size)))

time: 87.9 us -> 87.6 us (level)
  transfers between devices with their start and end apart: 6 -> 6, of which waited for: 4 -> 4; matrix products, arithmetic and copies ran while one was open for 12% -> 13% of each run, Pallas kernels for 10% -> 10%
where the time goes in v15:
time: 87.6 us; the launch traced here: 87.3 us
  waiting for transfers between devices  34.4 us (39%)
  starting transfers between devices  27.4 us (31%)
  matrix products  9.79 us (11%)
  Pallas kernels  9.13 us (10%)
  other arithmetic  4.7 us (5%)
  local copies, waits for them, and re-layouts  1.65 us (2%)
    ppermute x6, waiting for transfers between devices, from_behind(): return lax.ppermute(array, axis, pairs)  34.4 us
    ppermute x6, starting transfers between devices, from_behind(): return lax.ppermute(array, axis, pairs)  27.4 us
    pallas_call x1, Pallas kernels, dense_sides(): pl.pallas_call(dense_kernel, out_shape=[jax.ShapeDtypeStruct((rows_here,...  9.13 us
    dot_general x3, matrix products, pt_times(): lax.dot_general(p_own, dense[side], (((0,), (0,)), ((), ())), precision=M...  6.89 us
    dot_general x3, matrix products, mm(): jnp.dot(a, b, precision=MATMUL_PRECISION, preferred_element_type=jnp.floa...  2.91 us
  transfers between devices with their start and end apart: 6, of which 4 were waited for; matrix products, arithmetic and copies ran while one was open for 13% of the time, Pallas kernels for 10%

profile of v15, /device:TPU:1, one launch (start us, length us, event | category | flops | bytes accessed | tf_op | source)
XLA Modules:
  0.0 87.3 jit_solution(15368932684418542958)
XLA Ops:
  0.0 0.8 convert_multiply_fusion
  0.8 0.1 copy.8
  0.9 0.1 broadcast_in_dim.10
  0.9 0.1 mul.27
  1.0 1.4 %broadcast_multiply_fusion = f32[12,64,320]{2,1,0:T(8,128)S(1)} fusion(f32[12,64,320]{2,1,0:T(8,128)} %param.8, f32[12,320]{1,0:T(8,128)S(1)} %mul.27), kind=kLoop, calls=%fused_computation.5 | loop fusion | flops 245760 | bytes 1981440 | tf_op jit(solution)/shard_map/mul | solution.py:73
  2.4 4.4 %collective-permute-start = (f32[12,64,320]{2,1,0:T(8,128)S(1)}, f32[12,64,320]{2,1,0:T(8,128)S(1)}, u32[]{:S(2)}, u32[]{:S(2)}) collective-permute-start(f32[12,64,320]{2,1,0:T(8,128)S(1)} %broadcast_multiply_fusion), channel_id=1, source_target_pairs={{0,1},{1,2},{2,3},{3,4},{4,5},{5,6},{6,7},{7,8},{8,9},{9,10},{10,1... | collective-permute-start | bytes 2949128 | tf_op jit(solution)/shard_map/ppermute | solution.py:14
  6.8 7.4 %collective-permute-start.1 = (f32[12,64,320]{2,1,0:T(8,128)S(1)}, f32[12,64,320]{2,1,0:T(8,128)S(1)}, u32[]{:S(2)}, u32[]{:S(2)}) collective-permute-start(f32[12,64,320]{2,1,0:T(8,128)S(1)} %broadcast_multiply_fusion), channel_id=1, source_target_pairs={{1,0},{2,1},{3,2},{4,3},{5,4},{6,5},{7,6},{8,7},{9,8},{10,9},{11,1... | collective-permute-start | bytes 2949128 | tf_op jit(solution)/shard_map/ppermute | solution.py:14
  14.2 0.5 iota_add_fusion
  14.7 0.1 iota_compare_fusion.1
  14.8 0.8 select_reduce_fusion
  15.6 0.7 sub.23.slot_ref
  16.3 9.1 %shard_map.55 = (f32[12,64,768]{2,1,0:T(8,128)}, f32[12,64,768]{2,1,0:T(8,128)}, f32[12,64,768]{2,1,0:T(8,128)}) custom-call(s32[432]{0:T(512)} %sub.23.slot_ref, f32[12,64,896]{2,1,0:T(8,128)} %a_ref.1), custom_call_target="tpu_custom_call" | custom-call | tf_op jit(solution)/shard_map/pallas_call | solution.py:50
  25.4 3.4 %convolution_bitcast_fusion.2 = f32[320,768]{1,0:T(8,128)S(1)} fusion(f32[12,64,320]{2,1,0:T(8,128)S(1)} %broadcast_multiply_fusion, f32[12,64,768]{2,1,0:T(8,128)} %get-tuple-element.10), kind=kOutput, calls=%fused_computation.2 | convolution fusion | flops 1132462080 | bytes 4325376 | tf_op jit(solution)/shard_map/dot_general | solution.py:89
  28.8 1.7 %convolution_bitcast_fusion.1 = f32[320,768]{1,0:T(8,128)S(1)} fusion(f32[12,64,320]{2,1,0:T(8,128)S(1)} %broadcast_multiply_fusion, f32[12,64,768]{2,1,0:T(8,128)S(1)} %copy-done.3), kind=kOutput, calls=%fused_computation.1 | convolution fusion | flops 1132462080 | bytes 4325376 | tf_op jit(solution)/shard_map/dot_general | solution.py:89
  30.6 1.0 %fusion.3 = f32[320,320]{1,0:T(8,128)S(1)} fusion(f32[320,768]{1,0:T(8,128)S(1)} %convolution_bitcast_fusion.1, f32[768,320]{1,0:T(8,128)S(1)} %bitcast.23), kind=kOutput, calls=%fused_computation.18 | convolution fusion | flops 471859200 | bytes 2375680 | tf_op jit(solution)/shard_map/dot_general | solution.py:18
  31.6 0.7 copy-done.2
  32.3 1.7 %convolution_bitcast_fusion = f32[320,768]{1,0:T(8,128)S(1)} fusion(f32[12,64,320]{2,1,0:T(8,128)S(1)} %broadcast_multiply_fusion, f32[12,64,768]{2,1,0:T(8,128)S(1)} %copy-done.2), kind=kOutput, calls=%fused_computation | convolution fusion | flops 1132462080 | bytes 4325376 | tf_op jit(solution)/shard_map/dot_general | solution.py:89
  34.0 3.4 %collective-permute-done = f32[12,64,320]{2,1,0:T(8,128)S(1)} collective-permute-done((f32[12,64,320]{2,1,0:T(8,128)S(1)}, f32[12,64,320]{2,1,0:T(8,128)S(1)}, u32[]{:S(2)}, u32[]{:S(2)}) %collective-permute-start) | collective-permute-done | bytes 983072 | tf_op jit(solution)/shard_map/ppermute | solution.py:14
  37.4 1.0 %fusion.2 = f32[320,320]{1,0:T(8,128)S(1)} fusion(f32[320,768]{1,0:T(8,128)S(1)} %convolution_bitcast_fusion.2, f32[768,320]{1,0:T(8,128)S(1)} %bitcast.25), kind=kOutput, calls=%fused_computation.17 | convolution fusion | flops 471859200 | bytes 2375680 | tf_op jit(solution)/shard_map/dot_general | solution.py:18
  38.4 0.2 pad_add_fusion.1
  38.6 22.5 %collective-permute-done.1 = f32[12,64,320]{2,1,0:T(8,128)S(1)} collective-permute-done((f32[12,64,320]{2,1,0:T(8,128)S(1)}, f32[12,64,320]{2,1,0:T(8,128)S(1)}, u32[]{:S(2)}, u32[]{:S(2)}) %collective-permute-start.1) | collective-permute-done | bytes 983072 | tf_op jit(solution)/shard_map/ppermute | solution.py:14
  61.2 1.0 %fusion.4 = f32[320,320]{1,0:T(8,128)S(1)} fusion(f32[320,768]{1,0:T(8,128)S(1)} %convolution_bitcast_fusion, f32[768,320]{1,0:T(8,128)S(1)} %bitcast.24), kind=kOutput, calls=%fused_computation.19 | convolution fusion | flops 471859200 | bytes 2375680 | tf_op jit(solution)/shard_map/dot_general | solution.py:18
  62.1 0.1 pad_add_fusion
  62.3 2.2 %collective-permute-start.2 = (f32[64,448]{1,0:T(8,128)S(1)}, f32[64,448]{1,0:T(8,128)S(1)}, u32[]{:S(2)}, u32[]{:S(2)}) collective-permute-start(f32[64,448]{1,0:T(8,128)S(1)} %get-tuple-element.19), channel_id=1, source_target_pairs={{0,1},{1,2},{2,3},{3,4},{4,5},{5,6},{6,7},{7,8},{8,9},{9,10},{10,1... | collective-permute-start | bytes 344072 | tf_op jit(solution)/shard_map/ppermute | solution.py:14
  64.5 2.4 %collective-permute-start.3 = (f32[64,448]{1,0:T(8,128)S(1)}, f32[64,448]{1,0:T(8,128)S(1)}, u32[]{:S(2)}, u32[]{:S(2)}) collective-permute-start(f32[64,448]{1,0:T(8,128)S(1)} %get-tuple-element.18), channel_id=1, source_target_pairs={{0,2},{1,3},{2,4},{3,5},{4,6},{5,7},{6,8},{7,9},{8,10},{9,11},{10,... | collective-permute-start | bytes 344072 | tf_op jit(solution)/shard_map/ppermute | solution.py:14
  66.9 7.1 %collective-permute-start.4 = (f32[64,448]{1,0:T(8,128)S(1)}, f32[64,448]{1,0:T(8,128)S(1)}, u32[]{:S(2)}, u32[]{:S(2)}) collective-permute-start(f32[64,448]{1,0:T(8,128)S(1)} %get-tuple-element.17), channel_id=1, source_target_pairs={{1,0},{2,1},{3,2},{4,3},{5,4},{6,5},{7,6},{8,7},{9,8},{10,9},{11,1... | collective-permute-start | bytes 344072 | tf_op jit(solution)/shard_map/ppermute | solution.py:14
  74.0 3.9 %collective-permute-start.5 = (f32[64,448]{1,0:T(8,128)S(1)}, f32[64,448]{1,0:T(8,128)S(1)}, u32[]{:S(2)}, u32[]{:S(2)}) collective-permute-start(f32[64,448]{1,0:T(8,128)S(1)} %get-tuple-element.16), channel_id=1, source_target_pairs={{2,0},{3,1},{4,2},{5,3},{6,4},{7,5},{8,6},{9,7},{10,8},{11,9},{12,... | collective-permute-start | bytes 344072 | tf_op jit(solution)/shard_map/ppermute | solution.py:14
  78.0 0.0 collective-permute-done.2
  78.0 0.0 collective-permute-done.3
  78.0 0.1 collective-permute-done.4
  78.1 8.3 %collective-permute-done.5 = f32[64,448]{1,0:T(8,128)S(1)} collective-permute-done((f32[64,448]{1,0:T(8,128)S(1)}, f32[64,448]{1,0:T(8,128)S(1)}, u32[]{:S(2)}, u32[]{:S(2)}) %collective-permute-start.5) | collective-permute-done | bytes 114720 | tf_op jit(solution)/shard_map/ppermute | solution.py:14
  86.5 0.8 add_bitcast_fusion
  (11 shorter events, 0.1 us)
Async XLA Ops:
  1.0 13.7 %copy-start.1 = (s32[12]{0:T(128)S(1)}, s32[12]{0:T(128)}, u32[]{:S(2)}) copy-start(s32[12]{0:T(128)} %param.7) | copy-start | bytes 148
  1.0 13.8 %copy-start = (s32[12,14]{1,0:T(8,128)S(1)}, s32[12,14]{1,0:T(8,128)}, u32[]{:S(2)}) copy-start(s32[12,14]{1,0:T(8,128)} %param.6) | copy-start | bytes 2020
  2.4 35.0 %collective-permute-start = (f32[12,64,320]{2,1,0:T(8,128)S(1)}, f32[12,64,320]{2,1,0:T(8,128)S(1)}, u32[]{:S(2)}, u32[]{:S(2)}) collective-permute-start(f32[12,64,320]{2,1,0:T(8,128)S(1)} %broadcast_multiply_fusion), channel_id=1, source_target_pairs={{0,1},{1,2},{2,3},{3,4},{4,5},{5,6},{6,7},{7,8},{8,9},{9,10},{10,1... | collective-permute-start | bytes 2949128 | tf_op jit(solution)/shard_map/ppermute | solution.py:14
  6.8 54.3 %collective-permute-start.1 = (f32[12,64,320]{2,1,0:T(8,128)S(1)}, f32[12,64,320]{2,1,0:T(8,128)S(1)}, u32[]{:S(2)}, u32[]{:S(2)}) collective-permute-start(f32[12,64,320]{2,1,0:T(8,128)S(1)} %broadcast_multiply_fusion), channel_id=1, source_target_pairs={{1,0},{2,1},{3,2},{4,3},{5,4},{6,5},{7,6},{8,7},{9,8},{10,9},{11,1... | collective-permute-start | bytes 2949128 | tf_op jit(solution)/shard_map/ppermute | solution.py:14
  25.4 3.4 %copy-start.3 = (f32[12,64,768]{2,1,0:T(8,128)S(1)}, f32[12,64,768]{2,1,0:T(8,128)}, u32[]{:S(2)}) copy-start(f32[12,64,768]{2,1,0:T(8,128)} %get-tuple-element.11) | copy-start | bytes 7077892
  30.6 1.7 %copy-start.2 = (f32[12,64,768]{2,1,0:T(8,128)S(1)}, f32[12,64,768]{2,1,0:T(8,128)}, u32[]{:S(2)}) copy-start(f32[12,64,768]{2,1,0:T(8,128)} %get-tuple-element.12) | copy-start | bytes 7077892
  62.3 15.7 %collective-permute-start.2 = (f32[64,448]{1,0:T(8,128)S(1)}, f32[64,448]{1,0:T(8,128)S(1)}, u32[]{:S(2)}, u32[]{:S(2)}) collective-permute-start(f32[64,448]{1,0:T(8,128)S(1)} %get-tuple-element.19), channel_id=1, source_target_pairs={{0,1},{1,2},{2,3},{3,4},{4,5},{5,6},{6,7},{7,8},{8,9},{9,10},{10,1... | collective-permute-start | bytes 344072 | tf_op jit(solution)/shard_map/ppermute | solution.py:14
  64.5 13.4 %collective-permute-start.3 = (f32[64,448]{1,0:T(8,128)S(1)}, f32[64,448]{1,0:T(8,128)S(1)}, u32[]{:S(2)}, u32[]{:S(2)}) collective-permute-start(f32[64,448]{1,0:T(8,128)S(1)} %get-tuple-element.18), channel_id=1, source_target_pairs={{0,2},{1,3},{2,4},{3,5},{4,6},{5,7},{6,8},{7,9},{8,10},{9,11},{10,... | collective-permute-start | bytes 344072 | tf_op jit(solution)/shard_map/ppermute | solution.py:14
  66.9 11.2 %collective-permute-start.4 = (f32[64,448]{1,0:T(8,128)S(1)}, f32[64,448]{1,0:T(8,128)S(1)}, u32[]{:S(2)}, u32[]{:S(2)}) collective-permute-start(f32[64,448]{1,0:T(8,128)S(1)} %get-tuple-element.17), channel_id=1, source_target_pairs={{1,0},{2,1},{3,2},{4,3},{5,4},{6,5},{7,6},{8,7},{9,8},{10,9},{11,1... | collective-permute-start | bytes 344072 | tf_op jit(solution)/shard_map/ppermute | solution.py:14
  74.0 12.4 %collective-permute-start.5 = (f32[64,448]{1,0:T(8,128)S(1)}, f32[64,448]{1,0:T(8,128)S(1)}, u32[]{:S(2)}, u32[]{:S(2)}) collective-permute-start(f32[64,448]{1,0:T(8,128)S(1)} %get-tuple-element.16), channel_id=1, source_target_pairs={{2,0},{3,1},{4,2},{5,3},{6,4},{7,5},{8,6},{9,7},{10,8},{11,9},{12,... | collective-permute-start | bytes 344072 | tf_op jit(solution)/shard_map/ppermute | solution.py:14

commit v16 on v14

--- a/solution.py
+++ b/solution.py
@@ -219,12 +219,12 @@
 
     t_own = mm(pt_times(1), p_own)
     t_low = mm(pt_times(0), lower_rows.reshape(span, width))
-    t_high = mm(pt_times(2), upper_rows.reshape(span, width))
-    terms = (
-        jnp.pad(t_low, ((0, 0), (0, 2 * block_size)))
-        + jnp.pad(t_own, ((0, 0), (block_size, block_size)))
-        + jnp.pad(t_high, ((0, 0), (2 * block_size, 0)))
-    ).reshape(prol_slots, block_size, (prol_slots + 2) * block_size)
+    partial = jnp.pad(t_low, ((0, 0), (0, 2 * block_size))) + jnp.pad(t_own, ((0, 0), (block_size, block_size)))
+    partial, high_w = lax.optimization_barrier((partial, pt_times(2)))
+    t_high = mm(high_w, upper_rows.reshape(span, width))
+    terms = (partial + jnp.pad(t_high, ((0, 0), (2 * block_size, 0)))).reshape(
+        prol_slots, block_size, (prol_slots + 2) * block_size
+    )
 
     result = exchange(terms) + jnp.pad(terms[2], ((0, 0), (2 * block_size, 2 * block_size)))
     return result.reshape(1, block_size, (prol_slots + 6) * block_size)

time: 87.8 us -> 87.9 us (level)
  transfers between devices with their start and end apart: 2 -> 2, of which waited for: 2 -> 2; matrix products, arithmetic and copies ran while one was open for 12% -> 13% of each run, Pallas kernels for 10% -> 10%
where the time goes in v16:
time: 87.9 us; the launch traced here: 87.5 us
  Pallas kernels  32 us (36%)
  waiting for transfers between devices  25.9 us (29%)
  starting transfers between devices  11.8 us (13%)
  matrix products  9.79 us (11%)
  other arithmetic  5.49 us (6%)
  local copies, waits for them, and re-layouts  2.43 us (3%)
    ppermute x2, waiting for transfers between devices, from_behind(): return lax.ppermute(array, axis, pairs)  25.9 us
    pallas_call x1, Pallas kernels, exchange(): pl.pallas_call(exchange_kernel, out_shape=jax.ShapeDtypeStruct((block_siz...  22.8 us
    ppermute x2, starting transfers between devices, from_behind(): return lax.ppermute(array, axis, pairs)  11.8 us
    pallas_call x1, Pallas kernels, dense_sides(): pl.pallas_call(dense_kernel, out_shape=[jax.ShapeDtypeStruct((rows_here,...  9.14 us
    dot_general x3, matrix products, pt_times(): lax.dot_general(p_own, dense[side], (((0,), (0,)), ((), ())), precision=M...  6.88 us
    dot_general x3, matrix products, mm(): jnp.dot(a, b, precision=MATMUL_PRECISION, preferred_element_type=jnp.floa...  2.91 us
  transfers between devices with their start and end apart: 2, of which 2 were waited for; matrix products, arithmetic and copies ran while one was open for 13% of the time, Pallas kernels for 10%

profile of v16, /device:TPU:1, one launch (start us, length us, event | category | flops | bytes accessed | tf_op | source)
XLA Modules:
  0.0 87.5 jit_solution(7025238938251744011)
XLA Ops:
  0.0 0.8 convert_multiply_fusion
  0.8 0.1 copy.8
  0.9 0.1 broadcast_in_dim.10
  0.9 0.1 mul.27
  1.0 0.0 copy-start.2
  1.0 1.4 %broadcast_multiply_fusion = f32[12,64,320]{2,1,0:T(8,128)S(1)} fusion(f32[12,64,320]{2,1,0:T(8,128)} %param.8, f32[12,320]{1,0:T(8,128)S(1)} %mul.27), kind=kLoop, calls=%fused_computation.5 | loop fusion | flops 245760 | bytes 1981440 | tf_op jit(solution)/shard_map/mul | solution.py:196
  2.4 4.4 %collective-permute-start = (f32[12,64,320]{2,1,0:T(8,128)S(1)}, f32[12,64,320]{2,1,0:T(8,128)S(1)}, u32[]{:S(2)}, u32[]{:S(2)}) collective-permute-start(f32[12,64,320]{2,1,0:T(8,128)S(1)} %broadcast_multiply_fusion), channel_id=1, source_target_pairs={{0,1},{1,2},{2,3},{3,4},{4,5},{5,6},{6,7},{7,8},{8,9},{9,10},{10,1... | collective-permute-start | bytes 2949128 | tf_op jit(solution)/shard_map/ppermute | solution.py:14
  6.8 7.4 %collective-permute-start.1 = (f32[12,64,320]{2,1,0:T(8,128)S(1)}, f32[12,64,320]{2,1,0:T(8,128)S(1)}, u32[]{:S(2)}, u32[]{:S(2)}) collective-permute-start(f32[12,64,320]{2,1,0:T(8,128)S(1)} %broadcast_multiply_fusion), channel_id=1, source_target_pairs={{1,0},{2,1},{3,2},{4,3},{5,4},{6,5},{7,6},{8,7},{9,8},{10,9},{11,1... | collective-permute-start | bytes 2949128 | tf_op jit(solution)/shard_map/ppermute | solution.py:14
  14.2 0.5 iota_add_fusion
  14.7 0.0 copy-done.2
  14.7 0.1 iota_compare_fusion.1
  14.8 0.0 copy-done.1
  14.8 0.8 select_reduce_fusion
  15.6 0.7 sub.23.slot_ref
  16.3 9.1 %shard_map.55 = (f32[12,64,768]{2,1,0:T(8,128)}, f32[12,64,768]{2,1,0:T(8,128)}, f32[12,64,768]{2,1,0:T(8,128)}) custom-call(s32[432]{0:T(512)} %sub.23.slot_ref, f32[12,64,896]{2,1,0:T(8,128)} %a_ref.1), custom_call_target="tpu_custom_call" | custom-call | tf_op jit(solution)/shard_map/pallas_call | solution.py:50
  25.4 3.4 %convolution_bitcast_fusion.2 = f32[320,768]{1,0:T(8,128)S(1)} fusion(f32[12,64,320]{2,1,0:T(8,128)S(1)} %broadcast_multiply_fusion, f32[12,64,768]{2,1,0:T(8,128)} %get-tuple-element.10), kind=kOutput, calls=%fused_computation.2 | convolution fusion | flops 1132462080 | bytes 4325376 | tf_op jit(solution)/shard_map/dot_general | solution.py:212
  28.8 0.0 copy-done.4
  28.8 1.7 %convolution_bitcast_fusion.1 = f32[320,768]{1,0:T(8,128)S(1)} fusion(f32[12,64,320]{2,1,0:T(8,128)S(1)} %broadcast_multiply_fusion, f32[12,64,768]{2,1,0:T(8,128)S(1)} %copy-done.4), kind=kOutput, calls=%fused_computation.1 | convolution fusion | flops 1132462080 | bytes 4325376 | tf_op jit(solution)/shard_map/dot_general | solution.py:212
  30.6 0.0 copy-start.3
  30.6 1.0 %fusion.2 = f32[320,320]{1,0:T(8,128)S(1)} fusion(f32[320,768]{1,0:T(8,128)S(1)} %convolution_bitcast_fusion.1, f32[768,320]{1,0:T(8,128)S(1)} %bitcast.24), kind=kOutput, calls=%fused_computation.17 | convolution fusion | flops 471859200 | bytes 2375680 | tf_op jit(solution)/shard_map/dot_general | solution.py:18
  31.6 0.7 copy-done.3
  32.3 1.7 %convolution_bitcast_fusion = f32[320,768]{1,0:T(8,128)S(1)} fusion(f32[12,64,320]{2,1,0:T(8,128)S(1)} %broadcast_multiply_fusion, f32[12,64,768]{2,1,0:T(8,128)S(1)} %copy-done.3), kind=kOutput, calls=%fused_computation | convolution fusion | flops 1132462080 | bytes 4325376 | tf_op jit(solution)/shard_map/dot_general | solution.py:212
  34.0 3.4 %collective-permute-done = f32[12,64,320]{2,1,0:T(8,128)S(1)} collective-permute-done((f32[12,64,320]{2,1,0:T(8,128)S(1)}, f32[12,64,320]{2,1,0:T(8,128)S(1)}, u32[]{:S(2)}, u32[]{:S(2)}) %collective-permute-start) | collective-permute-done | bytes 983072 | tf_op jit(solution)/shard_map/ppermute | solution.py:14
  37.4 1.0 %fusion.1 = f32[320,320]{1,0:T(8,128)S(1)} fusion(f32[320,768]{1,0:T(8,128)S(1)} %convolution_bitcast_fusion.2, f32[768,320]{1,0:T(8,128)S(1)} %bitcast.27), kind=kOutput, calls=%fused_computation.16 | convolution fusion | flops 471859200 | bytes 2375680 | tf_op jit(solution)/shard_map/dot_general | solution.py:18
  38.4 0.2 pad_add_fusion.1
  38.6 22.5 %collective-permute-done.1 = f32[12,64,320]{2,1,0:T(8,128)S(1)} collective-permute-done((f32[12,64,320]{2,1,0:T(8,128)S(1)}, f32[12,64,320]{2,1,0:T(8,128)S(1)}, u32[]{:S(2)}, u32[]{:S(2)}) %collective-permute-start.1) | collective-permute-done | bytes 983072 | tf_op jit(solution)/shard_map/ppermute | solution.py:14
  61.2 1.0 %fusion.3 = f32[320,320]{1,0:T(8,128)S(1)} fusion(f32[320,768]{1,0:T(8,128)S(1)} %convolution_bitcast_fusion, f32[768,320]{1,0:T(8,128)S(1)} %bitcast.26), kind=kOutput, calls=%fused_computation.18 | convolution fusion | flops 471859200 | bytes 2375680 | tf_op jit(solution)/shard_map/dot_general | solution.py:18
  62.1 0.1 pad_add_fusion
  62.2 0.0 copy-start
  62.2 0.8 copy-done
  63.1 22.8 %shard_map.56 = f32[64,704]{1,0:T(8,128)} custom-call(f32[5,64,448]{2,1,0:T(8,128)} %bitcast.25), custom_call_target="tpu_custom_call" | custom-call | tf_op jit(solution)/shard_map/pallas_call | solution.py:162
  85.9 1.6 %add_bitcast_fusion = f32[1,64,704]{2,1,0:T(8,128)} fusion(f32[64,704]{1,0:T(8,128)} %shard_map.56, f32[64,448]{1,0:T(8,128)S(1)} %slice.5), kind=kLoop, calls=%fused_computation.6 | loop fusion | flops 45056 | bytes 475136 | tf_op jit(solution)/shard_map/reshape | solution.py:230
  (6 shorter events, 0.0 us)
Async XLA Ops:
  1.0 13.7 %copy-start.2 = (s32[12]{0:T(128)S(1)}, s32[12]{0:T(128)}, u32[]{:S(2)}) copy-start(s32[12]{0:T(128)} %param.7) | copy-start | bytes 148
  1.0 13.8 %copy-start.1 = (s32[12,14]{1,0:T(8,128)S(1)}, s32[12,14]{1,0:T(8,128)}, u32[]{:S(2)}) copy-start(s32[12,14]{1,0:T(8,128)} %param.6) | copy-start | bytes 2020
  2.4 35.0 %collective-permute-start = (f32[12,64,320]{2,1,0:T(8,128)S(1)}, f32[12,64,320]{2,1,0:T(8,128)S(1)}, u32[]{:S(2)}, u32[]{:S(2)}) collective-permute-start(f32[12,64,320]{2,1,0:T(8,128)S(1)} %broadcast_multiply_fusion), channel_id=1, source_target_pairs={{0,1},{1,2},{2,3},{3,4},{4,5},{5,6},{6,7},{7,8},{8,9},{9,10},{10,1... | collective-permute-start | bytes 2949128 | tf_op jit(solution)/shard_map/ppermute | solution.py:14
  6.8 54.3 %collective-permute-start.1 = (f32[12,64,320]{2,1,0:T(8,128)S(1)}, f32[12,64,320]{2,1,0:T(8,128)S(1)}, u32[]{:S(2)}, u32[]{:S(2)}) collective-permute-start(f32[12,64,320]{2,1,0:T(8,128)S(1)} %broadcast_multiply_fusion), channel_id=1, source_target_pairs={{1,0},{2,1},{3,2},{4,3},{5,4},{6,5},{7,6},{8,7},{9,8},{10,9},{11,1... | collective-permute-start | bytes 2949128 | tf_op jit(solution)/shard_map/ppermute | solution.py:14
  25.4 3.4 %copy-start.4 = (f32[12,64,768]{2,1,0:T(8,128)S(1)}, f32[12,64,768]{2,1,0:T(8,128)}, u32[]{:S(2)}) copy-start(f32[12,64,768]{2,1,0:T(8,128)} %get-tuple-element.11) | copy-start | bytes 7077892
  30.6 1.7 %copy-start.3 = (f32[12,64,768]{2,1,0:T(8,128)S(1)}, f32[12,64,768]{2,1,0:T(8,128)}, u32[]{:S(2)}) copy-start(f32[12,64,768]{2,1,0:T(8,128)} %get-tuple-element.12) | copy-start | bytes 7077892
  62.2 0.8 copy-start
